TPU v7x, 32 devices: a whole 2x2x4 slice. The times are simulated.
32 devices in a mesh: seq: 4 (over x, core), dp: 8 (over z, y).
Axes of the slice: x: 2, y: 2, z: 4, core: 2. Of those that a mesh axis runs over, the one named last changes fastest.
Arguments:
- tokens: bfloat16 [8, 1024, 1024], P('dp', 'seq'), may hold values from -6 to 6
- first_values: bfloat16 [8, 1024, 1024], P('dp', 'seq'), may hold values from -6 to 6
- value_grad_acc: float32 [8, 1024, 1024], P('dp', 'seq'), may hold values from -3 to 3
- segment_ids: int32 [8, 1024], P('dp'), may hold values from 0 to 5, never falling along the last dimension, each value on 1 to 512 neighbouring positions
- query_weight: bfloat16 [1024, 1024], P(('seq', 'dp')), may hold values from -0.1875 to 0.1875
- key_weight: bfloat16 [1024, 1024], P(('seq', 'dp')), may hold values from -0.1875 to 0.1875
- value_weight: bfloat16 [1024, 1024], P(('seq', 'dp')), may hold values from -0.1875 to 0.1875
- out_weight: bfloat16 [1024, 1024], P(('seq', 'dp')), may hold values from -1.5 to 1.5
- attn_gain: bfloat16 [1024], P(('seq', 'dp')), may hold values from 0.099609375 to 1.8984375
- gate_weight: bfloat16 [1024, 2816], P(('seq', 'dp')), may hold values from -0.1875 to 0.1875
- up_weight: bfloat16 [1024, 2816], P(('seq', 'dp')), may hold values from -0.1875 to 0.1875
- down_weight: bfloat16 [2816, 1024], P(('seq', 'dp')), may hold values from -0.109375 to 0.109375
- mlp_gain: bfloat16 [1024], P(('seq', 'dp')), may hold values from 0.099609375 to 1.8984375
- out_grad: bfloat16 [8, 1024, 1024], P('dp', 'seq'), may hold values from -6 to 6
Outputs:
- layer_out: bfloat16 [8, 1024, 1024], P('dp', 'seq')
- token_grad: bfloat16 [8, 1024, 1024], P('dp', 'seq')
- value_grad_out: float32 [8, 1024, 1024], P('dp', 'seq')
- grad_query: float32 [1024, 1024], P(('seq', 'dp'))
- grad_key: float32 [1024, 1024], P(('seq', 'dp'))
- grad_value: float32 [1024, 1024], P(('seq', 'dp'))
- grad_out: float32 [1024, 1024], P(('seq', 'dp'))
- grad_attn_gain: float32 [1024], P(('seq', 'dp'))
- grad_gate: float32 [1024, 2816], P(('seq', 'dp'))
- grad_up: float32 [1024, 2816], P(('seq', 'dp'))
- grad_down: float32 [2816, 1024], P(('seq', 'dp'))
- grad_mlp_gain: float32 [1024], P(('seq', 'dp'))
Inputs may be any that keep to these rules, and one draw needn't show every extreme that they name: `segment_ids`: along each sequence the ids never fall; a document holds 1 to 512 tokens, and one holds exactly 512.
All inputs are finite; a program needn't handle non-finite values.
Results may differ from a plain program's by a relative error of at most 0.015.
Values may be sent and summed in bfloat16 or wider, within the bound.
No kernel may reach another device: no remote copies, remote signals or barrier semaphores. Data moves between devices by JAX's collectives and lax.ppermute only.
A program may use at most 192 MiB of HBM per device.

v0:
```python
import functools
import math

import jax
import jax.numpy as jnp
from jax import lax
from jax.experimental import pallas as pl
from jax.experimental.pallas import tpu as pltpu
from jax.sharding import PartitionSpec as P

HEADS = 16
DOC_MOST = 512
SEQ = 4
BLOCK = 256

epsilon = 1e-06
masked_value = -1e30
bf16 = jnp.bfloat16
f32 = jnp.float32


def mul(a, b, ca, cb):
    return lax.dot_general(a, b, (((ca,), (cb,)), ((), ())), preferred_element_type=f32)


def params(mib):
    return pltpu.CompilerParams(vmem_limit_bytes=mib << 20)


VMEM = pl.BlockSpec(memory_space=pltpu.VMEM)
SMEM = pl.BlockSpec(memory_space=pltpu.SMEM)


def fixed(shape):
    return pl.BlockSpec(shape, lambda *_: (0,) * len(shape), pipeline_mode=pl.Buffered(1))


def sync(*values):
    return lax.optimization_barrier(values)


def after(value, *earlier):
    return lax.optimization_barrier((value, *earlier))[0]


def half_swap(field):
    lanes = field.shape[-1]
    lane = lax.broadcasted_iota(jnp.int32, field.shape, 1)
    up = pltpu.roll(field, lanes - 32, 1)
    down = pltpu.roll(field, 32, 1)
    return jnp.where(lane % 64 < 32, up, down)


def qkv_kernel(me_ref, tok_ref, first_ref, w_ref, gain_ref, cos_ref, sin_ref, nin_ref, q_ref, k_ref, v_ref):
    x = tok_ref[...].astype(f32)
    scale = lax.rsqrt(jnp.mean(x * x, axis=-1, keepdims=True) + epsilon)
    nin = (x * scale * gain_ref[...]).astype(bf16)
    nin_ref[...] = nin
    lin = mul(nin, w_ref[...], 1, 0)
    cos = jnp.concatenate([cos_ref[...]] * 2, axis=1)
    sin = jnp.concatenate([sin_ref[...]] * 2, axis=1)
    part = lin.shape[1] // 3
    q = lin[:, :part]
    q_ref[...] = ((q * cos + half_swap(q) * sin).astype(bf16).astype(f32) * 0.125).astype(bf16)
    k = lin[:, part : 2 * part]
    k_ref[...] = (k * cos + half_swap(k) * sin).astype(bf16)
    v_ref[...] = (0.5 * lin[:, 2 * part :] + 0.5 * first_ref[...].astype(f32)).astype(bf16)


def qkv_call(me, tok, first, w, gain, cos, sin):
    length, width = tok.shape
    rows = length // SEQ
    part = w.shape[1] // 3
    here = lambda k, m: (m[0] ^ k, 0)
    rel = lambda k, m: (k, 0)
    return pl.pallas_call(
        qkv_kernel,
        name="qkv",
        grid_spec=pltpu.PrefetchScalarGridSpec(
            num_scalar_prefetch=1,
            grid=(SEQ,),
            in_specs=[
                pl.BlockSpec((rows, width), rel),
                pl.BlockSpec((rows, part), rel),
                fixed(w.shape),
                fixed((1, width)),
                pl.BlockSpec((rows, 128), here),
                pl.BlockSpec((rows, 128), here),
            ],
            out_specs=[pl.BlockSpec((rows, width), here)] + [pl.BlockSpec((rows, part), here)] * 3,
        ),
        out_shape=[jax.ShapeDtypeStruct((length, width), bf16)]
        + [jax.ShapeDtypeStruct((length, part), bf16)] * 3,
        compiler_params=params(16),
    )(me, tok, first, w, gain, cos, sin)


def key_range(block):
    return max(0, block * BLOCK - (DOC_MOST // BLOCK) * BLOCK), (block + 1) * BLOCK


def column_of(row_ref):
    return jnp.broadcast_to(row_ref[...].astype(f32), (8, row_ref.shape[1])).T[:, :1]


def allowed_pairs(seg_col, seg_row, block, low, high):
    keys = lax.broadcasted_iota(jnp.int32, (high - low, BLOCK), 0) + low
    rows = lax.broadcasted_iota(jnp.int32, (high - low, BLOCK), 1) + block * BLOCK
    row = seg_row[:, block * BLOCK : (block + 1) * BLOCK].astype(f32)
    return (seg_col[low:high, :] == row) & (keys <= rows)


def head_lanes(field, head):
    lane = lax.broadcasted_iota(jnp.int32, field.shape, 1)
    return jnp.where(lane // 64 == head, field, jnp.zeros_like(field))


def half_rows(head):
    return pl.ds(pl.multiple_of(head * 64, 64), 64)


def attend_kernel(q_ref, k_ref, v_ref, seg_row, o_ref, lse_ref, turned, turned_out):
    length = q_ref.shape[0]
    seg_col = column_of(seg_row)
    turned[...] = v_ref[...].astype(f32).T.astype(bf16)

    def one_head(head, carry):
        for block in range(length // BLOCK):
            low, high = key_range(block)
            allowed = allowed_pairs(seg_col, seg_row, block, low, high)
            here = slice(block * BLOCK, (block + 1) * BLOCK)
            scores = mul(k_ref[low:high, :], head_lanes(q_ref[here, :], head), 1, 1)
            scores = jnp.where(allowed, scores, masked_value)
            top = jnp.max(scores, axis=0, keepdims=True)
            expo = jnp.exp(scores - top)
            total = jnp.sum(expo, axis=0, keepdims=True)
            probs = (expo * (1.0 / total)).astype(bf16)
            turned_out[half_rows(head), here] = mul(turned[half_rows(head), low:high], probs, 1, 0)
            lse_ref[0, pl.ds(head, 1), here] = top + jnp.log(total)
        return carry

    lax.fori_loop(0, 2, one_head, 0)
    for block in range(length // BLOCK):
        here = slice(block * BLOCK, (block + 1) * BLOCK)
        o_ref[here, :] = turned_out[:, here].T.astype(bf16)


def attend_call(q, k, v, seg_row):
    length, part = q.shape
    pairs = part // 128
    lanes = pl.BlockSpec((length, 128), lambda p: (0, p))
    return pl.pallas_call(
        attend_kernel,
        name="attend",
        grid=(pairs,),
        in_specs=[lanes] * 3 + [fixed((1, length))],
        out_specs=[lanes, pl.BlockSpec((1, 2, length), lambda p: (p, 0, 0))],
        out_shape=[jax.ShapeDtypeStruct((length, part), bf16), jax.ShapeDtypeStruct((pairs, 2, length), f32)],
        scratch_shapes=[pltpu.VMEM((128, length), bf16), pltpu.VMEM((128, length), f32)],
        compiler_params=params(24),
    )(q, k, v, seg_row)


def attend_back_kernel(
    dp, pieces, place_ref, q_ref, k_ref, v_ref, d0, d1, d2, d3, lse_ref, seg_row, cos_ref, sin_ref, nin_ref,
    *refs,
):
    outs, (da_ref, dk_sum, dv_sum, work, turned, turned_dq) = refs[:-6], refs[-6:]
    *along, d_ref = outs[: len(outs) - 2 * pieces]
    outs = outs[len(outs) - 2 * pieces :]
    length = q_ref.shape[0]
    rows = d0.shape[0]
    for k, ref in enumerate((d0, d1, d2, d3)):
        da_ref[pl.ds(pl.multiple_of((place_ref[0] ^ k) * rows, rows), rows), :] = ref[...]
    seg_col = column_of(seg_row)
    dk_sum[...] = jnp.zeros_like(dk_sum)
    dv_sum[...] = jnp.zeros_like(dv_sum)
    turned[...] = k_ref[...].astype(f32).T.astype(bf16)

    def one_head(head, carry):
        for block in range(length // BLOCK):
            low, high = key_range(block)
            allowed = allowed_pairs(seg_col, seg_row, block, low, high)
            here = slice(block * BLOCK, (block + 1) * BLOCK)
            q_head = head_lanes(q_ref[here, :], head)
            da_head = head_lanes(da_ref[here, :], head)
            scores = mul(k_ref[low:high, :], q_head, 1, 1)
            probs = jnp.where(allowed, jnp.exp(scores - lse_ref[0, pl.ds(head, 1), here]), 0.0)
            d_probs = mul(v_ref[low:high, :], da_head, 1, 1)
            delta = jnp.sum(probs * d_probs, axis=0, keepdims=True)
            d_scores = (probs * (d_probs - delta)).astype(bf16)
            turned_dq[half_rows(head), here] = mul(turned[half_rows(head), low:high], d_scores, 1, 0)
            dk_sum[low:high, :] += mul(d_scores, q_head, 1, 0)
            dv_sum[low:high, :] += mul(probs.astype(bf16), da_head, 1, 0)
        return carry

    lax.fori_loop(0, 2, one_head, 0)
    for block in range(length // BLOCK):
        here = slice(block * BLOCK, (block + 1) * BLOCK)
        dq = turned_dq[:, here].T * 0.125
        d_ref[here, :128] = (dq * cos_ref[here, :] - half_swap(dq) * sin_ref[here, :]).astype(bf16)
    dk = dk_sum[...]
    d_ref[:, 128:256] = (dk * cos_ref[...] - half_swap(dk) * sin_ref[...]).astype(bf16)
    d_ref[:, 256:] = (0.5 * dv_sum[...]).astype(bf16)
    if not outs:
        return
    kept_ref, sent_ref = outs
    part = work.shape[0]
    w_rows = part // dp
    first = 0
    if along:
        first = along[0].shape[0]
        sent_ref[:first, :] = along[0][...]
    for s in range(SEQ):
        work[...] = mul(nin_ref[:, s * part : (s + 1) * part], d_ref[...], 0, 0).astype(bf16)
        for slot in range(dp):
            here = pl.ds(pl.multiple_of(owner_index(place_ref, dp, slot) * w_rows, w_rows), w_rows)
            for t in range(3):
                at = (s * 3 + t) * w_rows
                piece = work[here, t * 128 : t * 128 + 128]
                if slot < dp // 2:
                    kept_ref[slot, at : at + w_rows, :] = piece
                else:
                    at += first + (slot - dp // 2) * kept_ref.shape[1]
                    sent_ref[at : at + w_rows, :] = piece


def attend_back_call(pair, place, q, k, v, da, lse, seg_row, cos, sin, nin, dp, pieces, along=()):
    length, width = nin.shape
    part = width // SEQ
    lanes = pl.BlockSpec((length, 128), lambda _: (0, pair), pipeline_mode=pl.Buffered(1))
    outs = [(length, 384)]
    if pieces:
        rows = 3 * width // dp
        outs += [(dp // 2, rows, 128), (sum(x.shape[0] for x in along) + dp // 2 * rows, 128)]
    return pl.pallas_call(
        functools.partial(attend_back_kernel, dp, pieces),
        name="attend_back",
        grid=(1,),
        in_specs=[SMEM]
        + [lanes] * 3
        + [pl.BlockSpec((length // SEQ, 128), lambda _: (0, pair), pipeline_mode=pl.Buffered(1))] * 4
        + [pl.BlockSpec((1, 2, length), lambda _: (pair, 0, 0)), fixed((1, length))]
        + [fixed((length, 128))] * 2
        + [fixed(nin.shape)]
        + [fixed(x.shape) for x in along],
        out_specs=[fixed(x) for x in outs],
        out_shape=[jax.ShapeDtypeStruct(x, bf16) for x in outs],
        scratch_shapes=[pltpu.VMEM((length, 128), bf16)]
        + [pltpu.VMEM((length, 128), f32)] * 2
        + [pltpu.VMEM((part, 384), bf16), pltpu.VMEM((128, length), bf16), pltpu.VMEM((128, length), f32)],
        compiler_params=params(60),
    )(place, q, k, v, *da, lse, seg_row, cos, sin, nin, *along)


def main_lanes(inner):
    return inner // 128 * 128


def pack_attn_kernel(
    place_ref, q_ref, k_ref, v_ref, o_ref, d_ref, ag_ref, mg_ref, tok_ref, c0, c1, c2, c3, orows_ref, drows_ref, *halves_refs
):
    me, owner = place_ref[0], place_ref[1]
    w_rows, width = q_ref.shape
    part = width // SEQ
    lane = lax.broadcasted_iota(jnp.int32, (1, 128), 1)
    spot = lane // w_rows == owner % (128 // w_rows)

    def spread(gain):
        return jnp.where(spot, jnp.concatenate([gain[...].astype(f32)] * (128 // w_rows), axis=1), 0.0)

    row = lax.broadcasted_iota(jnp.int32, (16, 128), 0)
    gains = jnp.where(row == 0, spread(ag_ref), jnp.where(row == 1, spread(mg_ref), 0.0)).astype(bf16)
    for k, out in enumerate((c0, c1, c2, c3)):
        at = 0
        for ref in (q_ref, k_ref, v_ref):
            for t in range(part // 128):
                lanes = pl.ds(pl.multiple_of((me ^ k) * part + t * 128, 128), 128)
                out[at : at + w_rows, :] = ref[:, lanes]
                at += w_rows
        out[at : at + 16, :] = gains
    for ref, out in ((o_ref, orows_ref), (d_ref, drows_ref)):
        rows = ref.shape[0]
        for t in range(width // 128):
            out[t * rows : (t + 1) * rows, :] = ref[:, t * 128 : t * 128 + 128]
    for i, out in enumerate(halves_refs):
        rows = out.shape[0]
        out[...] = tok_ref[i * rows : (i + 1) * rows, :]


def pack_attn(place, wq, wk, wv, wo, wd, attn_gain, mlp_gain, tok):
    w_rows, width = wq.shape
    tiles = width // 128
    shapes = [(3 * tiles // SEQ * w_rows + 16, 128)] * 4 + [(tiles * w_rows, 128), (tiles * wd.shape[0], 128)]
    shapes += [(tok.shape[0] // 2, width)] * 2
    return pl.pallas_call(
        pack_attn_kernel,
        name="pack_attn",
        grid=(1,),
        in_specs=[SMEM] + [fixed(w.shape) for w in (wq, wk, wv, wo, wd)] + [fixed((1, w_rows))] * 2 + [fixed(tok.shape)],
        out_specs=[fixed(x) for x in shapes],
        out_shape=[jax.ShapeDtypeStruct(x, bf16) for x in shapes],
        compiler_params=params(60),
    )(place, wq, wk, wv, wo, wd, attn_gain[None], mlp_gain[None], tok)


def pack_ffn_kernel(place_ref, g_ref, u_ref, c0, c1, c2, c3):
    me = place_ref[0]
    w_rows = g_ref.shape[0]
    inner = g_ref.shape[1] // SEQ
    main = main_lanes(inner)
    for s in range(SEQ):
        gate, up = g_ref[:, s * inner : (s + 1) * inner], u_ref[:, s * inner : (s + 1) * inner]
        tiles = [field[:, t * 128 : t * 128 + 128] for field in (gate, up) for t in range(main // 128)]
        tiles.append(jnp.concatenate([gate[:, main:], up[:, main:]], axis=1))
        for k, out in enumerate((c0, c1, c2, c3)):

            @pl.when(me ^ k == s)
            def _():
                for t, tile in enumerate(tiles):
                    out[t * w_rows : (t + 1) * w_rows, :] = tile


def pack_ffn(place, wg, wu):
    w_rows = wg.shape[0]
    inner = wg.shape[1] // SEQ
    return pl.pallas_call(
        pack_ffn_kernel,
        name="pack_ffn",
        grid=(1,),
        in_specs=[SMEM] + [fixed(w.shape) for w in (wg, wu)],
        out_specs=[fixed((2 * inner // 128 * w_rows, 128))] * 4,
        out_shape=[jax.ShapeDtypeStruct((2 * inner // 128 * w_rows, 128), bf16)] * 4,
        compiler_params=params(60),
    )(place, wg, wu)


def source_of(place_ref, dp, slot):
    groups = dp // 2
    b, j = slot // groups, slot % groups
    z, y = place_ref[2] // 2, place_ref[2] % 2
    return ((z + groups - j) % groups) * 2 + (y ^ b)


def assemble_attn_kernel(place_ref, *refs):
    dp = len(refs) - 4
    pieces, (w_ref, wo_ref, ag_ref, mg_ref) = refs[:dp], refs[dp:]
    width, lanes = w_ref.shape
    w_rows = width // (SEQ * dp)
    part = width // SEQ
    chunk = lanes // 128 * w_rows + 16
    ag_ref[...] = jnp.zeros_like(ag_ref)
    mg_ref[...] = jnp.zeros_like(mg_ref)
    for slot, piece in enumerate(pieces):
        src = source_of(place_ref, dp, slot)
        for k in range(SEQ):
            s = place_ref[0] ^ k
            row = pl.multiple_of(s * part + src * w_rows, w_rows)
            for t in range(lanes // 128):
                at = k * chunk + t * w_rows
                w_ref[pl.ds(row, w_rows), t * 128 : t * 128 + 128] = piece[at : at + w_rows, :]
            gains = piece[(k + 1) * chunk - 16 : (k + 1) * chunk, :].astype(f32)
            tile = (s * dp + src) * w_rows // 128
            ag_ref[pl.ds(tile, 1), :] += gains[0:1, :]
            mg_ref[pl.ds(tile, 1), :] += gains[1:2, :]
        row = pl.multiple_of(src * w_rows, w_rows)
        for t in range(width // 128):
            at = SEQ * chunk + t * w_rows
            wo_ref[pl.ds(row, w_rows), t * 128 : t * 128 + 128] = piece[at : at + w_rows, :]


def assemble_attn(place, pieces, width):
    shapes = [(width, 3 * width // SEQ), (width // SEQ, width), (width // 128, 128), (width // 128, 128)]
    return pl.pallas_call(
        assemble_attn_kernel,
        name="assemble_attn",
        grid=(1,),
        in_specs=[SMEM] + [fixed(x.shape) for x in pieces],
        out_specs=[fixed(x) for x in shapes],
        out_shape=[jax.ShapeDtypeStruct(x, t) for x, t in zip(shapes, (bf16, bf16, f32, f32))],
        compiler_params=params(12),
    )(place, *pieces)


def assemble_rows_kernel(place_ref, *refs):
    dp = len(refs) - 1
    pieces, out_ref = refs[:dp], refs[dp]
    count = out_ref.shape[0] // dp
    for slot, piece in enumerate(pieces):
        row = pl.multiple_of(source_of(place_ref, dp, slot) * count, 8)
        for t in range(out_ref.shape[1] // 128):
            out_ref[pl.ds(row, count), t * 128 : t * 128 + 128] = piece[t * count : (t + 1) * count, :]


def assemble_rows(place, pieces, width, inner):
    return pl.pallas_call(
        assemble_rows_kernel,
        name="assemble_rows",
        grid=(1,),
        in_specs=[SMEM] + [fixed(x.shape) for x in pieces],
        out_specs=fixed((inner, width)),
        out_shape=jax.ShapeDtypeStruct((inner, width), bf16),
        compiler_params=params(12),
    )(place, *pieces)


def ffn_kernel(me_ref, tok_ref, og_ref, a0, a1, a2, a3, wo0, wo1, wo2, wo3, gain_ref, w_ref, wd_ref, *outs):
    nm_ref, hid_ref, dgu_ref, mid_ref, *lists = outs
    step = pl.program_id(0)
    if len(w_ref.shape) == 3:
        pieces, w_ref = w_ref, lists.pop()
        dp = pieces.shape[0]
        width, lanes = w_ref.shape
        w_rows = width // (SEQ * dp)
        chunk = lanes // 128 * w_rows

        @pl.when(step == 0)
        def _():
            for k in range(SEQ):
                for src in range(dp):
                    row = pl.multiple_of((me_ref[0] ^ k) * (width // SEQ) + src * w_rows, w_rows)
                    for t in range(lanes // 128):
                        at = k * chunk + t * w_rows
                        w_ref[pl.ds(row, w_rows), t * 128 : t * 128 + 128] = pieces[src, at : at + w_rows, :]

    mid = tok_ref[...].astype(f32)
    inner = wd_ref.shape[0]
    main = main_lanes(inner)
    for a, wo in zip((a0, a1, a2, a3), (wo0, wo1, wo2, wo3)):
        mid = mid + mul(a[...], wo[...], 1, 0)
    scale = lax.rsqrt(jnp.mean(mid * mid, axis=-1, keepdims=True) + epsilon)
    nm = (mid * scale * gain_ref[...]).astype(bf16)
    nm_ref[...] = nm
    d_hidden = mul(og_ref[...], wd_ref[...], 1, 1)
    both = mul(nm, w_ref[...], 1, 0)

    def gated(gate, up, grad):
        sig = jax.nn.sigmoid(gate)
        silu = gate * sig
        return (
            (silu * up).astype(bf16),
            (grad * up * (sig * (1.0 + gate * (1.0 - sig)))).astype(bf16),
            (grad * silu).astype(bf16),
        )

    hid_main, dg_main, du_main = gated(both[:, :main], both[:, main : 2 * main], d_hidden[:, :main])
    last = both[:, 2 * main :]
    hid_last, dg_last, du_last = gated(last[:, : inner - main], last[:, inner - main :], d_hidden[:, main:])
    hid_ref[:, :main] = hid_main
    hid_ref[:, main:] = hid_last
    dgu_ref[:, :main] = dg_main
    dgu_ref[:, main : 2 * main] = du_main
    dgu_ref[:, 2 * main :] = jnp.concatenate([dg_last, du_last], axis=1)
    dnm = mul(dgu_ref[...], w_ref[...], 1, 1).astype(bf16)
    lo = mul(hid_ref[...], wd_ref[...], 1, 0).astype(bf16)
    dnm_kept, dnm_sent, lo_kept, lo_sent = lists
    rows = tok_ref.shape[0]
    for k in range(SEQ):

        @pl.when(step == SEQ - 1 - k)
        def _():
            here = slice(k // 2 * rows, (k // 2 + 1) * rows)
            (dnm_sent if k % 2 else dnm_kept)[here, :] = dnm
            (lo_sent if k % 2 else lo_kept)[here, :] = lo

    @pl.when(step == SEQ - 1)
    def _():
        mid_ref[...] = mid


def ffn_call(me, tok, og, att, wo, gain, w, wd):
    length, width = tok.shape
    rows = length // SEQ
    inner = wd.shape[0]
    part = att[0].shape[1]
    rel = lambda k, m: (SEQ - 1 - k, 0)
    here = lambda k, m: (m[0] ^ (SEQ - 1 - k), 0)
    return pl.pallas_call(
        ffn_kernel,
        name="ffn",
        grid_spec=pltpu.PrefetchScalarGridSpec(
            num_scalar_prefetch=1,
            grid=(SEQ,),
            in_specs=[pl.BlockSpec((rows, width), rel)] * 2
            + [pl.BlockSpec((rows, part), here)] * 4
            + [fixed(x.shape) for x in wo]
            + [fixed((1, width)), fixed(w.shape), fixed(wd.shape)],
            out_specs=[
                pl.BlockSpec((rows, width), rel),
                pl.BlockSpec((rows, inner), rel),
                pl.BlockSpec((rows, 2 * inner), rel),
                fixed((rows, width)),
            ]
            + [fixed((2 * rows, width))] * 4,
            scratch_shapes=[pltpu.VMEM((width, 2 * inner), bf16)] * (w.ndim - 2),
        ),
        out_shape=[
            jax.ShapeDtypeStruct((length, width), bf16),
            jax.ShapeDtypeStruct((length, inner), bf16),
            jax.ShapeDtypeStruct((length, 2 * inner), bf16),
            jax.ShapeDtypeStruct((rows, width), f32),
        ]
        + [jax.ShapeDtypeStruct((2 * rows, width), bf16)] * 4,
        compiler_params=params(60),
    )(me, tok, og, *att, *wo, gain, w, wd)


def owner_index(place_ref, dp, slot):
    groups = dp // 2
    b, j = slot // groups, slot % groups
    z, y = place_ref[2] // 2, place_ref[2] % 2
    return ((z + j) % groups) * 2 + (y ^ b)


def columns_grad_kernel(place_ref, act_ref, grad_ref, *refs):
    outs, work = refs[:-1], refs[-1]
    dp = len(outs)
    work[...] = mul(act_ref[...], grad_ref[...], 0, 0).astype(bf16)
    w_rows = work.shape[0] // dp
    for slot, ref in enumerate(outs):
        here = pl.ds(pl.multiple_of(owner_index(place_ref, dp, slot) * w_rows, w_rows), w_rows)
        for t in range(work.shape[1] // 128):
            ref[t * w_rows : (t + 1) * w_rows, :] = work[here, t * 128 : t * 128 + 128]


def columns_grad_plain(act, grad, dp):
    width, lanes = act.shape[1], grad.shape[1]
    w_rows = width // (SEQ * dp)
    grad = mul(act, grad, 0, 0).astype(bf16).reshape(SEQ, dp, w_rows, lanes // 128, 128)
    return grad.transpose(1, 0, 3, 2, 4).reshape(dp, -1, 128)


def columns_grad(place, act, grad, dp):
    length, width = act.shape
    lanes = grad.shape[1]
    part = width // SEQ
    chunk = lanes // 128 * (part // dp)
    return pl.pallas_call(
        columns_grad_kernel,
        name="columns_grad",
        grid_spec=pltpu.PrefetchScalarGridSpec(
            num_scalar_prefetch=1,
            grid=(SEQ,),
            in_specs=[pl.BlockSpec((length, part), lambda s, m: (0, s)), fixed(grad.shape)],
            out_specs=[pl.BlockSpec((chunk, 128), lambda s, m: (s, 0))] * dp,
            scratch_shapes=[pltpu.VMEM((part, lanes), bf16)],
        ),
        out_shape=[jax.ShapeDtypeStruct((SEQ * chunk, 128), bf16)] * dp,
        compiler_params=params(60),
    )(place, act, grad)


def out_grad_kernel(place_ref, act_ref, d0, d1, d2, d3, kept_ref, sent_ref, work):
    rows = d0.shape[0]
    total = 0.0
    for k, ref in enumerate((d0, d1, d2, d3)):
        act = act_ref[pl.ds(pl.multiple_of((place_ref[0] ^ k) * rows, rows), rows), :]
        total = total + mul(act, ref[...], 0, 0)
    work[...] = total.astype(bf16)
    dp = 2 * kept_ref.shape[0]
    count = work.shape[0] // dp
    at = 0
    for slot in range(dp):
        here = pl.ds(pl.multiple_of(owner_index(place_ref, dp, slot) * count, count), count)
        for t in range(work.shape[1] // 128):
            piece = work[here, t * 128 : t * 128 + 128]
            if slot < dp // 2:
                kept_ref[slot, t * count : (t + 1) * count, :] = piece
            else:
                sent_ref[at : at + count, :] = piece
                at += count


def out_projection_grad(place, act, d_branch, dp):
    width = d_branch[0].shape[1]
    part = act.shape[1]
    shape = (dp // 2, width // 128 * (part // dp), 128)
    sent = (shape[0] * shape[1], 128)
    return pl.pallas_call(
        out_grad_kernel,
        name="out_projection_grad",
        grid=(1,),
        in_specs=[SMEM, fixed(act.shape)] + [fixed(x.shape) for x in d_branch],
        out_specs=[fixed(shape), fixed(sent)],
        out_shape=[jax.ShapeDtypeStruct(shape, bf16), jax.ShapeDtypeStruct(sent, bf16)],
        scratch_shapes=[pltpu.VMEM((part, width), bf16)],
        compiler_params=params(24),
    )(place, act, *d_branch)


def down_grad_kernel(act_ref, grad_ref, out_ref):
    out_ref[...] = mul(act_ref[...], grad_ref[...], 0, 0).astype(bf16)


def down_grad(act, grad):
    length, width = grad.shape
    step = 256
    return pl.pallas_call(
        down_grad_kernel,
        name="down_grad",
        grid=(width // step,),
        in_specs=[fixed(act.shape), pl.BlockSpec((length, step), lambda c: (0, c))],
        out_specs=pl.BlockSpec((act.shape[1], step), lambda c: (0, c)),
        out_shape=jax.ShapeDtypeStruct((act.shape[1], width), bf16),
        compiler_params=params(60),
    )(act, grad)


def simple(kernel, name, args, outs, limit=24):
    return pl.pallas_call(
        kernel,
        name=name,
        grid=(1,),
        in_specs=[SMEM if x.dtype == jnp.int32 else fixed(x.shape) for x in args],
        out_specs=[fixed(x.shape) for x in outs],
        out_shape=outs,
        compiler_params=params(limit),
    )(*args)


def shaped(dtype, *shape):
    return jax.ShapeDtypeStruct(shape, dtype)


def sum_kernel(*refs):
    *ins, out = refs
    out[...] = sum(x[...].astype(f32) for x in ins).astype(out.dtype)


def total(*pieces):
    return simple(sum_kernel, "total", pieces, [shaped(bf16, *pieces[0].shape)])[0]


def halves_kernel(kept_ref, got_ref, near_ref, far_ref):
    rows = near_ref.shape[0]
    near_ref[...] = kept_ref[:rows, :].astype(f32) + got_ref[:rows, :].astype(f32)
    far_ref[...] = (kept_ref[rows:, :].astype(f32) + got_ref[rows:, :].astype(f32)).astype(bf16)


def halves(kept, got):
    rows, width = kept.shape[0] // 2, kept.shape[1]
    return simple(halves_kernel, "halves", (kept, got), [shaped(f32, rows, width), shaped(bf16, rows, width)])


def slots_kernel(kept_ref, got_ref, *outs):
    count = kept_ref.shape[1]
    at = got_ref.shape[0] - len(outs) * count
    for j, out in enumerate(outs):
        got = got_ref[at + j * count : at + (j + 1) * count, :]
        out[...] = (kept_ref[j].astype(f32) + got.astype(f32)).astype(out.dtype)


def slots(kept, got):
    shape = kept.shape[1:]
    outs = [shaped(f32, *shape)] + [shaped(bf16, *shape)] * (kept.shape[0] - 1)
    return simple(slots_kernel, "slots", (kept, got), outs)


def back_through_norm(grad, field, gain):
    scale = lax.rsqrt(jnp.mean(field * field, axis=-1, keepdims=True) + epsilon)
    unit = field * scale
    pressed = grad * gain
    return scale * (pressed - unit * jnp.mean(pressed * unit, axis=-1, keepdims=True))


def branch_kernel(near_ref, far_ref, mid_ref, og_ref, gain_ref, w0, w1, w2, w3, d_mid_ref, d_ref, a0, a1, a2, a3):
    grad = near_ref[...] + far_ref[...].astype(f32)
    d_mid = og_ref[...].astype(f32) + back_through_norm(grad, mid_ref[...], gain_ref[...])
    d_mid_ref[...] = d_mid
    d_branch = d_mid.astype(bf16)
    d_ref[...] = d_branch
    for w, a in ((w0, a0), (w1, a1), (w2, a2), (w3, a3)):
        a[...] = mul(d_branch, w[...], 1, 1).astype(bf16)


def token_grad_kernel(near_ref, far_ref, tok_ref, gain_ref, d_mid_ref, out_ref):
    grad = near_ref[...] + far_ref[...].astype(f32)
    out_ref[...] = (d_mid_ref[...] + back_through_norm(grad, tok_ref[...].astype(f32), gain_ref[...])).astype(bf16)


def cut_kernel(me_ref, *refs):
    ins, d_ref, (mine_ref, near_ref, far_ref) = refs[:-4], refs[-4], refs[-3:]
    groups = [ins[:4], ins[4:8], ins[8:]]
    count = far_ref.shape[0] - 2 * mine_ref.shape[0]
    far_ref[2 * mine_ref.shape[0] :, :] = d_ref[pl.ds(pl.multiple_of(((me_ref[0] >> 1) ^ 1) * count, count), count), 256:]
    me = me_ref[0]
    at = 0
    for pieces in groups:
        chunk = pieces[0].shape[0] // SEQ

        def chunk_of(s):
            here = pl.ds(pl.multiple_of(s * chunk, 8), chunk)
            return sum(x[here, :].astype(f32) for x in pieces).astype(bf16)

        mine_ref[at : at + chunk, :] = chunk_of(me)
        near_ref[at : at + chunk, :] = chunk_of(me ^ 1)
        for core in range(2):
            row = core * mine_ref.shape[0] + at
            far_ref[row : row + chunk, :] = chunk_of(((me >> 1) ^ 1) * 2 + core)
        at += chunk


def cut(me, attn, ffn, d_pair):
    rows = (attn[0][0].shape[0] * 2 + ffn[0].shape[0]) // SEQ
    outs = [shaped(bf16, n, 128) for n in (rows, rows, 2 * rows + d_pair.shape[0] // 2)]
    return simple(cut_kernel, "cut", (me, *attn[0], *attn[1], *ffn, d_pair), outs)


def relay_kernel(me_ref, near, far, d0_ref, d1_ref, far0_ref, out_ref):
    me = me_ref[0]
    core = (me & 1) ^ 1
    count = near.shape[0]
    out_ref[:count, :] = near[...]
    out_ref[count : 2 * count, :] = far[pl.ds(pl.multiple_of(core * count, 8), count), :]
    at = 2 * count
    rows = far0_ref.shape[0] // 2
    first = pl.multiple_of((me ^ 1) * rows, rows)
    for d_ref, far_ref, row in ((d0_ref, far0_ref, 0), (d1_ref, far, 2 * count)):
        out_ref[at : at + rows, :] = d_ref[pl.ds(first, rows), 256:]
        out_ref[at + rows : at + 2 * rows, :] = far_ref[pl.ds(pl.multiple_of(row + core * rows, 8), rows), :]
        at += 2 * rows


def value_grad_kernel(me_ref, acc_ref, d0_ref, d1_ref, far0_ref, far, got_ref, out_ref):
    me = me_ref[0]
    rows = acc_ref.shape[0]
    first = pl.multiple_of(me * rows, rows)
    at = far.shape[0] - 2 * rows

    for p, (d_ref, far_ref, row) in enumerate(((d0_ref, far0_ref, 0), (d1_ref, far, at))):
        pieces = (
            d_ref[pl.ds(first, rows), 256:],
            got_ref[at : at + rows, :],
            far_ref[pl.ds(pl.multiple_of(row + (me & 1) * rows, 8), rows), :],
            got_ref[at + rows : at + 2 * rows, :],
        )
        for k, piece in enumerate(pieces):
            lanes = pl.ds(pl.multiple_of((me ^ k) * 256 + p * 128, 128), 128)
            out_ref[:, lanes] = acc_ref[:, lanes] + piece.astype(f32)
        at += 2 * rows


def finish_kernel(
    me_ref, mine, far, got_ref, o0, o1, o2, o3, wq, wk, wv, wg, wu, ga_ref, gm_ref, down_ref,
    gq_ref, gk_ref, gv_ref, go_ref, gga_ref, gg_ref, gu_ref, ggm_ref, gd_ref, cols_a, cols_f,
):
    me = me_ref[0]
    gd_ref[...] = down_ref[...].astype(f32)
    count = mine.shape[0]
    at = 0
    for cols in (cols_a, cols_f):
        chunk = cols.shape[1]
        cols[0] = mine[at : at + chunk, :]
        cols[2] = far[pl.ds(pl.multiple_of((me & 1) * count + at, 8), chunk), :]
        cols[1] = got_ref[at : at + chunk, :]
        cols[3] = got_ref[count + at : count + at + chunk, :]
        at += chunk
    out = sum(x[...].astype(f32) for x in (o0, o1, o2, o3))
    w_rows, width = gq_ref.shape
    for t in range(width // 128):
        go_ref[:, t * 128 : t * 128 + 128] = out[t * w_rows : (t + 1) * w_rows, :]
    unpack_attn(me, cols_a, gq_ref, gk_ref, gv_ref)
    gga_ref[...] = gain_grad(((wq, gq_ref), (wk, gk_ref), (wv, gv_ref)), ga_ref)
    unpack_ffn(me, cols_f, gg_ref, gu_ref)
    ggm_ref[...] = gain_grad(((wg, gg_ref), (wu, gu_ref)), gm_ref)


def gain_grad(pairs, gain_ref):
    column = sum(jnp.sum(w[...].astype(f32) * g[...], axis=1, keepdims=True) for w, g in pairs)
    rows = column.shape[0]
    same = lax.broadcasted_iota(jnp.int32, (rows, rows), 0) == lax.broadcasted_iota(jnp.int32, (rows, rows), 1)
    return jnp.sum(jnp.where(same, column, 0.0), axis=0, keepdims=True) / gain_ref[...].astype(f32)


def unpack_attn(me, cols_ref, *outs):
    w_rows, width = outs[0].shape
    part = width // SEQ
    for s in range(SEQ):
        at = 0
        for t in range(part // 128):
            for ref in outs:
                lanes = slice(s * part + t * 128, s * part + t * 128 + 128)
                ref[:, lanes] = cols_ref[me ^ s, at : at + w_rows, :].astype(f32)
                at += w_rows


def unpack_ffn(me, cols_ref, gg_ref, gu_ref):
    w_rows = gg_ref.shape[0]
    inner = gg_ref.shape[1] // SEQ
    main = main_lanes(inner)
    rest = inner - main
    half = main // 128
    for s in range(SEQ):
        slot = me ^ s
        tiles = [cols_ref[slot, t * w_rows : (t + 1) * w_rows, :].astype(f32) for t in range(2 * inner // 128)]
        gg_ref[:, s * inner : (s + 1) * inner] = jnp.concatenate(tiles[:half] + [tiles[-1][:, :rest]], axis=1)
        gu_ref[:, s * inner : (s + 1) * inner] = jnp.concatenate(tiles[half : 2 * half] + [tiles[-1][:, rest:]], axis=1)


def unpack_kernel(me_ref, cols_a, cols_f, wq, wk, wv, wg, wu, ga_ref, gm_ref, gq_ref, gk_ref, gv_ref, gga_ref, gg_ref, gu_ref, ggm_ref):
    unpack_attn(me_ref[0], cols_a, gq_ref, gk_ref, gv_ref)
    gga_ref[...] = gain_grad(((wq, gq_ref), (wk, gk_ref), (wv, gv_ref)), ga_ref)
    unpack_ffn(me_ref[0], cols_f, gg_ref, gu_ref)
    ggm_ref[...] = gain_grad(((wg, gg_ref), (wu, gu_ref)), gm_ref)


def input_grad_kernel(me_ref, *refs):
    *d_refs, w_ref, kept_ref, sent_ref = refs
    step = pl.program_id(0)
    d_qkv = [d[:, i * 128 : i * 128 + 128] for i in range(3) for d in d_refs]
    grad = mul(jnp.concatenate(d_qkv, axis=1), w_ref[...], 1, 1).astype(bf16)
    rows = grad.shape[0]
    for k in range(SEQ):

        @pl.when(step == SEQ - 1 - k)
        def _():
            (sent_ref if k % 2 else kept_ref)[k // 2 * rows : (k // 2 + 1) * rows, :] = grad


def input_grad(me, d_qkv, w):
    length, part = d_qkv[0].shape
    width = w.shape[0]
    rows = length // SEQ
    here = lambda k, m: (m[0] ^ (SEQ - 1 - k), 0)
    return pl.pallas_call(
        input_grad_kernel,
        name="input_grad",
        grid_spec=pltpu.PrefetchScalarGridSpec(
            num_scalar_prefetch=1,
            grid=(SEQ,),
            in_specs=[pl.BlockSpec((rows, part), here)] * len(d_qkv) + [fixed(w.shape)],
            out_specs=[fixed((2 * rows, width))] * 2,
        ),
        out_shape=[jax.ShapeDtypeStruct((2 * rows, width), bf16)] * 2,
        compiler_params=params(16),
    )(me, *d_qkv, w)


def to_core(value):
    return lax.ppermute(value, "seq", [(i, i ^ 1) for i in range(SEQ)])


def to_chip(value):
    return lax.ppermute(value, "seq", [(i, i ^ 2) for i in range(SEQ)])


def to_both(value):
    return lax.ppermute(value, "seq", [(i, i ^ 3) for i in range(SEQ)])


def gather_rel(value):
    far = to_chip(value)
    return value, to_core(value), far, to_core(far)


def exchange_rel(pieces):
    return [pieces[0], to_core(pieces[1]), to_chip(pieces[2]), to_both(pieces[3])]


def scatter_sum(kept, sent):
    sums = add(kept, to_core(sent))
    rows = kept.shape[0] // 2
    return sums[:rows] + to_chip(sums[rows:].astype(bf16)).astype(f32)


def add(a, b):
    return a.astype(f32) + b.astype(f32)


def to_y(value):
    dp = lax.axis_size("dp")
    return lax.ppermute(value, "dp", [(i, i ^ 1) for i in range(dp)])


def to_z(value, hops=1):
    dp = lax.axis_size("dp")
    return lax.ppermute(value, "dp", [(i, (i + 2 * hops) % dp) for i in range(dp)])


def rotary(length, head_width):
    pairs = jnp.arange(head_width // 2, dtype=f32)
    freq = jnp.exp(pairs * (-2.0 * math.log(10000.0) / head_width))
    theta = jnp.arange(length, dtype=jnp.int32).astype(f32)[:, None] * freq[None, :]
    cos, sin = jnp.cos(theta), jnp.sin(theta)
    return jnp.concatenate([cos] * 4, axis=1), jnp.concatenate([-sin, sin] * 2, axis=1)


class Stage:
    def fence(self):
        names = list(vars(self))
        for name, value in zip(names, sync(*[getattr(self, name) for name in names])):
            setattr(self, name, value)


def body_direct(
    tokens, first_values, value_grad_acc, segment_ids, query_weight, key_weight, value_weight, out_weight,
    attn_gain, gate_weight, up_weight, down_weight, mlp_gain, out_grad,
):
    dp = lax.axis_size("dp")
    zs = dp // 2
    rows, width = tokens.shape[1:]
    length = segment_ids.shape[1]
    w_rows = query_weight.shape[0]
    part = width // SEQ
    inner = gate_weight.shape[1] // SEQ
    me = lax.axis_index("seq").astype(jnp.int32)
    mine = lax.axis_index("dp").astype(jnp.int32)
    me_arg = me[None]
    place = jnp.stack([me, me * dp + mine, mine])
    s = Stage()

    half = rows // 2
    *s.cols, s.orows, drows, tok_a, tok_b = pack_attn(
        place, query_weight, key_weight, value_weight, out_weight, down_weight, attn_gain, mlp_gain, tokens[0]
    )
    s.r, s.tok_far = [drows], [tok_a, tok_b]
    s.tokens, s.first, s.out_grad, s.segments = tokens[0], first_values[0], out_grad[0], segment_ids
    s.gate, s.up = gate_weight, up_weight
    s.fence()
    s.cols = exchange_rel(s.cols)
    s.ry = [to_y(s.r[0])]
    s.r.append(to_z(s.r[0]))
    s.fence()
    s.a = [jnp.concatenate([*s.cols, s.orows])]
    del s.cols, s.orows
    s.tok_far[0] = to_chip(s.tok_far[0])
    s.ay = [to_y(s.a[0])]
    s.a.append(to_z(s.a[0]))
    s.fcols = pack_ffn(place, s.gate, s.up)
    del s.gate, s.up
    s.fence()
    s.ay.append(to_y(s.a[1]))
    s.a.append(to_z(s.a[1]))
    s.f_piece = jnp.concatenate(exchange_rel(s.fcols))
    s.cos, s.sin = rotary(length, width // HEADS)
    del s.fcols
    s.fence()
    ffn_all = lax.all_gather(s.f_piece, "dp", axis=0, tiled=False)
    del s.f_piece
    s.tok_far[1] = to_chip(s.tok_far[1])
    s.ay.append(to_y(s.a[2]))
    s.a.append(to_z(s.a[2]))
    s.tok_near = to_core(s.tokens)
    s.first = [lax.dynamic_slice_in_dim(s.first, (me ^ k) * part, part, 1) for k in range(SEQ)]
    s.og_far = [s.out_grad[:half], s.out_grad[half:]]
    s.fence()
    s.ay.append(to_y(s.a[3]))
    s.first = jnp.concatenate(exchange_rel(s.first))
    tok_far = jnp.concatenate(s.tok_far)
    s.tok = jnp.concatenate([s.tokens, s.tok_near, tok_far, to_core(tok_far)])
    del s.tok_far, s.tok_near
    s.fence()
    s.ry.append(to_y(s.r[1]))
    s.r.append(to_z(s.r[1]))
    s.og_far[0] = to_chip(s.og_far[0])
    s.og = [s.out_grad, to_core(s.out_grad)]
    s.w_qkv, s.w_out, attn_gain_all, mlp_gain_all = assemble_attn(place, s.a + s.ay, width)
    s.attn_gain, s.mlp_gain = attn_gain_all.reshape(1, width), mlp_gain_all.reshape(1, width)
    s.nin, s.q, s.k, s.v = qkv_call(me_arg, s.tok, s.first, s.w_qkv, s.attn_gain, s.cos, s.sin)
    del s.a, s.ay, s.first
    s.fence()
    s.og_far[1] = to_chip(s.og_far[1])
    s.wo = [s.w_out, to_core(s.w_out), to_chip(s.w_out)]
    s.ry.append(to_y(s.r[2]))
    s.r.append(to_z(s.r[2]))
    s.attended, s.lse = attend_call(s.q, s.k, s.v, s.segments)
    del s.w_out
    s.fence()
    att_far = to_chip(s.attended)
    s.ry.append(to_y(s.r[3]))
    s.att = [s.attended, to_core(s.attended), att_far]
    s.wo.append(to_core(s.wo[2]))
    og_far = jnp.concatenate(s.og_far)
    s.og = jnp.concatenate([*s.og, og_far, to_core(og_far)])
    s.fence()
    s.att.append(to_core(s.att[2]))
    s.w_down = assemble_rows(place, s.r + s.ry, width, inner)
    del s.r, s.ry, s.og_far
    s.fence()
    s.nm, s.hidden, s.d_gu, s.mid, s.dnm, dnm_sent, s.lo, s.lo_sent = ffn_call(
        me_arg, s.tok, s.og, s.att, s.wo, s.mlp_gain, ffn_all, s.w_down
    )
    s.dnm, s.dnm_far = halves(s.dnm, to_core(dnm_sent))
    del s.tok, s.att, s.w_down
    s.fence()
    s.dnm_far = to_chip(s.dnm_far)
    pieces = list(columns_grad(place, s.nm, s.d_gu, dp))
    s.f_kept, s.f_sent = pieces[:zs], pieces[zs:]
    s.g_down = down_grad(after(s.hidden, pieces[0]), s.og)
    g_down = lax.psum_scatter(s.g_down, "dp", scatter_dimension=0, tiled=True)
    del s.nm, s.d_gu, s.hidden, s.og
    s.fence()
    s.f_sent[3] = to_y(s.f_sent[3])
    lo_got = to_core(s.lo_sent)
    s.d_middle, s.d_branch, *s.d_att = simple(
        branch_kernel,
        "branch",
        (s.dnm, s.dnm_far, s.mid, s.out_grad, s.mlp_gain, *s.wo),
        [shaped(f32, rows, width), shaped(bf16, rows, width)] + [shaped(bf16, rows, part)] * SEQ,
    )
    s.lo, s.lo_far = halves(s.lo, lo_got)
    del s.dnm, s.dnm_far, s.wo, s.lo_sent, s.g_down
    s.fence()
    s.d_att = exchange_rel(s.d_att)
    s.f_sent[2] = to_y(s.f_sent[2])
    s.f = to_z(total(s.f_kept[3], s.f_sent[3]))
    s.fence()

    def back(pair, *along):
        return attend_back_call(
            pair, place, s.q, s.k, s.v, s.d_att, s.lse, s.segments, s.cos, s.sin, s.nin, dp, True, along
        )

    def other_chip_values(d_pair):
        return lax.dynamic_slice(d_pair, (((me >> 1) ^ 1) * 2 * rows, 256), (2 * rows, 128))

    s.f_sent[1] = to_y(s.f_sent[1])
    s.f = to_z(total(s.f_kept[2], s.f_sent[2], s.f))
    s.d_branch = [s.d_branch, to_core(s.d_branch), to_chip(s.d_branch)]
    d_pair, kept, sent = back(0, s.f_sent[0])
    s.d_qkv, s.kept, s.sent = [d_pair], [kept], [sent]
    s.fence()
    s.sent[0] = to_y(s.sent[0])
    s.f = to_z(total(s.f_kept[1], s.f_sent[1], s.f))
    s.lo_far = to_chip(s.lo_far)
    s.d_branch.append(to_core(s.d_branch[2]))
    s.values_far = to_chip(other_chip_values(s.d_qkv[0]))
    d_pair, kept, sent = back(1)
    s.d_qkv.append(d_pair)
    s.dnin, s.dnin_sent = input_grad(me_arg, s.d_qkv, s.w_qkv)
    s.kept.append(kept)
    s.sent.append(sent)
    del s.nin, s.d_att, s.w_qkv
    s.fence()

    def over_z(first, *others):
        return [first] + [to_z(piece, j + 1) for j, piece in enumerate(others)]

    s.sent[1] = to_y(s.sent[1])
    s.kept[0] = over_z(*slots(s.kept[0], s.sent[0]))
    s.dnin, s.dnin_far = halves(s.dnin, to_core(s.dnin_sent))
    s.out_kept, s.out_sent = out_projection_grad(place, s.attended, s.d_branch, dp)
    del s.d_branch, s.attended, s.dnin_sent
    s.fence()
    s.kept[1] = over_z(*slots(s.kept[1], s.sent[1]))
    s.out_sent = to_y(s.out_sent)
    s.dnin_far = to_chip(s.dnin_far)
    s.layer_out = total(s.mid, s.lo, s.lo_far)
    del s.lo, s.lo_far, s.mid
    s.fence()
    s.mine, s.near, far = cut(me_arg, s.kept, (s.f_kept[0], s.sent[0], s.f), s.d_qkv[1])
    s.far = to_chip(far)
    s.out_kept = over_z(*slots(s.out_kept, s.out_sent))
    s.token_grad = simple(
        token_grad_kernel,
        "token_grad",
        (s.dnin, s.dnin_far, s.tokens, s.attn_gain, s.d_middle),
        [shaped(bf16, rows, width)],
        60,
    )[0]
    s.g_down = g_down
    del s.kept, s.sent, s.out_sent, s.dnin, s.d_middle, s.f, s.f_kept, s.f_sent
    s.fence()
    count = s.mine.shape[0]
    args = (me_arg, s.near, s.far, *s.d_qkv, s.values_far)
    got = to_core(simple(relay_kernel, "relay", args, [shaped(bf16, 2 * count + SEQ * rows, 128)])[0])
    weights = (query_weight, key_weight, value_weight, gate_weight, up_weight)
    shapes = [(w_rows, width)] * 4 + [(1, w_rows)] + [(w_rows, SEQ * inner)] * 2 + [(1, w_rows), g_down.shape]
    args = (s.mine, s.far, got, *s.out_kept, *weights, attn_gain[None], mlp_gain[None], s.g_down)
    a_rows = 3 * part // 128 * w_rows
    g_q, g_k, g_v, g_out, attn_gain_grad, g_gate, g_up, mlp_gain_grad, g_down = pl.pallas_call(
        finish_kernel,
        name="finish",
        grid=(1,),
        in_specs=[SMEM] + [fixed(x.shape) for x in args],
        out_specs=[fixed(x) for x in shapes],
        out_shape=[shaped(f32, *x) for x in shapes],
        scratch_shapes=[pltpu.VMEM((SEQ, a_rows, 128), bf16), pltpu.VMEM((SEQ, count - a_rows, 128), bf16)],
        compiler_params=params(24),
    )(me_arg, *args)
    value_grad_out = simple(
        value_grad_kernel,
        "value_grad",
        (me_arg, value_grad_acc[0], *s.d_qkv, s.values_far, s.far, got),
        [shaped(f32, rows, width)],
    )[0]
    return (
        s.layer_out[None],
        s.token_grad[None],
        value_grad_out[None],
        g_q,
        g_k,
        g_v,
        g_out,
        attn_gain_grad[0],
        g_gate,
        g_up,
        g_down,
        mlp_gain_grad[0],
    )


def body_plain(
    tokens, first_values, value_grad_acc, segment_ids, query_weight, key_weight, value_weight, out_weight,
    attn_gain, gate_weight, up_weight, down_weight, mlp_gain, out_grad,
):
    dp = lax.axis_size("dp")
    rows, width = tokens.shape[1:]
    length = segment_ids.shape[1]
    w_rows, d_rows = query_weight.shape[0], down_weight.shape[0]
    part = width // SEQ
    inner = gate_weight.shape[1] // SEQ
    main = main_lanes(inner)
    me = lax.axis_index("seq").astype(jnp.int32)
    mine = lax.axis_index("dp").astype(jnp.int32)
    me_arg = me[None]
    place = jnp.stack([me, me * dp + mine, mine])

    def columns(weight, count):
        return weight.reshape(w_rows, SEQ, count).transpose(1, 0, 2)

    owner = jnp.arange(width) // w_rows == me * dp + mine

    def spread(gain):
        full = jnp.where(owner, jnp.tile(gain, width // w_rows), jnp.zeros((), bf16))
        cut = 3 * part
        return jnp.stack([full[:cut], jnp.pad(full[cut:], (0, 2 * cut - width))])

    gains = jnp.concatenate([spread(attn_gain), spread(mlp_gain), jnp.zeros((4, 3 * part), bf16)])
    attn_cols = jnp.concatenate([columns(w, part) for w in (query_weight, key_weight, value_weight)], axis=2)
    attn_cols = jnp.concatenate([attn_cols, jnp.broadcast_to(gains[None], (SEQ,) + gains.shape)], axis=1)
    gate_cols, up_cols = columns(gate_weight, inner), columns(up_weight, inner)
    ffn_cols = jnp.concatenate(
        [gate_cols[:, :, :main], up_cols[:, :, :main], gate_cols[:, :, main:], up_cols[:, :, main:]], axis=2
    )
    attn_cols = lax.all_to_all(attn_cols, "seq", split_axis=0, concat_axis=0, tiled=True)
    ffn_cols = lax.all_to_all(ffn_cols, "seq", split_axis=0, concat_axis=0, tiled=True)
    attn_all = lax.all_gather(attn_cols.reshape(-1, 3 * part), "dp", axis=0, tiled=True)
    attn_all = attn_all.reshape(dp, SEQ, w_rows + 8, 3 * part)
    w_qkv = attn_all[:, :, :w_rows].transpose(1, 0, 2, 3).reshape(width, 3 * part)
    gain_all = jnp.sum(attn_all[:, :, w_rows : w_rows + 4].astype(f32), axis=(0, 1))
    attn_gain_all = jnp.concatenate([gain_all[0], gain_all[1]])[None, :width]
    mlp_gain_all = jnp.concatenate([gain_all[2], gain_all[3]])[None, :width]
    w_out = lax.all_gather(out_weight, "dp", axis=0, tiled=True)
    w_down = lax.all_gather(down_weight, "dp", axis=0, tiled=True)
    ffn_all = lax.all_gather(ffn_cols.reshape(-1, 2 * inner), "dp", axis=0, tiled=True)
    w_ffn = ffn_all.reshape(dp, SEQ, w_rows, 2 * inner).transpose(1, 0, 2, 3).reshape(width, 2 * inner)

    cos, sin = rotary(length, width // HEADS)
    tok = jnp.concatenate(gather_rel(tokens[0]))
    og = jnp.concatenate(gather_rel(out_grad[0]))
    first_cols = first_values[0].reshape(rows, SEQ, part)
    first = exchange_rel([lax.dynamic_index_in_dim(first_cols, me ^ k, 1, keepdims=False) for k in range(SEQ)])
    nin, q, k, v = qkv_call(me_arg, tok, jnp.concatenate(first), w_qkv, attn_gain_all, cos, sin)
    attended, lse = attend_call(q, k, v, segment_ids)
    wo = gather_rel(w_out)
    nm, hidden, d_gu, mid, *sums = ffn_call(me_arg, tok, og, gather_rel(attended), wo, mlp_gain_all, w_ffn, w_down)
    layer_out = (mid + scatter_sum(*sums[2:])).astype(bf16)
    d_middle = out_grad[0].astype(f32) + back_through_norm(scatter_sum(*sums[:2]), mid, mlp_gain_all)
    d_branch = d_middle.astype(bf16)
    d_att = exchange_rel([mul(d_branch, w, 1, 1).astype(bf16) for w in wo])
    d_branch_all = jnp.stack(gather_rel(d_branch))[me ^ jnp.arange(SEQ)].reshape(length, width)
    d_qkv = [
        attend_back_call(pair, place, q, k, v, d_att, lse, segment_ids, cos, sin, nin, dp, False)[0] for pair in range(2)
    ]
    dnin = scatter_sum(*input_grad(me_arg, d_qkv, w_qkv))
    token_grad = d_middle + back_through_norm(dnin, tokens[0].astype(f32), attn_gain_all)
    dv = jnp.concatenate([d[:, 256:] for d in d_qkv], axis=1)
    dv = exchange_rel([lax.dynamic_slice_in_dim(dv, (me ^ i) * rows, rows, 0) for i in range(SEQ)])
    dv = jnp.stack(dv)[me ^ jnp.arange(SEQ)].transpose(1, 0, 2).reshape(rows, width)
    value_grad_out = value_grad_acc[0] + dv.astype(f32)

    def over_dp(grads):
        return lax.psum_scatter(grads.reshape(-1, 128), "dp", scatter_dimension=0, tiled=True)

    def to_rows(sums):
        sums = sums.reshape(SEQ, -1, 128)
        return jnp.stack(exchange_rel([lax.dynamic_index_in_dim(sums, me ^ i, 0, keepdims=False) for i in range(SEQ)]))

    attn_sums = over_dp(columns_grad_plain(nin, jnp.concatenate(d_qkv, axis=1), dp))
    ffn_sums = over_dp(columns_grad_plain(nm, d_gu, dp))
    g_out = lax.psum_scatter(mul(attended, d_branch_all, 0, 0).astype(bf16), "dp", scatter_dimension=0, tiled=True)
    g_down = lax.psum_scatter(mul(hidden, og, 0, 0).astype(bf16), "dp", scatter_dimension=0, tiled=True)
    weights = (query_weight, key_weight, value_weight, gate_weight, up_weight)
    shapes = [(w_rows, width)] * 3 + [(1, w_rows)] + [(w_rows, SEQ * inner)] * 2 + [(1, w_rows)]
    args = (me_arg, to_rows(attn_sums), to_rows(ffn_sums), *weights, attn_gain[None], mlp_gain[None])
    g_q, g_k, g_v, attn_gain_grad, g_gate, g_up, mlp_gain_grad = simple(
        unpack_kernel, "unpack", args, [shaped(f32, *x) for x in shapes]
    )
    return (
        layer_out[None],
        token_grad.astype(bf16)[None],
        value_grad_out[None],
        g_q,
        g_k,
        g_v,
        g_out.astype(f32),
        attn_gain_grad[0],
        g_gate,
        g_up,
        g_down.astype(f32),
        mlp_gain_grad[0],
    )


def solution(mesh):
    token = P("dp", "seq", None)
    weight = P(("seq", "dp"), None)
    gain = P(("seq", "dp"))
    return jax.shard_map(
        body_direct if mesh.shape["dp"] == 8 else body_plain,
        mesh=mesh,
        in_specs=(token, token, token, P("dp", None), weight, weight, weight, weight, gain, weight, weight, weight, gain, token),
        out_specs=(token, token, token, weight, weight, weight, weight, gain, weight, weight, weight, gain),
        check_vma=False,
    )
```

profile of v0, /device:TPU:0, one launch (start us, length us, event | category | flops | bytes accessed | tf_op | source)
XLA Modules:
  0.0 269.2 jit_solution(5301186007952340303)
XLA Ops:
  7.8 2.3 pack_attn.1
  10.1 3.1 %collective-permute-start.3 = (bf16[704,128]{1,0:T(8,128)(2,1)}, bf16[704,128]{1,0:T(8,128)(2,1)S(1)}, u32[]{:S(2)}, u32[]{:S(2)}) collective-permute-start(bf16[704,128]{1,0:T(8,128)(2,1)} %get-tuple-element.739.refs_0_), channel_id=1, source_target_pairs={{0,2},{1,3},{2,4},{3,5},{4,6},{5,7},{6,0},{7,1},{8,10},{9,11},{10,... | collective-permute-start | bytes 540680 | tf_op jit(solution)/shard_map/ppermute | solution.py:877
  13.2 1.5 collective-permute-start.4
  14.7 1.5 collective-permute-start.1
  16.6 2.6 collective-permute-done.1
  22.1 1.6 collective-permute-start.6
  24.4 1.5 collective-permute-start.5
  25.8 3.1 %fusion = (f32[1024,32]{1,0:T(8,128)}, f32[1024,32]{1,0:T(8,128)}, f32[1024,32]{1,0:T(8,128)}) fusion(f32[32]{0:T(128)S(1)} %multiply_exponential_fusion, f32[1024]{0:T(1024)S(1)} %iota_convert_fusion), kind=kLoop, calls=%fused_computation.8 | loop fusion | flops 65536 | bytes 397440 | tf_op jit(solution)/shard_map/neg | solution.py:885
  29.0 2.3 pack_ffn.1
  33.4 1.4 collective-permute-start.8
  34.7 1.3 collective-permute-start.9
  36.1 1.3 collective-permute-start.11
  38.0 3.4 %pad_maximum_fusion = (f32[1024,128]{1,0:T(8,128)S(1)}, f32[1024,128]{1,0:T(8,128)S(1)}) fusion(f32[1024,32]{1,0:T(8,128)} %get-tuple-element.1068, f32[1024,32]{1,0:T(8,128)} %get-tuple-element.1067, f32[1024,32]{1,0:T(8,128)} %get-tuple-element.1066), kind=kLoop, calls=%fused_computation.2 | loop fusion | flops 786432 | bytes 1441792 | tf_op jit(solution)/shard_map/concatenate | solution.py:885
  41.4 1.3 collective-permute-done.11
  47.0 6.3 %collective-permute-done.13 = bf16[128,1024]{1,0:T(8,128)(2,1)S(1)} collective-permute-done((bf16[128,1024]{1,0:T(8,128)(2,1)}, bf16[128,1024]{1,0:T(8,128)(2,1)S(1)}, u32[]{:S(2)}, u32[]{:S(2)}) %collective-permute-start.13) | collective-permute-done | bytes 262176 | tf_op jit(solution)/shard_map/ppermute | solution.py:844
  53.4 1.4 collective-permute-done.14.refs_3_
  59.0 1.5 collective-permute-done.19
  60.5 1.7 collective-permute-done.18
  62.3 2.9 %collective-permute-done.20.refs_7_ = bf16[1088,128]{1,0:T(8,128)(2,1)S(1)} collective-permute-done((bf16[1088,128]{1,0:T(8,128)(2,1)S(1)}, bf16[1088,128]{1,0:T(8,128)(2,1)S(1)}, u32[]{:S(2)}, u32[]{:S(2)}) %collective-permute-start.20) | collective-permute-done | bytes 278560 | tf_op jit(solution)/shard_map/ppermute | solution.py:872
  68.3 3.4 %qkv.1 = (bf16[1024,1024]{1,0:T(8,128)(2,1)S(1)}, bf16[1024,256]{1,0:T(8,128)(2,1)S(1)}, bf16[1024,256]{1,0:T(8,128)(2,1)S(1)}, bf16[1024,256]{1,0:T(8,128)(2,1)S(1)}) custom-call(s32[1]{0:T(128)} %bitcast.me_ref, bf16[1024,1024]{1,0:T(8,128)(2,1)S(1)} %constant_dynamic-update-slice_fusion.5.tok_ref, bf16[1024,256]{1,0:T(8,128)(2,1)S(1)} %pad_maximum_fusion.2.first_ref, ...), custom_call_target="tpu_custom_call" | custom-call | tf_op jit(solution)/shard_map/qkv/pallas_call | solution.py:76
  71.7 1.4 copy-done.5
  73.1 1.5 collective-permute-done.22.refs_2_
  74.7 1.3 collective-permute-start.30
  77.8 9.0 %attend.1 = (bf16[1024,256]{1,0:T(8,128)(2,1)S(1)}, f32[2,2,1024]{2,1,0:T(2,128)S(1)}) custom-call(bf16[1024,256]{1,0:T(8,128)(2,1)S(1)} %get-tuple-element.923.q_ref, bf16[1024,256]{1,0:T(8,128)(2,1)S(1)} %get-tuple-element.924.k_ref, bf16[1024,256]{1,0:T(8,128)(2,1)S(1)} %get-tuple-element.925.v_ref, s32[1,1024]{1,0:T(1,128)S(1)} %copy-done.74), custom_call_target="tpu_custom_call" | custom-call | tf_op jit(solution)/shard_map/attend/pallas_call | solution.py:152
  86.8 2.6 collective-permute-done.26.refs_3_
  89.5 5.2 %collective-permute-done.28 = bf16[128,1024]{1,0:T(8,128)(2,1)S(1)} collective-permute-done((bf16[128,1024]{1,0:T(8,128)(2,1)S(1)}, bf16[128,1024]{1,0:T(8,128)(2,1)S(1)}, u32[]{:S(2)}, u32[]{:S(2)}) %collective-permute-start.28) | collective-permute-done | bytes 262176 | tf_op jit(solution)/shard_map/ppermute | solution.py:844
  95.3 1.2 collective-permute-start.35
  97.6 5.2 %collective-permute-done.31.refs_7_ = bf16[704,128]{1,0:T(8,128)(2,1)S(1)} collective-permute-done((bf16[704,128]{1,0:T(8,128)(2,1)S(1)}, bf16[704,128]{1,0:T(8,128)(2,1)S(1)}, u32[]{:S(2)}, u32[]{:S(2)}) %collective-permute-start.31) | collective-permute-done | bytes 180256 | tf_op jit(solution)/shard_map/ppermute | solution.py:872
  102.8 6.4 %collective-permute-done.35.a2 = bf16[1024,256]{1,0:T(8,128)(2,1)S(1)} collective-permute-done((bf16[1024,256]{1,0:T(8,128)(2,1)S(1)}, bf16[1024,256]{1,0:T(8,128)(2,1)S(1)}, u32[]{:S(2)}, u32[]{:S(2)}) %collective-permute-start.35) | collective-permute-done | bytes 524320 | tf_op jit(solution)/shard_map/ppermute | solution.py:844
  112.0 21.1 %ffn.1 = (bf16[1024,1024]{1,0:T(8,128)(2,1)}, bf16[1024,704]{1,0:T(8,128)(2,1)}, bf16[1024,1408]{1,0:T(8,128)(2,1)}, f32[256,1024]{1,0:T(8,128)}, bf16[512,1024]...) custom-call(s32[1]{0:T(128)} %bitcast.me_ref, ...), custom_call_target="tpu_custom_call" | custom-call | tf_op jit(solution)/shard_map/ffn/pallas_call | solution.py:478
  133.8 2.5 collective-permute-done.37.got_ref
  139.4 1.2 collective-permute-start.38
  140.6 8.1 %columns_grad.1 = (bf16[1408,128]{1,0:T(8,128)(2,1)}, bf16[1408,128]{1,0:T(8,128)(2,1)}, bf16[1408,128]{1,0:T(8,128)(2,1)}, bf16[1408,128]{1,0:T(8,128)(2,1)}, b...) custom-call(s32[3]{0:T(128)} %pad_add_fusion.place_ref, ...), custom_call_target="tpu_custom_call" | custom-call | tf_op jit(solution)/shard_map/columns_grad/pallas_call | solution.py:538
  148.8 5.6 %down_grad.1 = bf16[704,1024]{1,0:T(8,128)(2,1)} custom-call(bf16[1024,704]{1,0:T(8,128)(2,1)} %get-tuple-element.817.act_ref, bf16[1024,1024]{1,0:T(8,128)(2,1)} %copy-done.80), custom_call_target="tpu_custom_call" | custom-call | tf_op jit(solution)/shard_map/down_grad/pallas_call | solution.py:598
  156.4 1.2 copy-done.38
  157.6 2.8 %branch.1 = (f32[256,1024]{1,0:T(8,128)S(1)}, bf16[256,1024]{1,0:T(8,128)(2,1)}, bf16[256,256]{1,0:T(8,128)(2,1)S(1)}, bf16[256,256]{1,0:T(8,128)(2,1)S(1)}, bf1...) custom-call(f32[256,1024]{1,0:T(8,128)S(1)} %copy-done.38, bf16[256,1024]{1,0:T(8,128)(2,1)} %collective-permute-done.38.far_ref, ...), custom_call_target="tpu_custom_call" | custom-call | tf_op jit(solution)/shard_map/branch/pallas_call | solution.py:610
  162.5 2.8 %collective-permute-done.40.refs_1_ = bf16[1408,128]{1,0:T(8,128)(2,1)S(1)} collective-permute-done((bf16[1408,128]{1,0:T(8,128)(2,1)S(1)}, bf16[1408,128]{1,0:T(8,128)(2,1)S(1)}, u32[]{:S(2)}, u32[]{:S(2)}) %collective-permute-start.40) | collective-permute-done | bytes 360480 | tf_op jit(solution)/shard_map/ppermute | solution.py:872
  168.4 4.4 %collective-permute-done.43.d2 = bf16[256,256]{1,0:T(8,128)(2,1)S(1)} collective-permute-done((bf16[256,256]{1,0:T(8,128)(2,1)S(1)}, bf16[256,256]{1,0:T(8,128)(2,1)S(1)}, u32[]{:S(2)}, u32[]{:S(2)}) %collective-permute-start.43) | collective-permute-done | bytes 131104 | tf_op jit(solution)/shard_map/ppermute | solution.py:844
  172.8 2.0 collective-permute-done.44.d3
  175.3 2.5 collective-permute-done.45.refs_2_
  180.3 11.0 %attend_back.2 = (bf16[1024,384]{1,0:T(8,128)(2,1)}, bf16[4,384,128]{2,1,0:T(8,128)(2,1)}, bf16[2944,128]{1,0:T(8,128)(2,1)}) custom-call(s32[3]{0:T(128)} %pad_add_fusion.place_ref, bf16[1024,256]{1,0:T(8,128)(2,1)} %copy-done.10, bf16[1024,256]{1,0:T(8,128)(2,1)} %copy-done.11, bf16[1024,256]{1,0:T(8,128)(2,1)} %copy-done.12, bf16[256,256]{1,0:T(8,128)(2,1)} %copy-done.41, ...), custom_call_target="tpu_custom_call" | custom-call | tf_op jit(solution)/shard_map/attend_back/pallas_call | solution.py:236
  191.3 1.6 collective-permute-done.49.refs_2_
  194.0 1.2 collective-permute-start.51
  197.9 10.9 %attend_back.3 = (bf16[1024,384]{1,0:T(8,128)(2,1)}, bf16[4,384,128]{2,1,0:T(8,128)(2,1)}, bf16[1536,128]{1,0:T(8,128)(2,1)}) custom-call(s32[3]{0:T(128)} %pad_add_fusion.place_ref, bf16[1024,256]{1,0:T(8,128)(2,1)} %copy-done.10, bf16[1024,256]{1,0:T(8,128)(2,1)} %copy-done.11, bf16[1024,256]{1,0:T(8,128)(2,1)} %copy-done.12, bf16[256,256]{1,0:T(8,128)(2,1)} %copy-done.41, ...), custom_call_target="tpu_custom_call" | custom-call | tf_op jit(solution)/shard_map/attend_back/pallas_call | solution.py:236
  210.0 2.7 input_grad.1
  212.7 1.9 collective-permute-done.52.refs_10_
  214.7 1.6 collective-permute-start.58
  216.4 2.7 %collective-permute-start.56 = (bf16[384,128]{1,0:T(8,128)(2,1)S(1)}, bf16[384,128]{1,0:T(8,128)(2,1)S(1)}, u32[]{:S(2)}, u32[]{:S(2)}) collective-permute-start(bf16[384,128]{1,0:T(8,128)(2,1)S(1)} %get-tuple-element.967), channel_id=1, source_target_pairs={{0,4},{1,5},{2,6},{3,7},{4,0},{5,1},{6,2},{7,3},{8,12},{9,13},{10,... | collective-permute-start | bytes 294920 | tf_op jit(solution)/shard_map/ppermute | solution.py:877
  219.2 1.3 collective-permute-start.57
  220.5 2.2 out_projection_grad.1
  224.0 3.3 %collective-permute-done.56.refs_2_ = bf16[384,128]{1,0:T(8,128)(2,1)S(1)} collective-permute-done((bf16[384,128]{1,0:T(8,128)(2,1)S(1)}, bf16[384,128]{1,0:T(8,128)(2,1)S(1)}, u32[]{:S(2)}, u32[]{:S(2)}) %collective-permute-start.56) | collective-permute-done | bytes 98336 | tf_op jit(solution)/shard_map/ppermute | solution.py:877
  228.4 1.4 collective-permute-start.63
  229.8 1.4 collective-permute-start.64
  231.4 2.4 collective-permute-start.61
  233.8 1.6 collective-permute-start.62
  235.4 2.0 total.7
  237.3 1.6 collective-permute-done.60.refs_5_
  238.9 4.6 %collective-permute-done.61.refs_6_ = bf16[384,128]{1,0:T(8,128)(2,1)S(1)} collective-permute-done((bf16[384,128]{1,0:T(8,128)(2,1)S(1)}, bf16[384,128]{1,0:T(8,128)(2,1)S(1)}, u32[]{:S(2)}, u32[]{:S(2)}) %collective-permute-start.61) | collective-permute-done | bytes 98336 | tf_op jit(solution)/shard_map/ppermute | solution.py:877
  243.5 2.1 cut.1
  247.6 2.2 collective-permute-start.65
  249.8 2.3 collective-permute-start.66
  252.1 3.1 %token_grad.1 = bf16[256,1024]{1,0:T(8,128)(2,1)} custom-call(f32[256,1024]{1,0:T(8,128)} %copy-done.36, bf16[256,1024]{1,0:T(8,128)(2,1)} %copy-done.89, bf16[256,1024]{1,0:T(8,128)(2,1)} %bitcast.31, f32[1,1024]{1,0:T(1,128)} %bitcast.23, f32[256,1024]{1,0:T(8,128)} %copy-done.35), custom_call_target="tpu_custom_call" | custom-call | tf_op jit(solution)/shard_map/token_grad/pallas_call | solution.py:610
  256.8 1.9 collective-permute-done.69.got_ref
  260.1 2.3 finish.1
  (328 shorter events, 51.3 us)
Async XLA Ops:
  7.2 104.1 %all-gather.3.cloned.1.call-start = ((), (), s32[]{:S(2)}) async-start(), calls=%async_computation.2 | async-start | bytes 3244032 | tf_op jit(solution)/shard_map/all_gather | solution.py:938
  10.1 10.1 %collective-permute-start.3 = (bf16[704,128]{1,0:T(8,128)(2,1)}, bf16[704,128]{1,0:T(8,128)(2,1)S(1)}, u32[]{:S(2)}, u32[]{:S(2)}) collective-permute-start(bf16[704,128]{1,0:T(8,128)(2,1)} %get-tuple-element.739.refs_0_), channel_id=1, source_target_pairs={{0,2},{1,3},{2,4},{3,5},{4,6},{5,7},{6,0},{7,1},{8,10},{9,11},{10,... | collective-permute-start | bytes 540680 | tf_op jit(solution)/shard_map/ppermute | solution.py:877
  13.2 7.0 %collective-permute-start.4 = (bf16[704,128]{1,0:T(8,128)(2,1)}, bf16[704,128]{1,0:T(8,128)(2,1)S(1)}, u32[]{:S(2)}, u32[]{:S(2)}) collective-permute-start(bf16[704,128]{1,0:T(8,128)(2,1)} %get-tuple-element.739.refs_0_), channel_id=1, source_target_pairs={{0,1},{1,0},{2,3},{3,2},{4,5},{5,4},{6,7},{7,6},{8,9},{9,8},{10,11... | collective-permute-start | bytes 540680 | tf_op jit(solution)/shard_map/ppermute | solution.py:872
  22.1 10.6 %collective-permute-start.6 = (bf16[1088,128]{1,0:T(8,128)(2,1)S(1)}, bf16[1088,128]{1,0:T(8,128)(2,1)S(1)}, u32[]{:S(2)}, u32[]{:S(2)}) collective-permute-start(bf16[1088,128]{1,0:T(8,128)(2,1)S(1)} %constant_dynamic-update-slice_fusion.refs_0_), channel_id=1, source_target_pairs={{0,2},{1,3},{2,4},{3,5},{4,6},{5,7},{6,0},{7,1},{8,10},{9,11},{10,... | collective-permute-start | bytes 835592 | tf_op jit(solution)/shard_map/ppermute | solution.py:877
  23.7 8.9 %collective-permute-start.7 = (bf16[1088,128]{1,0:T(8,128)(2,1)S(1)}, bf16[1088,128]{1,0:T(8,128)(2,1)S(1)}, u32[]{:S(2)}, u32[]{:S(2)}) collective-permute-start(bf16[1088,128]{1,0:T(8,128)(2,1)S(1)} %constant_dynamic-update-slice_fusion.refs_0_), channel_id=1, source_target_pairs={{0,1},{1,0},{2,3},{3,2},{4,5},{5,4},{6,7},{7,6},{8,9},{9,8},{10,11... | collective-permute-start | bytes 835592 | tf_op jit(solution)/shard_map/ppermute | solution.py:872
  24.4 8.1 %collective-permute-start.5 = (bf16[128,1024]{1,0:T(8,128)(2,1)}, bf16[128,1024]{1,0:T(8,128)(2,1)S(1)}, u32[]{:S(2)}, u32[]{:S(2)}) collective-permute-start(bf16[128,1024]{1,0:T(8,128)(2,1)} %get-tuple-element.560), channel_id=1, source_target_pairs={{0,16},{8,24},{16,0},{24,8},{1,17},{9,25},{17,1},{25,9},{2,18},{10... | collective-permute-start | bytes 786440 | tf_op jit(solution)/shard_map/ppermute | solution.py:844
  33.4 10.1 %collective-permute-start.8 = (bf16[1088,128]{1,0:T(8,128)(2,1)S(1)}, bf16[1088,128]{1,0:T(8,128)(2,1)S(1)}, u32[]{:S(2)}, u32[]{:S(2)}) collective-permute-start(bf16[1088,128]{1,0:T(8,128)(2,1)S(1)} %collective-permute-done.6.refs_1_), channel_id=1, source_target_pairs={{0,2},{1,3},{2,4},{3,5},{4,6},{5,7},{6,0},{7,1},{8,10},{9,11},{10,... | collective-permute-start | bytes 835592 | tf_op jit(solution)/shard_map/ppermute | solution.py:877
  34.7 8.8 %collective-permute-start.9 = (bf16[1088,128]{1,0:T(8,128)(2,1)S(1)}, bf16[1088,128]{1,0:T(8,128)(2,1)S(1)}, u32[]{:S(2)}, u32[]{:S(2)}) collective-permute-start(bf16[1088,128]{1,0:T(8,128)(2,1)S(1)} %collective-permute-done.6.refs_1_), channel_id=1, source_target_pairs={{0,1},{1,0},{2,3},{3,2},{4,5},{5,4},{6,7},{7,6},{8,9},{9,8},{10,11... | collective-permute-start | bytes 835592 | tf_op jit(solution)/shard_map/ppermute | solution.py:872
  36.1 5.3 %collective-permute-start.12 = (bf16[352,128]{1,0:T(8,128)(2,1)}, bf16[352,128]{1,0:T(8,128)(2,1)S(1)}, u32[]{:S(2)}, u32[]{:S(2)}) collective-permute-start(bf16[352,128]{1,0:T(8,128)(2,1)} %get-tuple-element.593), channel_id=1, source_target_pairs={{0,24},{8,16},{16,8},{24,0},{1,25},{9,17},{17,9},{25,1},{2,26},{10... | collective-permute-start | bytes 270344 | tf_op jit(solution)/shard_map/ppermute | solution.py:848
  36.1 6.7 %collective-permute-start.11 = (bf16[352,128]{1,0:T(8,128)(2,1)}, bf16[352,128]{1,0:T(8,128)(2,1)S(1)}, u32[]{:S(2)}, u32[]{:S(2)}) collective-permute-start(bf16[352,128]{1,0:T(8,128)(2,1)} %get-tuple-element.592), channel_id=1, source_target_pairs={{0,16},{8,24},{16,0},{24,8},{1,17},{9,25},{17,1},{25,9},{2,18},{10... | collective-permute-start | bytes 270344 | tf_op jit(solution)/shard_map/ppermute | solution.py:844
  37.4 5.4 %collective-permute-start.10 = (bf16[352,128]{1,0:T(8,128)(2,1)}, bf16[352,128]{1,0:T(8,128)(2,1)S(1)}, u32[]{:S(2)}, u32[]{:S(2)}) collective-permute-start(bf16[352,128]{1,0:T(8,128)(2,1)} %get-tuple-element.591), channel_id=1, source_target_pairs={{0,8},{8,0},{16,24},{24,16},{1,9},{9,1},{17,25},{25,17},{2,10},{10... | collective-permute-start | bytes 270344 | tf_op jit(solution)/shard_map/ppermute | solution.py:840
  43.6 211.7 %reduce-scatter.2.cloned.1.call-start = ((), (), s32[]{:S(2)}) async-start(), calls=%async_computation.1 | async-start | bytes 1622016 | tf_op jit(solution)/shard_map/reduce_scatter | solution.py:990
  43.6 11.1 %collective-permute-start.16 = (bf16[256,1024]{1,0:T(8,128)(2,1)S(1)}, bf16[256,1024]{1,0:T(8,128)(2,1)}, u32[]{:S(2)}, u32[]{:S(2)}) collective-permute-start(bf16[256,1024]{1,0:T(8,128)(2,1)S(1)} %bitcast.32), channel_id=1, source_target_pairs={{0,8},{8,0},{16,24},{24,16},{1,9},{9,1},{17,25},{25,17},{2,10},{10... | collective-permute-start | bytes 1572872 | tf_op jit(solution)/shard_map/ppermute | solution.py:840
  44.0 10.7 %collective-permute-start.14 = (bf16[1088,128]{1,0:T(8,128)(2,1)S(1)}, bf16[1088,128]{1,0:T(8,128)(2,1)S(1)}, u32[]{:S(2)}, u32[]{:S(2)}) collective-permute-start(bf16[1088,128]{1,0:T(8,128)(2,1)S(1)} %collective-permute-done.8.refs_2_), channel_id=1, source_target_pairs={{0,2},{1,3},{2,4},{3,5},{4,6},{5,7},{6,0},{7,1},{8,10},{9,11},{10,... | collective-permute-start | bytes 835592 | tf_op jit(solution)/shard_map/ppermute | solution.py:877
  44.2 10.5 %collective-permute-start.15 = (bf16[1088,128]{1,0:T(8,128)(2,1)S(1)}, bf16[1088,128]{1,0:T(8,128)(2,1)S(1)}, u32[]{:S(2)}, u32[]{:S(2)}) collective-permute-start(bf16[1088,128]{1,0:T(8,128)(2,1)S(1)} %collective-permute-done.8.refs_2_), channel_id=1, source_target_pairs={{0,1},{1,0},{2,3},{3,2},{4,5},{5,4},{6,7},{7,6},{8,9},{9,8},{10,11... | collective-permute-start | bytes 835592 | tf_op jit(solution)/shard_map/ppermute | solution.py:872
  45.1 8.2 %collective-permute-start.13 = (bf16[128,1024]{1,0:T(8,128)(2,1)}, bf16[128,1024]{1,0:T(8,128)(2,1)S(1)}, u32[]{:S(2)}, u32[]{:S(2)}) collective-permute-start(bf16[128,1024]{1,0:T(8,128)(2,1)} %get-tuple-element.597), channel_id=1, source_target_pairs={{0,16},{8,24},{16,0},{24,8},{1,17},{9,25},{17,1},{25,9},{2,18},{10... | collective-permute-start | bytes 786440 | tf_op jit(solution)/shard_map/ppermute | solution.py:844
  54.7 5.7 %collective-permute-start.19 = (bf16[256,256]{1,0:T(8,128)(2,1)S(1)}, bf16[256,256]{1,0:T(8,128)(2,1)S(1)}, u32[]{:S(2)}, u32[]{:S(2)}) collective-permute-start(bf16[256,256]{1,0:T(8,128)(2,1)S(1)} %get-tuple-element.616), channel_id=1, source_target_pairs={{0,24},{8,16},{16,8},{24,0},{1,25},{9,17},{17,9},{25,1},{2,26},{10... | collective-permute-start | bytes 393224 | tf_op jit(solution)/shard_map/ppermute | solution.py:848
  54.7 7.4 %collective-permute-start.18 = (bf16[256,256]{1,0:T(8,128)(2,1)S(1)}, bf16[256,256]{1,0:T(8,128)(2,1)S(1)}, u32[]{:S(2)}, u32[]{:S(2)}) collective-permute-start(bf16[256,256]{1,0:T(8,128)(2,1)S(1)} %get-tuple-element.615), channel_id=1, source_target_pairs={{0,16},{8,24},{16,0},{24,8},{1,17},{9,25},{17,1},{25,9},{2,18},{10... | collective-permute-start | bytes 393224 | tf_op jit(solution)/shard_map/ppermute | solution.py:844
  55.6 6.6 %collective-permute-start.17 = (bf16[256,256]{1,0:T(8,128)(2,1)S(1)}, bf16[256,256]{1,0:T(8,128)(2,1)S(1)}, u32[]{:S(2)}, u32[]{:S(2)}) collective-permute-start(bf16[256,256]{1,0:T(8,128)(2,1)S(1)} %get-tuple-element.614), channel_id=1, source_target_pairs={{0,8},{8,0},{16,24},{24,16},{1,9},{9,1},{17,25},{25,17},{2,10},{10... | collective-permute-start | bytes 393224 | tf_op jit(solution)/shard_map/ppermute | solution.py:840
  56.6 8.6 %collective-permute-start.20 = (bf16[1088,128]{1,0:T(8,128)(2,1)S(1)}, bf16[1088,128]{1,0:T(8,128)(2,1)S(1)}, u32[]{:S(2)}, u32[]{:S(2)}) collective-permute-start(bf16[1088,128]{1,0:T(8,128)(2,1)S(1)} %collective-permute-done.14.refs_3_), channel_id=1, source_target_pairs={{0,1},{1,0},{2,3},{3,2},{4,5},{5,4},{6,7},{7,6},{8,9},{9,8},{10,11... | collective-permute-start | bytes 835592 | tf_op jit(solution)/shard_map/ppermute | solution.py:872
  57.5 4.7 %collective-permute-start.21 = (bf16[256,1024]{1,0:T(8,128)(2,1)S(1)}, bf16[256,1024]{1,0:T(8,128)(2,1)S(1)}, u32[]{:S(2)}, u32[]{:S(2)}) collective-permute-start(bf16[256,1024]{1,0:T(8,128)(2,1)S(1)} %pad_maximum_fusion.3), channel_id=1, source_target_pairs={{0,8},{8,0},{16,24},{24,16},{1,9},{9,1},{17,25},{25,17},{2,10},{10... | collective-permute-start | bytes 1572872 | tf_op jit(solution)/shard_map/ppermute | solution.py:840
  65.2 9.4 %collective-permute-start.25 = (bf16[256,1024]{1,0:T(8,128)(2,1)S(1)}, bf16[256,1024]{1,0:T(8,128)(2,1)S(1)}, u32[]{:S(2)}, u32[]{:S(2)}) collective-permute-start(bf16[256,1024]{1,0:T(8,128)(2,1)S(1)} %bitcast.18), channel_id=1, source_target_pairs={{0,8},{8,0},{16,24},{24,16},{1,9},{9,1},{17,25},{25,17},{2,10},{10... | collective-permute-start | bytes 1572872 | tf_op jit(solution)/shard_map/ppermute | solution.py:840
  65.2 9.4 %collective-permute-start.24 = (bf16[128,1024]{1,0:T(8,128)(2,1)S(1)}, bf16[128,1024]{1,0:T(8,128)(2,1)S(1)}, u32[]{:S(2)}, u32[]{:S(2)}) collective-permute-start(bf16[128,1024]{1,0:T(8,128)(2,1)S(1)} %get-tuple-element.642), channel_id=1, source_target_pairs={{0,16},{8,24},{16,0},{24,8},{1,17},{9,25},{17,1},{25,9},{2,18},{10... | collective-permute-start | bytes 786440 | tf_op jit(solution)/shard_map/ppermute | solution.py:844
  65.9 8.6 %collective-permute-start.22 = (bf16[704,128]{1,0:T(8,128)(2,1)S(1)}, bf16[704,128]{1,0:T(8,128)(2,1)S(1)}, u32[]{:S(2)}, u32[]{:S(2)}) collective-permute-start(bf16[704,128]{1,0:T(8,128)(2,1)S(1)} %copy-done.63), channel_id=1, source_target_pairs={{0,2},{1,3},{2,4},{3,5},{4,6},{5,7},{6,0},{7,1},{8,10},{9,11},{10,... | collective-permute-start | bytes 540680 | tf_op jit(solution)/shard_map/ppermute | solution.py:877
  65.9 8.6 %collective-permute-start.23 = (bf16[704,128]{1,0:T(8,128)(2,1)S(1)}, bf16[704,128]{1,0:T(8,128)(2,1)S(1)}, u32[]{:S(2)}, u32[]{:S(2)}) collective-permute-start(bf16[704,128]{1,0:T(8,128)(2,1)S(1)} %copy-done.63), channel_id=1, source_target_pairs={{0,1},{1,0},{2,3},{3,2},{4,5},{5,4},{6,7},{7,6},{8,9},{9,8},{10,11... | collective-permute-start | bytes 540680 | tf_op jit(solution)/shard_map/ppermute | solution.py:872
  74.6 20.0 %collective-permute-start.29 = (bf16[256,1024]{1,0:T(8,128)(2,1)S(1)}, bf16[256,1024]{1,0:T(8,128)(2,1)S(1)}, u32[]{:S(2)}, u32[]{:S(2)}) collective-permute-start(bf16[256,1024]{1,0:T(8,128)(2,1)S(1)} %get-tuple-element.847.wo0.w0), channel_id=1, source_target_pairs={{0,8},{8,0},{16,24},{24,16},{1,9},{9,1},{17,25},{25,17},{2,10},{10... | collective-permute-start | bytes 1572872 | tf_op jit(solution)/shard_map/ppermute | solution.py:840
  74.7 20.0 %collective-permute-start.30 = (bf16[256,1024]{1,0:T(8,128)(2,1)S(1)}, bf16[256,1024]{1,0:T(8,128)(2,1)S(1)}, u32[]{:S(2)}, u32[]{:S(2)}) collective-permute-start(bf16[256,1024]{1,0:T(8,128)(2,1)S(1)} %get-tuple-element.847.wo0.w0), channel_id=1, source_target_pairs={{0,16},{8,24},{16,0},{24,8},{1,17},{9,25},{17,1},{25,9},{2,18},{10... | collective-permute-start | bytes 1572872 | tf_op jit(solution)/shard_map/ppermute | solution.py:844
  76.0 18.6 %collective-permute-start.28 = (bf16[128,1024]{1,0:T(8,128)(2,1)S(1)}, bf16[128,1024]{1,0:T(8,128)(2,1)S(1)}, u32[]{:S(2)}, u32[]{:S(2)}) collective-permute-start(bf16[128,1024]{1,0:T(8,128)(2,1)S(1)} %get-tuple-element.673), channel_id=1, source_target_pairs={{0,16},{8,24},{16,0},{24,8},{1,17},{9,25},{17,1},{25,9},{2,18},{10... | collective-permute-start | bytes 786440 | tf_op jit(solution)/shard_map/ppermute | solution.py:844
  76.8 12.7 %collective-permute-start.26 = (bf16[704,128]{1,0:T(8,128)(2,1)S(1)}, bf16[704,128]{1,0:T(8,128)(2,1)S(1)}, u32[]{:S(2)}, u32[]{:S(2)}) collective-permute-start(bf16[704,128]{1,0:T(8,128)(2,1)S(1)} %collective-permute-done.22.refs_2_), channel_id=1, source_target_pairs={{0,2},{1,3},{2,4},{3,5},{4,6},{5,7},{6,0},{7,1},{8,10},{9,11},{10,... | collective-permute-start | bytes 540680 | tf_op jit(solution)/shard_map/ppermute | solution.py:877
  76.9 12.6 %collective-permute-start.27 = (bf16[704,128]{1,0:T(8,128)(2,1)S(1)}, bf16[704,128]{1,0:T(8,128)(2,1)S(1)}, u32[]{:S(2)}, u32[]{:S(2)}) collective-permute-start(bf16[704,128]{1,0:T(8,128)(2,1)S(1)} %collective-permute-done.22.refs_2_), channel_id=1, source_target_pairs={{0,1},{1,0},{2,3},{3,2},{4,5},{5,4},{6,7},{7,6},{8,9},{9,8},{10,11... | collective-permute-start | bytes 540680 | tf_op jit(solution)/shard_map/ppermute | solution.py:872
  94.8 8.0 %collective-permute-start.34 = (bf16[1024,256]{1,0:T(8,128)(2,1)S(1)}, bf16[1024,256]{1,0:T(8,128)(2,1)S(1)}, u32[]{:S(2)}, u32[]{:S(2)}) collective-permute-start(bf16[1024,256]{1,0:T(8,128)(2,1)S(1)} %get-tuple-element.976.a0.act_ref), channel_id=1, source_target_pairs={{0,8},{8,0},{16,24},{24,16},{1,9},{9,1},{17,25},{25,17},{2,10},{10... | collective-permute-start | bytes 1572872 | tf_op jit(solution)/shard_map/ppermute | solution.py:840
  95.3 13.9 %collective-permute-start.35 = (bf16[1024,256]{1,0:T(8,128)(2,1)S(1)}, bf16[1024,256]{1,0:T(8,128)(2,1)S(1)}, u32[]{:S(2)}, u32[]{:S(2)}) collective-permute-start(bf16[1024,256]{1,0:T(8,128)(2,1)S(1)} %get-tuple-element.976.a0.act_ref), channel_id=1, source_target_pairs={{0,16},{8,24},{16,0},{24,8},{1,17},{9,25},{17,1},{25,9},{2,18},{10... | collective-permute-start | bytes 1572872 | tf_op jit(solution)/shard_map/ppermute | solution.py:844
  96.5 6.3 %collective-permute-start.31 = (bf16[704,128]{1,0:T(8,128)(2,1)S(1)}, bf16[704,128]{1,0:T(8,128)(2,1)S(1)}, u32[]{:S(2)}, u32[]{:S(2)}) collective-permute-start(bf16[704,128]{1,0:T(8,128)(2,1)S(1)} %collective-permute-done.26.refs_3_), channel_id=1, source_target_pairs={{0,1},{1,0},{2,3},{3,2},{4,5},{5,4},{6,7},{7,6},{8,9},{9,8},{10,11... | collective-permute-start | bytes 540680 | tf_op jit(solution)/shard_map/ppermute | solution.py:872
  97.3 5.5 %collective-permute-start.33 = (bf16[256,1024]{1,0:T(8,128)(2,1)S(1)}, bf16[256,1024]{1,0:T(8,128)(2,1)S(1)}, u32[]{:S(2)}, u32[]{:S(2)}) collective-permute-start(bf16[256,1024]{1,0:T(8,128)(2,1)S(1)} %collective-permute-done.30.wo2.w2), channel_id=1, source_target_pairs={{0,8},{8,0},{16,24},{24,16},{1,9},{9,1},{17,25},{25,17},{2,10},{10... | collective-permute-start | bytes 1572872 | tf_op jit(solution)/shard_map/ppermute | solution.py:840
  139.4 15.1 %collective-permute-start.38 = (bf16[256,1024]{1,0:T(8,128)(2,1)}, bf16[256,1024]{1,0:T(8,128)(2,1)}, u32[]{:S(2)}, u32[]{:S(2)}) collective-permute-start(bf16[256,1024]{1,0:T(8,128)(2,1)} %get-tuple-element.805), channel_id=1, source_target_pairs={{0,16},{8,24},{16,0},{24,8},{1,17},{9,25},{17,1},{25,9},{2,18},{10... | collective-permute-start | bytes 1572872 | tf_op jit(solution)/shard_map/ppermute | solution.py:844
  154.4 6.1 %collective-permute-start.39 = (bf16[512,1024]{1,0:T(8,128)(2,1)}, bf16[512,1024]{1,0:T(8,128)(2,1)S(1)}, u32[]{:S(2)}, u32[]{:S(2)}) collective-permute-start(bf16[512,1024]{1,0:T(8,128)(2,1)} %get-tuple-element.835), channel_id=1, source_target_pairs={{0,8},{8,0},{16,24},{24,16},{1,9},{9,1},{17,25},{25,17},{2,10},{10... | collective-permute-start | bytes 3145736 | tf_op jit(solution)/shard_map/ppermute | solution.py:840
  154.5 10.8 %collective-permute-start.40 = (bf16[1408,128]{1,0:T(8,128)(2,1)S(1)}, bf16[1408,128]{1,0:T(8,128)(2,1)S(1)}, u32[]{:S(2)}, u32[]{:S(2)}) collective-permute-start(bf16[1408,128]{1,0:T(8,128)(2,1)S(1)} %copy-done.94), channel_id=1, source_target_pairs={{0,1},{1,0},{2,3},{3,2},{4,5},{5,4},{6,7},{7,6},{8,9},{9,8},{10,11... | collective-permute-start | bytes 1081352 | tf_op jit(solution)/shard_map/ppermute | solution.py:872
  165.3 10.0 %collective-permute-start.41 = (bf16[1408,128]{1,0:T(8,128)(2,1)S(1)}, bf16[1408,128]{1,0:T(8,128)(2,1)S(1)}, u32[]{:S(2)}, u32[]{:S(2)}) collective-permute-start(bf16[1408,128]{1,0:T(8,128)(2,1)S(1)} %copy-done.93), channel_id=1, source_target_pairs={{0,1},{1,0},{2,3},{3,2},{4,5},{5,4},{6,7},{7,6},{8,9},{9,8},{10,11... | collective-permute-start | bytes 1081352 | tf_op jit(solution)/shard_map/ppermute | solution.py:872
  166.2 11.5 %collective-permute-start.45 = (bf16[1408,128]{1,0:T(8,128)(2,1)S(1)}, bf16[1408,128]{1,0:T(8,128)(2,1)S(1)}, u32[]{:S(2)}, u32[]{:S(2)}) collective-permute-start(bf16[1408,128]{1,0:T(8,128)(2,1)S(1)} %total.4), channel_id=1, source_target_pairs={{0,2},{1,3},{2,4},{3,5},{4,6},{5,7},{6,0},{7,1},{8,10},{9,11},{10,... | collective-permute-start | bytes 1081352 | tf_op jit(solution)/shard_map/ppermute | solution.py:877
  166.5 6.3 %collective-permute-start.43 = (bf16[256,256]{1,0:T(8,128)(2,1)S(1)}, bf16[256,256]{1,0:T(8,128)(2,1)S(1)}, u32[]{:S(2)}, u32[]{:S(2)}) collective-permute-start(bf16[256,256]{1,0:T(8,128)(2,1)S(1)} %get-tuple-element.884), channel_id=1, source_target_pairs={{0,16},{8,24},{16,0},{24,8},{1,17},{9,25},{17,1},{25,9},{2,18},{10... | collective-permute-start | bytes 393224 | tf_op jit(solution)/shard_map/ppermute | solution.py:844
  167.3 7.6 %collective-permute-start.44 = (bf16[256,256]{1,0:T(8,128)(2,1)S(1)}, bf16[256,256]{1,0:T(8,128)(2,1)S(1)}, u32[]{:S(2)}, u32[]{:S(2)}) collective-permute-start(bf16[256,256]{1,0:T(8,128)(2,1)S(1)} %get-tuple-element.885), channel_id=1, source_target_pairs={{0,24},{8,16},{16,8},{24,0},{1,25},{9,17},{17,9},{25,1},{2,26},{10... | collective-permute-start | bytes 393224 | tf_op jit(solution)/shard_map/ppermute | solution.py:848
  177.7 15.1 %collective-permute-start.47 = (bf16[256,1024]{1,0:T(8,128)(2,1)}, bf16[256,1024]{1,0:T(8,128)(2,1)S(1)}, u32[]{:S(2)}, u32[]{:S(2)}) collective-permute-start(bf16[256,1024]{1,0:T(8,128)(2,1)} %get-tuple-element.977.d0), channel_id=1, source_target_pairs={{0,8},{8,0},{16,24},{24,16},{1,9},{9,1},{17,25},{25,17},{2,10},{10... | collective-permute-start | bytes 1572872 | tf_op jit(solution)/shard_map/ppermute | solution.py:840
  177.7 15.9 %collective-permute-start.48 = (bf16[256,1024]{1,0:T(8,128)(2,1)}, bf16[256,1024]{1,0:T(8,128)(2,1)}, u32[]{:S(2)}, u32[]{:S(2)}) collective-permute-start(bf16[256,1024]{1,0:T(8,128)(2,1)} %get-tuple-element.977.d0), channel_id=1, source_target_pairs={{0,16},{8,24},{16,0},{24,8},{1,17},{9,25},{17,1},{25,9},{2,18},{10... | collective-permute-start | bytes 1572872 | tf_op jit(solution)/shard_map/ppermute | solution.py:844
  178.5 12.8 %collective-permute-start.46 = (bf16[1408,128]{1,0:T(8,128)(2,1)S(1)}, bf16[1408,128]{1,0:T(8,128)(2,1)S(1)}, u32[]{:S(2)}, u32[]{:S(2)}) collective-permute-start(bf16[1408,128]{1,0:T(8,128)(2,1)S(1)} %copy-done.92), channel_id=1, source_target_pairs={{0,1},{1,0},{2,3},{3,2},{4,5},{5,4},{6,7},{7,6},{8,9},{9,8},{10,11... | collective-permute-start | bytes 1081352 | tf_op jit(solution)/shard_map/ppermute | solution.py:872
  179.9 12.9 %collective-permute-start.49 = (bf16[1408,128]{1,0:T(8,128)(2,1)S(1)}, bf16[1408,128]{1,0:T(8,128)(2,1)S(1)}, u32[]{:S(2)}, u32[]{:S(2)}) collective-permute-start(bf16[1408,128]{1,0:T(8,128)(2,1)S(1)} %total.5), channel_id=1, source_target_pairs={{0,2},{1,3},{2,4},{3,5},{4,6},{5,7},{6,0},{7,1},{8,10},{9,11},{10,... | collective-permute-start | bytes 1081352 | tf_op jit(solution)/shard_map/ppermute | solution.py:877
  193.7 20.9 %collective-permute-start.53 = (bf16[2944,128]{1,0:T(8,128)(2,1)}, bf16[2944,128]{1,0:T(8,128)(2,1)S(1)}, u32[]{:S(2)}, u32[]{:S(2)}) collective-permute-start(bf16[2944,128]{1,0:T(8,128)(2,1)} %get-tuple-element.948), channel_id=1, source_target_pairs={{0,1},{1,0},{2,3},{3,2},{4,5},{5,4},{6,7},{7,6},{8,9},{9,8},{10,11... | collective-permute-start | bytes 2261000 | tf_op jit(solution)/shard_map/ppermute | solution.py:872
  194.0 20.6 %collective-permute-start.50 = (bf16[256,1024]{1,0:T(8,128)(2,1)}, bf16[256,1024]{1,0:T(8,128)(2,1)}, u32[]{:S(2)}, u32[]{:S(2)}) collective-permute-start(bf16[256,1024]{1,0:T(8,128)(2,1)} %collective-permute-done.48.d2), channel_id=1, source_target_pairs={{0,8},{8,0},{16,24},{24,16},{1,9},{9,1},{17,25},{25,17},{2,10},{10... | collective-permute-start | bytes 1572872 | tf_op jit(solution)/shard_map/ppermute | solution.py:840
  194.0 20.6 %collective-permute-start.51 = (bf16[256,1024]{1,0:T(8,128)(2,1)}, bf16[256,1024]{1,0:T(8,128)(2,1)}, u32[]{:S(2)}, u32[]{:S(2)}) collective-permute-start(bf16[256,1024]{1,0:T(8,128)(2,1)} %get-tuple-element.937), channel_id=1, source_target_pairs={{0,16},{8,24},{16,0},{24,8},{1,17},{9,25},{17,1},{25,9},{2,18},{10... | collective-permute-start | bytes 1572872 | tf_op jit(solution)/shard_map/ppermute | solution.py:844
  196.1 18.5 %collective-permute-start.52 = (bf16[1408,128]{1,0:T(8,128)(2,1)}, bf16[1408,128]{1,0:T(8,128)(2,1)}, u32[]{:S(2)}, u32[]{:S(2)}) collective-permute-start(bf16[1408,128]{1,0:T(8,128)(2,1)} %total.6), channel_id=1, source_target_pairs={{0,2},{1,3},{2,4},{3,5},{4,6},{5,7},{6,0},{7,1},{8,10},{9,11},{10,... | collective-permute-start | bytes 1081352 | tf_op jit(solution)/shard_map/ppermute | solution.py:877
  197.1 15.6 %collective-permute-start.54 = (bf16[512,128]{1,0:T(8,128)(2,1)S(1)}, bf16[512,128]{1,0:T(8,128)(2,1)S(1)}, u32[]{:S(2)}, u32[]{:S(2)}) collective-permute-start(bf16[512,128]{1,0:T(8,128)(2,1)S(1)} %constant_dynamic-slice_fusion.4), channel_id=1, source_target_pairs={{0,16},{8,24},{16,0},{24,8},{1,17},{9,25},{17,1},{25,9},{2,18},{10... | collective-permute-start | bytes 393224 | tf_op jit(solution)/shard_map/ppermute | solution.py:844
  214.6 8.1 %collective-permute-start.59 = (bf16[512,1024]{1,0:T(8,128)(2,1)S(1)}, bf16[512,1024]{1,0:T(8,128)(2,1)S(1)}, u32[]{:S(2)}, u32[]{:S(2)}) collective-permute-start(bf16[512,1024]{1,0:T(8,128)(2,1)S(1)} %get-tuple-element.973), channel_id=1, source_target_pairs={{0,8},{8,0},{16,24},{24,16},{1,9},{9,1},{17,25},{25,17},{2,10},{10... | collective-permute-start | bytes 3145736 | tf_op jit(solution)/shard_map/ppermute | solution.py:840
  214.7 13.7 %collective-permute-start.58 = (bf16[1536,128]{1,0:T(8,128)(2,1)S(1)}, bf16[1536,128]{1,0:T(8,128)(2,1)S(1)}, u32[]{:S(2)}, u32[]{:S(2)}) collective-permute-start(bf16[1536,128]{1,0:T(8,128)(2,1)S(1)} %copy-done.91), channel_id=1, source_target_pairs={{0,1},{1,0},{2,3},{3,2},{4,5},{5,4},{6,7},{7,6},{8,9},{9,8},{10,11... | collective-permute-start | bytes 1179656 | tf_op jit(solution)/shard_map/ppermute | solution.py:872
  216.4 7.6 %collective-permute-start.55 = (bf16[384,128]{1,0:T(8,128)(2,1)S(1)}, bf16[384,128]{1,0:T(8,128)(2,1)S(1)}, u32[]{:S(2)}, u32[]{:S(2)}) collective-permute-start(bf16[384,128]{1,0:T(8,128)(2,1)S(1)} %get-tuple-element.966), channel_id=1, source_target_pairs={{0,2},{1,3},{2,4},{3,5},{4,6},{5,7},{6,0},{7,1},{8,10},{9,11},{10,... | collective-permute-start | bytes 294920 | tf_op jit(solution)/shard_map/ppermute | solution.py:877
  216.4 10.8 %collective-permute-start.56 = (bf16[384,128]{1,0:T(8,128)(2,1)S(1)}, bf16[384,128]{1,0:T(8,128)(2,1)S(1)}, u32[]{:S(2)}, u32[]{:S(2)}) collective-permute-start(bf16[384,128]{1,0:T(8,128)(2,1)S(1)} %get-tuple-element.967), channel_id=1, source_target_pairs={{0,4},{1,5},{2,6},{3,7},{4,0},{5,1},{6,2},{7,3},{8,12},{9,13},{10,... | collective-permute-start | bytes 294920 | tf_op jit(solution)/shard_map/ppermute | solution.py:877
  219.2 8.1 %collective-permute-start.57 = (bf16[384,128]{1,0:T(8,128)(2,1)S(1)}, bf16[384,128]{1,0:T(8,128)(2,1)S(1)}, u32[]{:S(2)}, u32[]{:S(2)}) collective-permute-start(bf16[384,128]{1,0:T(8,128)(2,1)S(1)} %get-tuple-element.968), channel_id=1, source_target_pairs={{0,6},{1,7},{2,0},{3,1},{4,2},{5,3},{6,4},{7,5},{8,14},{9,15},{10,... | collective-permute-start | bytes 294920 | tf_op jit(solution)/shard_map/ppermute | solution.py:877
  228.4 15.1 %collective-permute-start.63 = (bf16[256,1024]{1,0:T(8,128)(2,1)S(1)}, bf16[256,1024]{1,0:T(8,128)(2,1)S(1)}, u32[]{:S(2)}, u32[]{:S(2)}) collective-permute-start(bf16[256,1024]{1,0:T(8,128)(2,1)S(1)} %get-tuple-element.1003), channel_id=1, source_target_pairs={{0,16},{8,24},{16,0},{24,8},{1,17},{9,25},{17,1},{25,9},{2,18},{10... | collective-permute-start | bytes 1572872 | tf_op jit(solution)/shard_map/ppermute | solution.py:844
  229.8 13.7 %collective-permute-start.64 = (bf16[1024,128]{1,0:T(8,128)(2,1)S(1)}, bf16[1024,128]{1,0:T(8,128)(2,1)S(1)}, u32[]{:S(2)}, u32[]{:S(2)}) collective-permute-start(bf16[1024,128]{1,0:T(8,128)(2,1)S(1)} %get-tuple-element.1005), channel_id=1, source_target_pairs={{0,1},{1,0},{2,3},{3,2},{4,5},{5,4},{6,7},{7,6},{8,9},{9,8},{10,11... | collective-permute-start | bytes 786440 | tf_op jit(solution)/shard_map/ppermute | solution.py:872
  231.3 7.6 %collective-permute-start.60 = (bf16[384,128]{1,0:T(8,128)(2,1)S(1)}, bf16[384,128]{1,0:T(8,128)(2,1)S(1)}, u32[]{:S(2)}, u32[]{:S(2)}) collective-permute-start(bf16[384,128]{1,0:T(8,128)(2,1)S(1)} %get-tuple-element.997), channel_id=1, source_target_pairs={{0,2},{1,3},{2,4},{3,5},{4,6},{5,7},{6,0},{7,1},{8,10},{9,11},{10,... | collective-permute-start | bytes 294920 | tf_op jit(solution)/shard_map/ppermute | solution.py:877
  231.4 12.1 %collective-permute-start.61 = (bf16[384,128]{1,0:T(8,128)(2,1)S(1)}, bf16[384,128]{1,0:T(8,128)(2,1)S(1)}, u32[]{:S(2)}, u32[]{:S(2)}) collective-permute-start(bf16[384,128]{1,0:T(8,128)(2,1)S(1)} %get-tuple-element.998), channel_id=1, source_target_pairs={{0,4},{1,5},{2,6},{3,7},{4,0},{5,1},{6,2},{7,3},{8,12},{9,13},{10,... | collective-permute-start | bytes 294920 | tf_op jit(solution)/shard_map/ppermute | solution.py:877
  233.8 9.7 %collective-permute-start.62 = (bf16[384,128]{1,0:T(8,128)(2,1)S(1)}, bf16[384,128]{1,0:T(8,128)(2,1)S(1)}, u32[]{:S(2)}, u32[]{:S(2)}) collective-permute-start(bf16[384,128]{1,0:T(8,128)(2,1)S(1)} %get-tuple-element.999), channel_id=1, source_target_pairs={{0,6},{1,7},{2,0},{3,1},{4,2},{5,3},{6,4},{7,5},{8,14},{9,15},{10,... | collective-permute-start | bytes 294920 | tf_op jit(solution)/shard_map/ppermute | solution.py:877
  245.6 11.0 %collective-permute-start.68 = (bf16[1600,128]{1,0:T(8,128)(2,1)}, bf16[1600,128]{1,0:T(8,128)(2,1)S(1)}, u32[]{:S(2)}, u32[]{:S(2)}) collective-permute-start(bf16[1600,128]{1,0:T(8,128)(2,1)} %get-tuple-element.1035), channel_id=1, source_target_pairs={{0,16},{8,24},{16,0},{24,8},{1,17},{9,25},{17,1},{25,9},{2,18},{10... | collective-permute-start | bytes 1228808 | tf_op jit(solution)/shard_map/ppermute | solution.py:844
  247.6 7.7 %collective-permute-start.65 = (bf16[256,128]{1,0:T(8,128)(2,1)}, bf16[256,128]{1,0:T(8,128)(2,1)S(1)}, u32[]{:S(2)}, u32[]{:S(2)}) collective-permute-start(bf16[256,128]{1,0:T(8,128)(2,1)} %get-tuple-element.1018), channel_id=1, source_target_pairs={{0,2},{1,3},{2,4},{3,5},{4,6},{5,7},{6,0},{7,1},{8,10},{9,11},{10,... | collective-permute-start | bytes 196616 | tf_op jit(solution)/shard_map/ppermute | solution.py:877
  249.8 5.9 %collective-permute-start.66 = (bf16[256,128]{1,0:T(8,128)(2,1)}, bf16[256,128]{1,0:T(8,128)(2,1)}, u32[]{:S(2)}, u32[]{:S(2)}) collective-permute-start(bf16[256,128]{1,0:T(8,128)(2,1)} %get-tuple-element.1019), channel_id=1, source_target_pairs={{0,4},{1,5},{2,6},{3,7},{4,0},{5,1},{6,2},{7,3},{8,12},{9,13},{10,... | collective-permute-start | bytes 196616 | tf_op jit(solution)/shard_map/ppermute | solution.py:877
  252.0 4.6 %collective-permute-start.67 = (bf16[256,128]{1,0:T(8,128)(2,1)}, bf16[256,128]{1,0:T(8,128)(2,1)}, u32[]{:S(2)}, u32[]{:S(2)}) collective-permute-start(bf16[256,128]{1,0:T(8,128)(2,1)} %get-tuple-element.1020), channel_id=1, source_target_pairs={{0,6},{1,7},{2,0},{3,1},{4,2},{5,3},{6,4},{7,5},{8,14},{9,15},{10,... | collective-permute-start | bytes 196616 | tf_op jit(solution)/shard_map/ppermute | solution.py:877
  (103 other events, 814.4 us)
Sparse Core Ops, SparseCore 0:
  43.7 59.9 all-gather.2
  180.3 70.6 reduce-scatter.1
where the time goes:
time: 270 us; the launch traced here: 269 us
  Pallas kernels  98.1 us (36%)
  waiting for transfers between devices  73 us (27%)
  starting transfers between devices  55.9 us (21%)
  local copies, waits for them, and re-layouts  18.9 us (7%)
  between operations  15.3 us (6%)
  other arithmetic  8.06 us (3%)
    ppermute x16, waiting for transfers between devices, to_chip(): return lax.ppermute(value, 'seq', [(i, i ^ 2) for i in range(SEQ)])  29.1 us
    ppermute x18, waiting for transfers between devices, to_z(): lax.ppermute(value, 'dp', [(i, (i + 2 * hops) % dp) for i in range(dp)])  22.3 us
    pallas_call x2, Pallas kernels, attend_back_call(): pl.pallas_call(functools.partial(attend_back_kernel, dp, pieces), name='a...  21.9 us
    pallas_call x1, Pallas kernels, ffn_call(): pl.pallas_call(ffn_kernel, name='ffn', grid_spec=pltpu.PrefetchScalarGrid...  21.1 us
    ppermute x18, starting transfers between devices, to_z(): lax.ppermute(value, 'dp', [(i, (i + 2 * hops) % dp) for i in range(dp)])  19.7 us
    ppermute x16, starting transfers between devices, to_chip(): return lax.ppermute(value, 'seq', [(i, i ^ 2) for i in range(SEQ)])  16.8 us
    unnamed x202, local copies, waits for them, and re-layouts  15.8 us
    pallas_call x15, Pallas kernels, simple(): pl.pallas_call(kernel, name=name, grid=(1,), in_specs=[SMEM if x.dtype ==...  15.3 us
  transfers between devices with their start and end apart: 72, of which 30 were waited for; matrix products, arithmetic and copies ran while one was open for 4% of the time, Pallas kernels for 26%

commit v1 on v0

--- a/solution.py
+++ b/solution.py
@@ -258,9 +258,10 @@
 
 
 def pack_attn_kernel(
-    place_ref, q_ref, k_ref, v_ref, o_ref, d_ref, ag_ref, mg_ref, tok_ref, c0, c1, c2, c3, orows_ref, drows_ref, *halves_refs
+    q_ref, k_ref, v_ref, o_ref, d_ref, ag_ref, mg_ref, tok_ref, c0, c1, c2, c3, orows_ref, drows_ref, *halves_refs
 ):
-    me, owner = place_ref[0], place_ref[1]
+    me = lax.axis_index("seq")
+    owner = me * lax.axis_size("dp") + lax.axis_index("dp")
     w_rows, width = q_ref.shape
     part = width // SEQ
     lane = lax.broadcasted_iota(jnp.int32, (1, 128), 1)
@@ -288,7 +289,7 @@
         out[...] = tok_ref[i * rows : (i + 1) * rows, :]
 
 
-def pack_attn(place, wq, wk, wv, wo, wd, attn_gain, mlp_gain, tok):
+def pack_attn(wq, wk, wv, wo, wd, attn_gain, mlp_gain, tok):
     w_rows, width = wq.shape
     tiles = width // 128
     shapes = [(3 * tiles // SEQ * w_rows + 16, 128)] * 4 + [(tiles * w_rows, 128), (tiles * wd.shape[0], 128)]
@@ -297,11 +298,11 @@
         pack_attn_kernel,
         name="pack_attn",
         grid=(1,),
-        in_specs=[SMEM] + [fixed(w.shape) for w in (wq, wk, wv, wo, wd)] + [fixed((1, w_rows))] * 2 + [fixed(tok.shape)],
+        in_specs=[fixed(w.shape) for w in (wq, wk, wv, wo, wd)] + [fixed((1, w_rows))] * 2 + [fixed(tok.shape)],
         out_specs=[fixed(x) for x in shapes],
         out_shape=[jax.ShapeDtypeStruct(x, bf16) for x in shapes],
         compiler_params=params(60),
-    )(place, wq, wk, wv, wo, wd, attn_gain[None], mlp_gain[None], tok)
+    )(wq, wk, wv, wo, wd, attn_gain[None], mlp_gain[None], tok)
 
 
 def pack_ffn_kernel(place_ref, g_ref, u_ref, c0, c1, c2, c3):
@@ -911,7 +912,7 @@
 
     half = rows // 2
     *s.cols, s.orows, drows, tok_a, tok_b = pack_attn(
-        place, query_weight, key_weight, value_weight, out_weight, down_weight, attn_gain, mlp_gain, tokens[0]
+        query_weight, key_weight, value_weight, out_weight, down_weight, attn_gain, mlp_gain, tokens[0]
     )
     s.r, s.tok_far = [drows], [tok_a, tok_b]
     s.tokens, s.first, s.out_grad, s.segments = tokens[0], first_values[0], out_grad[0], segment_ids
@@ -967,15 +968,14 @@
     del s.w_out
     s.fence()
     att_far = to_chip(s.attended)
-    s.ry.append(to_y(s.r[3]))
+    s.w_down = assemble_rows(place, s.r + s.ry + [to_y(s.r[3])], width, inner)
     s.att = [s.attended, to_core(s.attended), att_far]
     s.wo.append(to_core(s.wo[2]))
     og_far = jnp.concatenate(s.og_far)
     s.og = jnp.concatenate([*s.og, og_far, to_core(og_far)])
+    del s.r, s.ry, s.og_far
     s.fence()
     s.att.append(to_core(s.att[2]))
-    s.w_down = assemble_rows(place, s.r + s.ry, width, inner)
-    del s.r, s.ry, s.og_far
     s.fence()
     s.nm, s.hidden, s.d_gu, s.mid, s.dnm, dnm_sent, s.lo, s.lo_sent = ffn_call(
         me_arg, s.tok, s.og, s.att, s.wo, s.mlp_gain, ffn_all, s.w_down
@@ -1043,14 +1043,14 @@
     del s.d_branch, s.attended, s.dnin_sent
     s.fence()
     s.kept[1] = over_z(*slots(s.kept[1], s.sent[1]))
-    s.out_sent = to_y(s.out_sent)
+    s.out_kept = slots(s.out_kept, to_y(s.out_sent))
     s.dnin_far = to_chip(s.dnin_far)
     s.layer_out = total(s.mid, s.lo, s.lo_far)
     del s.lo, s.lo_far, s.mid
     s.fence()
     s.mine, s.near, far = cut(me_arg, s.kept, (s.f_kept[0], s.sent[0], s.f), s.d_qkv[1])
     s.far = to_chip(far)
-    s.out_kept = over_z(*slots(s.out_kept, s.out_sent))
+    s.out_kept = over_z(*s.out_kept)
     s.token_grad = simple(
         token_grad_kernel,
         "token_grad",

time: 270 us -> 269 us (level)
  transfers between devices with their start and end apart: 72 -> 72, of which waited for: 30 -> 32; matrix products, arithmetic and copies ran while one was open for 4% -> 4% of each run, Pallas kernels for 26% -> 26%
where the time goes in v1:
time: 269 us; the launch traced here: 268 us
  Pallas kernels  98.1 us (36%)
  waiting for transfers between devices  71.3 us (27%)
  starting transfers between devices  56.5 us (21%)
  local copies, waits for them, and re-layouts  18.8 us (7%)
  between operations  15.3 us (6%)
  other arithmetic  7.62 us (3%)
    ppermute x16, waiting for transfers between devices, to_chip(): return lax.ppermute(value, 'seq', [(i, i ^ 2) for i in range(SEQ)])  26.9 us
    pallas_call x2, Pallas kernels, attend_back_call(): pl.pallas_call(functools.partial(attend_back_kernel, dp, pieces), name='a...  21.9 us
    pallas_call x1, Pallas kernels, ffn_call(): pl.pallas_call(ffn_kernel, name='ffn', grid_spec=pltpu.PrefetchScalarGrid...  21.1 us
    ppermute x18, starting transfers between devices, to_z(): lax.ppermute(value, 'dp', [(i, (i + 2 * hops) % dp) for i in range(dp)])  21.1 us
    ppermute x18, waiting for transfers between devices, to_z(): lax.ppermute(value, 'dp', [(i, (i + 2 * hops) % dp) for i in range(dp)])  20.1 us
    ppermute x16, starting transfers between devices, to_chip(): return lax.ppermute(value, 'seq', [(i, i ^ 2) for i in range(SEQ)])  16.7 us
    unnamed x202, local copies, waits for them, and re-layouts  15.8 us
    pallas_call x15, Pallas kernels, simple(): pl.pallas_call(kernel, name=name, grid=(1,), in_specs=[SMEM if x.dtype ==...  15.3 us
  transfers between devices with their start and end apart: 72, of which 32 were waited for; matrix products, arithmetic and copies ran while one was open for 4% of the time, Pallas kernels for 26%

profile of v1, /device:TPU:0, one launch (start us, length us, event | category | flops | bytes accessed | tf_op | source)
XLA Modules:
  0.0 267.7 jit_solution(15569146194513593088)
XLA Ops:
  7.2 2.3 pack_attn.1
  9.5 3.1 %collective-permute-start.3 = (bf16[704,128]{1,0:T(8,128)(2,1)}, bf16[704,128]{1,0:T(8,128)(2,1)S(1)}, u32[]{:S(2)}, u32[]{:S(2)}) collective-permute-start(bf16[704,128]{1,0:T(8,128)(2,1)} %get-tuple-element.704.refs_0_), channel_id=1, source_target_pairs={{0,2},{1,3},{2,4},{3,5},{4,6},{5,7},{6,0},{7,1},{8,10},{9,11},{10,... | collective-permute-start | bytes 540680 | tf_op jit(solution)/shard_map/ppermute | solution.py:878
  12.6 1.5 collective-permute-start.4
  14.1 1.5 collective-permute-start.1
  16.0 2.6 collective-permute-done.1
  21.4 1.6 collective-permute-start.6
  24.3 1.5 collective-permute-start.5
  25.8 3.0 %fusion = (f32[1024,32]{1,0:T(8,128)S(1)}, f32[1024,32]{1,0:T(8,128)}, f32[1024,32]{1,0:T(8,128)}) fusion(f32[32]{0:T(128)S(1)} %multiply_exponential_fusion, f32[1024]{0:T(1024)S(1)} %iota_convert_fusion), kind=kLoop, calls=%fused_computation.8 | loop fusion | flops 65536 | bytes 397440 | tf_op jit(solution)/shard_map/neg | solution.py:886
  28.9 2.3 pack_ffn.1
  33.2 1.6 collective-permute-start.8
  34.7 1.3 collective-permute-start.9
  36.1 1.3 collective-permute-start.11
  38.0 3.1 %pad_maximum_fusion = (f32[1024,128]{1,0:T(8,128)S(1)}, f32[1024,128]{1,0:T(8,128)S(1)}) fusion(f32[1024,32]{1,0:T(8,128)} %get-tuple-element.1058, f32[1024,32]{1,0:T(8,128)} %get-tuple-element.1057, f32[1024,32]{1,0:T(8,128)S(1)} %get-tuple-element.1056), kind=kLoop, calls=%fused_computation.2 | loop fusion | flops 786432 | bytes 1441792 | tf_op jit(solution)/shard_map/concatenate | solution.py:886
  41.2 1.5 collective-permute-done.11
  47.0 6.3 %collective-permute-done.13 = bf16[128,1024]{1,0:T(8,128)(2,1)S(1)} collective-permute-done((bf16[128,1024]{1,0:T(8,128)(2,1)}, bf16[128,1024]{1,0:T(8,128)(2,1)S(1)}, u32[]{:S(2)}, u32[]{:S(2)}) %collective-permute-start.13) | collective-permute-done | bytes 262176 | tf_op jit(solution)/shard_map/ppermute | solution.py:845
  53.3 1.4 collective-permute-done.14.refs_3_
  59.0 1.5 collective-permute-done.19
  60.4 2.1 collective-permute-done.18
  62.7 2.5 collective-permute-done.20.refs_7_
  65.9 1.2 collective-permute-start.23
  68.3 3.3 %qkv.1 = (bf16[1024,1024]{1,0:T(8,128)(2,1)S(1)}, bf16[1024,256]{1,0:T(8,128)(2,1)S(1)}, bf16[1024,256]{1,0:T(8,128)(2,1)S(1)}, bf16[1024,256]{1,0:T(8,128)(2,1)S(1)}) custom-call(s32[1]{0:T(128)} %bitcast.5.me_ref, bf16[1024,1024]{1,0:T(8,128)(2,1)S(1)} %constant_dynamic-update-slice_fusion.5.tok_ref, bf16[1024,256]{1,0:T(8,128)(2,1)S(1)} %pad_maximum_fusion.2.first_ref, ...), custom_call_target="tpu_custom_call" | custom-call | tf_op jit(solution)/shard_map/qkv/pallas_call | solution.py:76
  71.7 1.4 copy-done.5
  73.1 1.5 collective-permute-done.22.refs_2_
  74.6 1.3 collective-permute-start.30
  77.8 9.0 %attend.1 = (bf16[1024,256]{1,0:T(8,128)(2,1)S(1)}, f32[2,2,1024]{2,1,0:T(2,128)S(1)}) custom-call(bf16[1024,256]{1,0:T(8,128)(2,1)S(1)} %get-tuple-element.911.q_ref, bf16[1024,256]{1,0:T(8,128)(2,1)S(1)} %get-tuple-element.912.k_ref, bf16[1024,256]{1,0:T(8,128)(2,1)S(1)} %get-tuple-element.913.v_ref, s32[1,1024]{1,0:T(1,128)S(1)} %copy-done.72), custom_call_target="tpu_custom_call" | custom-call | tf_op jit(solution)/shard_map/attend/pallas_call | solution.py:152
  87.4 2.0 collective-permute-done.26.refs_3_
  89.4 5.2 %collective-permute-done.28 = bf16[128,1024]{1,0:T(8,128)(2,1)S(1)} collective-permute-done((bf16[128,1024]{1,0:T(8,128)(2,1)S(1)}, bf16[128,1024]{1,0:T(8,128)(2,1)S(1)}, u32[]{:S(2)}, u32[]{:S(2)}) %collective-permute-start.28) | collective-permute-done | bytes 262176 | tf_op jit(solution)/shard_map/ppermute | solution.py:845
  95.2 1.3 collective-permute-start.35
  97.6 6.0 %collective-permute-done.33.refs_7_ = bf16[704,128]{1,0:T(8,128)(2,1)S(1)} collective-permute-done((bf16[704,128]{1,0:T(8,128)(2,1)S(1)}, bf16[704,128]{1,0:T(8,128)(2,1)S(1)}, u32[]{:S(2)}, u32[]{:S(2)}) %collective-permute-start.33) | collective-permute-done | bytes 180256 | tf_op jit(solution)/shard_map/ppermute | solution.py:873
  105.7 3.5 %collective-permute-done.35.a2 = bf16[1024,256]{1,0:T(8,128)(2,1)S(1)} collective-permute-done((bf16[1024,256]{1,0:T(8,128)(2,1)S(1)}, bf16[1024,256]{1,0:T(8,128)(2,1)S(1)}, u32[]{:S(2)}, u32[]{:S(2)}) %collective-permute-start.35) | collective-permute-done | bytes 524320 | tf_op jit(solution)/shard_map/ppermute | solution.py:845
  109.2 1.9 collective-permute-done.36.a3
  111.9 21.1 %ffn.1 = (bf16[1024,1024]{1,0:T(8,128)(2,1)}, bf16[1024,704]{1,0:T(8,128)(2,1)}, bf16[1024,1408]{1,0:T(8,128)(2,1)}, f32[256,1024]{1,0:T(8,128)}, bf16[512,1024]...) custom-call(s32[1]{0:T(128)} %bitcast.5.me_ref, ...), custom_call_target="tpu_custom_call" | custom-call | tf_op jit(solution)/shard_map/ffn/pallas_call | solution.py:479
  133.2 2.7 %collective-permute-done.37.got_ref = bf16[512,1024]{1,0:T(8,128)(2,1)S(1)} collective-permute-done((bf16[512,1024]{1,0:T(8,128)(2,1)}, bf16[512,1024]{1,0:T(8,128)(2,1)S(1)}, u32[]{:S(2)}, u32[]{:S(2)}) %collective-permute-start.37) | collective-permute-done | bytes 1048608 | tf_op jit(solution)/shard_map/ppermute | solution.py:841
  136.0 1.2 copy-done.34
  139.1 1.3 collective-permute-start.38
  140.4 8.1 %columns_grad.1 = (bf16[1408,128]{1,0:T(8,128)(2,1)}, bf16[1408,128]{1,0:T(8,128)(2,1)}, bf16[1408,128]{1,0:T(8,128)(2,1)}, bf16[1408,128]{1,0:T(8,128)(2,1)}, b...) custom-call(s32[3]{0:T(128)} %pad_add_fusion.place_ref, ...), custom_call_target="tpu_custom_call" | custom-call | tf_op jit(solution)/shard_map/columns_grad/pallas_call | solution.py:539
  148.6 5.6 %down_grad.1 = bf16[704,1024]{1,0:T(8,128)(2,1)} custom-call(bf16[1024,704]{1,0:T(8,128)(2,1)} %get-tuple-element.805.act_ref, bf16[1024,1024]{1,0:T(8,128)(2,1)} %copy-done.80), custom_call_target="tpu_custom_call" | custom-call | tf_op jit(solution)/shard_map/down_grad/pallas_call | solution.py:599
  157.4 2.8 %branch.1 = (f32[256,1024]{1,0:T(8,128)S(1)}, bf16[256,1024]{1,0:T(8,128)(2,1)}, bf16[256,256]{1,0:T(8,128)(2,1)S(1)}, bf16[256,256]{1,0:T(8,128)(2,1)S(1)}, bf1...) custom-call(f32[256,1024]{1,0:T(8,128)S(1)} %copy-done.38, bf16[256,1024]{1,0:T(8,128)(2,1)} %collective-permute-done.38.far_ref, ...), custom_call_target="tpu_custom_call" | custom-call | tf_op jit(solution)/shard_map/branch/pallas_call | solution.py:611
  162.2 2.8 %collective-permute-done.40.refs_1_ = bf16[1408,128]{1,0:T(8,128)(2,1)S(1)} collective-permute-done((bf16[1408,128]{1,0:T(8,128)(2,1)S(1)}, bf16[1408,128]{1,0:T(8,128)(2,1)S(1)}, u32[]{:S(2)}, u32[]{:S(2)}) %collective-permute-start.40) | collective-permute-done | bytes 360480 | tf_op jit(solution)/shard_map/ppermute | solution.py:873
  168.1 4.4 %collective-permute-done.43.d2 = bf16[256,256]{1,0:T(8,128)(2,1)S(1)} collective-permute-done((bf16[256,256]{1,0:T(8,128)(2,1)S(1)}, bf16[256,256]{1,0:T(8,128)(2,1)S(1)}, u32[]{:S(2)}, u32[]{:S(2)}) %collective-permute-start.43) | collective-permute-done | bytes 131104 | tf_op jit(solution)/shard_map/ppermute | solution.py:845
  172.6 2.0 collective-permute-done.44.d3
  175.0 2.4 collective-permute-done.45.refs_2_
  180.0 11.0 %attend_back.2 = (bf16[1024,384]{1,0:T(8,128)(2,1)}, bf16[4,384,128]{2,1,0:T(8,128)(2,1)}, bf16[2944,128]{1,0:T(8,128)(2,1)}) custom-call(s32[3]{0:T(128)} %pad_add_fusion.place_ref, bf16[1024,256]{1,0:T(8,128)(2,1)} %copy-done.10, bf16[1024,256]{1,0:T(8,128)(2,1)} %copy-done.11, bf16[1024,256]{1,0:T(8,128)(2,1)} %copy-done.12, bf16[256,256]{1,0:T(8,128)(2,1)} %copy-done.41, ...), custom_call_target="tpu_custom_call" | custom-call | tf_op jit(solution)/shard_map/attend_back/pallas_call | solution.py:236
  191.0 1.6 collective-permute-done.49.refs_2_
  197.7 10.9 %attend_back.3 = (bf16[1024,384]{1,0:T(8,128)(2,1)}, bf16[4,384,128]{2,1,0:T(8,128)(2,1)}, bf16[1536,128]{1,0:T(8,128)(2,1)}) custom-call(s32[3]{0:T(128)} %pad_add_fusion.place_ref, bf16[1024,256]{1,0:T(8,128)(2,1)} %copy-done.10, bf16[1024,256]{1,0:T(8,128)(2,1)} %copy-done.11, bf16[1024,256]{1,0:T(8,128)(2,1)} %copy-done.12, bf16[256,256]{1,0:T(8,128)(2,1)} %copy-done.41, ...), custom_call_target="tpu_custom_call" | custom-call | tf_op jit(solution)/shard_map/attend_back/pallas_call | solution.py:236
  209.7 2.7 %input_grad.1 = (bf16[512,1024]{1,0:T(8,128)(2,1)S(1)}, bf16[512,1024]{1,0:T(8,128)(2,1)S(1)}) custom-call(s32[1]{0:T(128)} %bitcast.5.me_ref, bf16[1024,384]{1,0:T(8,128)(2,1)S(1)} %copy-done.6, bf16[1024,384]{1,0:T(8,128)(2,1)S(1)} %copy-done, bf16[1024,768]{1,0:T(8,128)(2,1)S(1)} %copy-done.8), custom_call_target="tpu_custom_call" | custom-call | tf_op jit(solution)/shard_map/input_grad/pallas_call | solution.py:826
  212.4 1.9 collective-permute-done.52.refs_10_
  214.4 1.6 collective-permute-start.58
  216.2 2.7 %collective-permute-start.56 = (bf16[384,128]{1,0:T(8,128)(2,1)S(1)}, bf16[384,128]{1,0:T(8,128)(2,1)S(1)}, u32[]{:S(2)}, u32[]{:S(2)}) collective-permute-start(bf16[384,128]{1,0:T(8,128)(2,1)S(1)} %get-tuple-element.955), channel_id=1, source_target_pairs={{0,4},{1,5},{2,6},{3,7},{4,0},{5,1},{6,2},{7,3},{8,12},{9,13},{10,... | collective-permute-start | bytes 294920 | tf_op jit(solution)/shard_map/ppermute | solution.py:878
  218.9 1.3 collective-permute-start.57
  220.3 2.2 out_projection_grad.1
  223.7 3.3 %collective-permute-done.56.refs_2_ = bf16[384,128]{1,0:T(8,128)(2,1)S(1)} collective-permute-done((bf16[384,128]{1,0:T(8,128)(2,1)S(1)}, bf16[384,128]{1,0:T(8,128)(2,1)S(1)}, u32[]{:S(2)}, u32[]{:S(2)}) %collective-permute-start.56) | collective-permute-done | bytes 98336 | tf_op jit(solution)/shard_map/ppermute | solution.py:878
  228.1 1.4 collective-permute-start.63
  229.5 1.5 collective-permute-start.64
  231.2 2.2 collective-permute-start.61
  233.4 1.7 collective-permute-start.62
  235.1 2.0 total.7
  238.7 4.8 %collective-permute-done.61.refs_6_ = bf16[384,128]{1,0:T(8,128)(2,1)S(1)} collective-permute-done((bf16[384,128]{1,0:T(8,128)(2,1)S(1)}, bf16[384,128]{1,0:T(8,128)(2,1)S(1)}, u32[]{:S(2)}, u32[]{:S(2)}) %collective-permute-start.61) | collective-permute-done | bytes 98336 | tf_op jit(solution)/shard_map/ppermute | solution.py:878
  243.5 2.1 cut.1
  245.9 3.0 %collective-permute-start.65 = (bf16[256,128]{1,0:T(8,128)(2,1)}, bf16[256,128]{1,0:T(8,128)(2,1)S(1)}, u32[]{:S(2)}, u32[]{:S(2)}) collective-permute-start(bf16[256,128]{1,0:T(8,128)(2,1)} %get-tuple-element.1008), channel_id=1, source_target_pairs={{0,2},{1,3},{2,4},{3,5},{4,6},{5,7},{6,0},{7,1},{8,10},{9,11},{10,... | collective-permute-start | bytes 196616 | tf_op jit(solution)/shard_map/ppermute | solution.py:878
  249.8 1.6 collective-permute-start.67
  251.4 3.1 %token_grad.1 = bf16[256,1024]{1,0:T(8,128)(2,1)} custom-call(f32[256,1024]{1,0:T(8,128)} %copy-done.36, bf16[256,1024]{1,0:T(8,128)(2,1)} %copy-done.89, bf16[256,1024]{1,0:T(8,128)(2,1)} %bitcast.31, f32[1,1024]{1,0:T(1,128)} %bitcast.23, f32[256,1024]{1,0:T(8,128)} %copy-done.35), custom_call_target="tpu_custom_call" | custom-call | tf_op jit(solution)/shard_map/token_grad/pallas_call | solution.py:611
  255.2 1.9 collective-permute-done.69.got_ref
  258.6 2.3 finish.1
  (328 shorter events, 51.6 us)
Async XLA Ops:
  7.2 103.9 %all-gather.3.cloned.1.call-start = ((), (), s32[]{:S(2)}) async-start(), calls=%async_computation.2 | async-start | bytes 3244032 | tf_op jit(solution)/shard_map/all_gather | solution.py:939
  9.5 10.1 %collective-permute-start.3 = (bf16[704,128]{1,0:T(8,128)(2,1)}, bf16[704,128]{1,0:T(8,128)(2,1)S(1)}, u32[]{:S(2)}, u32[]{:S(2)}) collective-permute-start(bf16[704,128]{1,0:T(8,128)(2,1)} %get-tuple-element.704.refs_0_), channel_id=1, source_target_pairs={{0,2},{1,3},{2,4},{3,5},{4,6},{5,7},{6,0},{7,1},{8,10},{9,11},{10,... | collective-permute-start | bytes 540680 | tf_op jit(solution)/shard_map/ppermute | solution.py:878
  12.6 7.0 %collective-permute-start.4 = (bf16[704,128]{1,0:T(8,128)(2,1)}, bf16[704,128]{1,0:T(8,128)(2,1)S(1)}, u32[]{:S(2)}, u32[]{:S(2)}) collective-permute-start(bf16[704,128]{1,0:T(8,128)(2,1)} %get-tuple-element.704.refs_0_), channel_id=1, source_target_pairs={{0,1},{1,0},{2,3},{3,2},{4,5},{5,4},{6,7},{7,6},{8,9},{9,8},{10,11... | collective-permute-start | bytes 540680 | tf_op jit(solution)/shard_map/ppermute | solution.py:873
  21.4 10.9 %collective-permute-start.6 = (bf16[1088,128]{1,0:T(8,128)(2,1)S(1)}, bf16[1088,128]{1,0:T(8,128)(2,1)S(1)}, u32[]{:S(2)}, u32[]{:S(2)}) collective-permute-start(bf16[1088,128]{1,0:T(8,128)(2,1)S(1)} %constant_dynamic-update-slice_fusion.refs_0_), channel_id=1, source_target_pairs={{0,2},{1,3},{2,4},{3,5},{4,6},{5,7},{6,0},{7,1},{8,10},{9,11},{10,... | collective-permute-start | bytes 835592 | tf_op jit(solution)/shard_map/ppermute | solution.py:878
  23.1 9.3 %collective-permute-start.7 = (bf16[1088,128]{1,0:T(8,128)(2,1)S(1)}, bf16[1088,128]{1,0:T(8,128)(2,1)S(1)}, u32[]{:S(2)}, u32[]{:S(2)}) collective-permute-start(bf16[1088,128]{1,0:T(8,128)(2,1)S(1)} %constant_dynamic-update-slice_fusion.refs_0_), channel_id=1, source_target_pairs={{0,1},{1,0},{2,3},{3,2},{4,5},{5,4},{6,7},{7,6},{8,9},{9,8},{10,11... | collective-permute-start | bytes 835592 | tf_op jit(solution)/shard_map/ppermute | solution.py:873
  24.3 8.0 %collective-permute-start.5 = (bf16[128,1024]{1,0:T(8,128)(2,1)}, bf16[128,1024]{1,0:T(8,128)(2,1)S(1)}, u32[]{:S(2)}, u32[]{:S(2)}) collective-permute-start(bf16[128,1024]{1,0:T(8,128)(2,1)} %get-tuple-element.555), channel_id=1, source_target_pairs={{0,16},{8,24},{16,0},{24,8},{1,17},{9,25},{17,1},{25,9},{2,18},{10... | collective-permute-start | bytes 786440 | tf_op jit(solution)/shard_map/ppermute | solution.py:845
  33.2 10.4 %collective-permute-start.8 = (bf16[1088,128]{1,0:T(8,128)(2,1)S(1)}, bf16[1088,128]{1,0:T(8,128)(2,1)S(1)}, u32[]{:S(2)}, u32[]{:S(2)}) collective-permute-start(bf16[1088,128]{1,0:T(8,128)(2,1)S(1)} %collective-permute-done.6.refs_1_), channel_id=1, source_target_pairs={{0,2},{1,3},{2,4},{3,5},{4,6},{5,7},{6,0},{7,1},{8,10},{9,11},{10,... | collective-permute-start | bytes 835592 | tf_op jit(solution)/shard_map/ppermute | solution.py:878
  34.7 8.8 %collective-permute-start.9 = (bf16[1088,128]{1,0:T(8,128)(2,1)S(1)}, bf16[1088,128]{1,0:T(8,128)(2,1)S(1)}, u32[]{:S(2)}, u32[]{:S(2)}) collective-permute-start(bf16[1088,128]{1,0:T(8,128)(2,1)S(1)} %collective-permute-done.6.refs_1_), channel_id=1, source_target_pairs={{0,1},{1,0},{2,3},{3,2},{4,5},{5,4},{6,7},{7,6},{8,9},{9,8},{10,11... | collective-permute-start | bytes 835592 | tf_op jit(solution)/shard_map/ppermute | solution.py:873
  36.1 5.1 %collective-permute-start.12 = (bf16[352,128]{1,0:T(8,128)(2,1)}, bf16[352,128]{1,0:T(8,128)(2,1)S(1)}, u32[]{:S(2)}, u32[]{:S(2)}) collective-permute-start(bf16[352,128]{1,0:T(8,128)(2,1)} %get-tuple-element.588), channel_id=1, source_target_pairs={{0,24},{8,16},{16,8},{24,0},{1,25},{9,17},{17,9},{25,1},{2,26},{10... | collective-permute-start | bytes 270344 | tf_op jit(solution)/shard_map/ppermute | solution.py:849
  36.1 6.7 %collective-permute-start.11 = (bf16[352,128]{1,0:T(8,128)(2,1)}, bf16[352,128]{1,0:T(8,128)(2,1)S(1)}, u32[]{:S(2)}, u32[]{:S(2)}) collective-permute-start(bf16[352,128]{1,0:T(8,128)(2,1)} %get-tuple-element.587), channel_id=1, source_target_pairs={{0,16},{8,24},{16,0},{24,8},{1,17},{9,25},{17,1},{25,9},{2,18},{10... | collective-permute-start | bytes 270344 | tf_op jit(solution)/shard_map/ppermute | solution.py:845
  37.4 5.4 %collective-permute-start.10 = (bf16[352,128]{1,0:T(8,128)(2,1)}, bf16[352,128]{1,0:T(8,128)(2,1)S(1)}, u32[]{:S(2)}, u32[]{:S(2)}) collective-permute-start(bf16[352,128]{1,0:T(8,128)(2,1)} %get-tuple-element.586), channel_id=1, source_target_pairs={{0,8},{8,0},{16,24},{24,16},{1,9},{9,1},{17,25},{25,17},{2,10},{10... | collective-permute-start | bytes 270344 | tf_op jit(solution)/shard_map/ppermute | solution.py:841
  43.6 210.9 %reduce-scatter.2.cloned.1.call-start = ((), (), s32[]{:S(2)}) async-start(), calls=%async_computation.1 | async-start | bytes 1622016 | tf_op jit(solution)/shard_map/reduce_scatter | solution.py:990
  43.6 11.1 %collective-permute-start.16 = (bf16[256,1024]{1,0:T(8,128)(2,1)S(1)}, bf16[256,1024]{1,0:T(8,128)(2,1)}, u32[]{:S(2)}, u32[]{:S(2)}) collective-permute-start(bf16[256,1024]{1,0:T(8,128)(2,1)S(1)} %bitcast.32), channel_id=1, source_target_pairs={{0,8},{8,0},{16,24},{24,16},{1,9},{9,1},{17,25},{25,17},{2,10},{10... | collective-permute-start | bytes 1572872 | tf_op jit(solution)/shard_map/ppermute | solution.py:841
  43.8 10.9 %collective-permute-start.14 = (bf16[1088,128]{1,0:T(8,128)(2,1)S(1)}, bf16[1088,128]{1,0:T(8,128)(2,1)S(1)}, u32[]{:S(2)}, u32[]{:S(2)}) collective-permute-start(bf16[1088,128]{1,0:T(8,128)(2,1)S(1)} %collective-permute-done.8.refs_2_), channel_id=1, source_target_pairs={{0,2},{1,3},{2,4},{3,5},{4,6},{5,7},{6,0},{7,1},{8,10},{9,11},{10,... | collective-permute-start | bytes 835592 | tf_op jit(solution)/shard_map/ppermute | solution.py:878
  44.2 10.5 %collective-permute-start.15 = (bf16[1088,128]{1,0:T(8,128)(2,1)S(1)}, bf16[1088,128]{1,0:T(8,128)(2,1)S(1)}, u32[]{:S(2)}, u32[]{:S(2)}) collective-permute-start(bf16[1088,128]{1,0:T(8,128)(2,1)S(1)} %collective-permute-done.8.refs_2_), channel_id=1, source_target_pairs={{0,1},{1,0},{2,3},{3,2},{4,5},{5,4},{6,7},{7,6},{8,9},{9,8},{10,11... | collective-permute-start | bytes 835592 | tf_op jit(solution)/shard_map/ppermute | solution.py:873
  45.1 8.2 %collective-permute-start.13 = (bf16[128,1024]{1,0:T(8,128)(2,1)}, bf16[128,1024]{1,0:T(8,128)(2,1)S(1)}, u32[]{:S(2)}, u32[]{:S(2)}) collective-permute-start(bf16[128,1024]{1,0:T(8,128)(2,1)} %get-tuple-element.592), channel_id=1, source_target_pairs={{0,16},{8,24},{16,0},{24,8},{1,17},{9,25},{17,1},{25,9},{2,18},{10... | collective-permute-start | bytes 786440 | tf_op jit(solution)/shard_map/ppermute | solution.py:845
  54.7 5.7 %collective-permute-start.19 = (bf16[256,256]{1,0:T(8,128)(2,1)S(1)}, bf16[256,256]{1,0:T(8,128)(2,1)S(1)}, u32[]{:S(2)}, u32[]{:S(2)}) collective-permute-start(bf16[256,256]{1,0:T(8,128)(2,1)S(1)} %get-tuple-element.611), channel_id=1, source_target_pairs={{0,24},{8,16},{16,8},{24,0},{1,25},{9,17},{17,9},{25,1},{2,26},{10... | collective-permute-start | bytes 393224 | tf_op jit(solution)/shard_map/ppermute | solution.py:849
  54.7 7.8 %collective-permute-start.18 = (bf16[256,256]{1,0:T(8,128)(2,1)S(1)}, bf16[256,256]{1,0:T(8,128)(2,1)S(1)}, u32[]{:S(2)}, u32[]{:S(2)}) collective-permute-start(bf16[256,256]{1,0:T(8,128)(2,1)S(1)} %get-tuple-element.610), channel_id=1, source_target_pairs={{0,16},{8,24},{16,0},{24,8},{1,17},{9,25},{17,1},{25,9},{2,18},{10... | collective-permute-start | bytes 393224 | tf_op jit(solution)/shard_map/ppermute | solution.py:845
  55.8 6.8 %collective-permute-start.17 = (bf16[256,256]{1,0:T(8,128)(2,1)S(1)}, bf16[256,256]{1,0:T(8,128)(2,1)S(1)}, u32[]{:S(2)}, u32[]{:S(2)}) collective-permute-start(bf16[256,256]{1,0:T(8,128)(2,1)S(1)} %get-tuple-element.609), channel_id=1, source_target_pairs={{0,8},{8,0},{16,24},{24,16},{1,9},{9,1},{17,25},{25,17},{2,10},{10... | collective-permute-start | bytes 393224 | tf_op jit(solution)/shard_map/ppermute | solution.py:841
  56.6 8.6 %collective-permute-start.20 = (bf16[1088,128]{1,0:T(8,128)(2,1)S(1)}, bf16[1088,128]{1,0:T(8,128)(2,1)S(1)}, u32[]{:S(2)}, u32[]{:S(2)}) collective-permute-start(bf16[1088,128]{1,0:T(8,128)(2,1)S(1)} %collective-permute-done.14.refs_3_), channel_id=1, source_target_pairs={{0,1},{1,0},{2,3},{3,2},{4,5},{5,4},{6,7},{7,6},{8,9},{9,8},{10,11... | collective-permute-start | bytes 835592 | tf_op jit(solution)/shard_map/ppermute | solution.py:873
  65.2 9.4 %collective-permute-start.25 = (bf16[256,1024]{1,0:T(8,128)(2,1)S(1)}, bf16[256,1024]{1,0:T(8,128)(2,1)S(1)}, u32[]{:S(2)}, u32[]{:S(2)}) collective-permute-start(bf16[256,1024]{1,0:T(8,128)(2,1)S(1)} %bitcast.18), channel_id=1, source_target_pairs={{0,8},{8,0},{16,24},{24,16},{1,9},{9,1},{17,25},{25,17},{2,10},{10... | collective-permute-start | bytes 1572872 | tf_op jit(solution)/shard_map/ppermute | solution.py:841
  65.2 9.4 %collective-permute-start.24 = (bf16[128,1024]{1,0:T(8,128)(2,1)S(1)}, bf16[128,1024]{1,0:T(8,128)(2,1)S(1)}, u32[]{:S(2)}, u32[]{:S(2)}) collective-permute-start(bf16[128,1024]{1,0:T(8,128)(2,1)S(1)} %get-tuple-element.637), channel_id=1, source_target_pairs={{0,16},{8,24},{16,0},{24,8},{1,17},{9,25},{17,1},{25,9},{2,18},{10... | collective-permute-start | bytes 786440 | tf_op jit(solution)/shard_map/ppermute | solution.py:845
  65.9 8.6 %collective-permute-start.22 = (bf16[704,128]{1,0:T(8,128)(2,1)S(1)}, bf16[704,128]{1,0:T(8,128)(2,1)S(1)}, u32[]{:S(2)}, u32[]{:S(2)}) collective-permute-start(bf16[704,128]{1,0:T(8,128)(2,1)S(1)} %copy-done.63), channel_id=1, source_target_pairs={{0,2},{1,3},{2,4},{3,5},{4,6},{5,7},{6,0},{7,1},{8,10},{9,11},{10,... | collective-permute-start | bytes 540680 | tf_op jit(solution)/shard_map/ppermute | solution.py:878
  65.9 8.6 %collective-permute-start.23 = (bf16[704,128]{1,0:T(8,128)(2,1)S(1)}, bf16[704,128]{1,0:T(8,128)(2,1)S(1)}, u32[]{:S(2)}, u32[]{:S(2)}) collective-permute-start(bf16[704,128]{1,0:T(8,128)(2,1)S(1)} %copy-done.63), channel_id=1, source_target_pairs={{0,1},{1,0},{2,3},{3,2},{4,5},{5,4},{6,7},{7,6},{8,9},{9,8},{10,11... | collective-permute-start | bytes 540680 | tf_op jit(solution)/shard_map/ppermute | solution.py:873
  74.5 20.0 %collective-permute-start.29 = (bf16[256,1024]{1,0:T(8,128)(2,1)S(1)}, bf16[256,1024]{1,0:T(8,128)(2,1)S(1)}, u32[]{:S(2)}, u32[]{:S(2)}) collective-permute-start(bf16[256,1024]{1,0:T(8,128)(2,1)S(1)} %get-tuple-element.835.wo0.w0), channel_id=1, source_target_pairs={{0,8},{8,0},{16,24},{24,16},{1,9},{9,1},{17,25},{25,17},{2,10},{10... | collective-permute-start | bytes 1572872 | tf_op jit(solution)/shard_map/ppermute | solution.py:841
  74.6 20.0 %collective-permute-start.30 = (bf16[256,1024]{1,0:T(8,128)(2,1)S(1)}, bf16[256,1024]{1,0:T(8,128)(2,1)S(1)}, u32[]{:S(2)}, u32[]{:S(2)}) collective-permute-start(bf16[256,1024]{1,0:T(8,128)(2,1)S(1)} %get-tuple-element.835.wo0.w0), channel_id=1, source_target_pairs={{0,16},{8,24},{16,0},{24,8},{1,17},{9,25},{17,1},{25,9},{2,18},{10... | collective-permute-start | bytes 1572872 | tf_op jit(solution)/shard_map/ppermute | solution.py:845
  76.0 18.6 %collective-permute-start.28 = (bf16[128,1024]{1,0:T(8,128)(2,1)S(1)}, bf16[128,1024]{1,0:T(8,128)(2,1)S(1)}, u32[]{:S(2)}, u32[]{:S(2)}) collective-permute-start(bf16[128,1024]{1,0:T(8,128)(2,1)S(1)} %get-tuple-element.668), channel_id=1, source_target_pairs={{0,16},{8,24},{16,0},{24,8},{1,17},{9,25},{17,1},{25,9},{2,18},{10... | collective-permute-start | bytes 786440 | tf_op jit(solution)/shard_map/ppermute | solution.py:845
  76.7 12.7 %collective-permute-start.26 = (bf16[704,128]{1,0:T(8,128)(2,1)S(1)}, bf16[704,128]{1,0:T(8,128)(2,1)S(1)}, u32[]{:S(2)}, u32[]{:S(2)}) collective-permute-start(bf16[704,128]{1,0:T(8,128)(2,1)S(1)} %collective-permute-done.22.refs_2_), channel_id=1, source_target_pairs={{0,2},{1,3},{2,4},{3,5},{4,6},{5,7},{6,0},{7,1},{8,10},{9,11},{10,... | collective-permute-start | bytes 540680 | tf_op jit(solution)/shard_map/ppermute | solution.py:878
  76.9 12.5 %collective-permute-start.27 = (bf16[704,128]{1,0:T(8,128)(2,1)S(1)}, bf16[704,128]{1,0:T(8,128)(2,1)S(1)}, u32[]{:S(2)}, u32[]{:S(2)}) collective-permute-start(bf16[704,128]{1,0:T(8,128)(2,1)S(1)} %collective-permute-done.22.refs_2_), channel_id=1, source_target_pairs={{0,1},{1,0},{2,3},{3,2},{4,5},{5,4},{6,7},{7,6},{8,9},{9,8},{10,11... | collective-permute-start | bytes 540680 | tf_op jit(solution)/shard_map/ppermute | solution.py:873
  94.7 10.9 %collective-permute-start.31 = (bf16[256,1024]{1,0:T(8,128)(2,1)S(1)}, bf16[256,1024]{1,0:T(8,128)(2,1)S(1)}, u32[]{:S(2)}, u32[]{:S(2)}) collective-permute-start(bf16[256,1024]{1,0:T(8,128)(2,1)S(1)} %pad_maximum_fusion.4), channel_id=1, source_target_pairs={{0,8},{8,0},{16,24},{24,16},{1,9},{9,1},{17,25},{25,17},{2,10},{10... | collective-permute-start | bytes 1572872 | tf_op jit(solution)/shard_map/ppermute | solution.py:841
  94.8 10.9 %collective-permute-start.34 = (bf16[1024,256]{1,0:T(8,128)(2,1)S(1)}, bf16[1024,256]{1,0:T(8,128)(2,1)S(1)}, u32[]{:S(2)}, u32[]{:S(2)}) collective-permute-start(bf16[1024,256]{1,0:T(8,128)(2,1)S(1)} %get-tuple-element.964.a0.act_ref), channel_id=1, source_target_pairs={{0,8},{8,0},{16,24},{24,16},{1,9},{9,1},{17,25},{25,17},{2,10},{10... | collective-permute-start | bytes 1572872 | tf_op jit(solution)/shard_map/ppermute | solution.py:841
  95.2 13.9 %collective-permute-start.35 = (bf16[1024,256]{1,0:T(8,128)(2,1)S(1)}, bf16[1024,256]{1,0:T(8,128)(2,1)S(1)}, u32[]{:S(2)}, u32[]{:S(2)}) collective-permute-start(bf16[1024,256]{1,0:T(8,128)(2,1)S(1)} %get-tuple-element.964.a0.act_ref), channel_id=1, source_target_pairs={{0,16},{8,24},{16,0},{24,8},{1,17},{9,25},{17,1},{25,9},{2,18},{10... | collective-permute-start | bytes 1572872 | tf_op jit(solution)/shard_map/ppermute | solution.py:845
  96.5 9.1 %collective-permute-start.32 = (bf16[256,1024]{1,0:T(8,128)(2,1)S(1)}, bf16[256,1024]{1,0:T(8,128)(2,1)S(1)}, u32[]{:S(2)}, u32[]{:S(2)}) collective-permute-start(bf16[256,1024]{1,0:T(8,128)(2,1)S(1)} %collective-permute-done.30.wo2.w2), channel_id=1, source_target_pairs={{0,8},{8,0},{16,24},{24,16},{1,9},{9,1},{17,25},{25,17},{2,10},{10... | collective-permute-start | bytes 1572872 | tf_op jit(solution)/shard_map/ppermute | solution.py:841
  96.5 7.0 %collective-permute-start.33 = (bf16[704,128]{1,0:T(8,128)(2,1)S(1)}, bf16[704,128]{1,0:T(8,128)(2,1)S(1)}, u32[]{:S(2)}, u32[]{:S(2)}) collective-permute-start(bf16[704,128]{1,0:T(8,128)(2,1)S(1)} %collective-permute-done.26.refs_3_), channel_id=1, source_target_pairs={{0,1},{1,0},{2,3},{3,2},{4,5},{5,4},{6,7},{7,6},{8,9},{9,8},{10,11... | collective-permute-start | bytes 540680 | tf_op jit(solution)/shard_map/ppermute | solution.py:873
  139.1 15.1 %collective-permute-start.38 = (bf16[256,1024]{1,0:T(8,128)(2,1)}, bf16[256,1024]{1,0:T(8,128)(2,1)}, u32[]{:S(2)}, u32[]{:S(2)}) collective-permute-start(bf16[256,1024]{1,0:T(8,128)(2,1)} %get-tuple-element.793), channel_id=1, source_target_pairs={{0,16},{8,24},{16,0},{24,8},{1,17},{9,25},{17,1},{25,9},{2,18},{10... | collective-permute-start | bytes 1572872 | tf_op jit(solution)/shard_map/ppermute | solution.py:845
  154.2 6.0 %collective-permute-start.39 = (bf16[512,1024]{1,0:T(8,128)(2,1)}, bf16[512,1024]{1,0:T(8,128)(2,1)S(1)}, u32[]{:S(2)}, u32[]{:S(2)}) collective-permute-start(bf16[512,1024]{1,0:T(8,128)(2,1)} %get-tuple-element.823), channel_id=1, source_target_pairs={{0,8},{8,0},{16,24},{24,16},{1,9},{9,1},{17,25},{25,17},{2,10},{10... | collective-permute-start | bytes 3145736 | tf_op jit(solution)/shard_map/ppermute | solution.py:841
  154.2 10.8 %collective-permute-start.40 = (bf16[1408,128]{1,0:T(8,128)(2,1)S(1)}, bf16[1408,128]{1,0:T(8,128)(2,1)S(1)}, u32[]{:S(2)}, u32[]{:S(2)}) collective-permute-start(bf16[1408,128]{1,0:T(8,128)(2,1)S(1)} %copy-done.94), channel_id=1, source_target_pairs={{0,1},{1,0},{2,3},{3,2},{4,5},{5,4},{6,7},{7,6},{8,9},{9,8},{10,11... | collective-permute-start | bytes 1081352 | tf_op jit(solution)/shard_map/ppermute | solution.py:873
  165.0 10.0 %collective-permute-start.41 = (bf16[1408,128]{1,0:T(8,128)(2,1)S(1)}, bf16[1408,128]{1,0:T(8,128)(2,1)S(1)}, u32[]{:S(2)}, u32[]{:S(2)}) collective-permute-start(bf16[1408,128]{1,0:T(8,128)(2,1)S(1)} %copy-done.93), channel_id=1, source_target_pairs={{0,1},{1,0},{2,3},{3,2},{4,5},{5,4},{6,7},{7,6},{8,9},{9,8},{10,11... | collective-permute-start | bytes 1081352 | tf_op jit(solution)/shard_map/ppermute | solution.py:873
  165.9 11.5 %collective-permute-start.45 = (bf16[1408,128]{1,0:T(8,128)(2,1)S(1)}, bf16[1408,128]{1,0:T(8,128)(2,1)S(1)}, u32[]{:S(2)}, u32[]{:S(2)}) collective-permute-start(bf16[1408,128]{1,0:T(8,128)(2,1)S(1)} %total.4), channel_id=1, source_target_pairs={{0,2},{1,3},{2,4},{3,5},{4,6},{5,7},{6,0},{7,1},{8,10},{9,11},{10,... | collective-permute-start | bytes 1081352 | tf_op jit(solution)/shard_map/ppermute | solution.py:878
  166.3 6.3 %collective-permute-start.43 = (bf16[256,256]{1,0:T(8,128)(2,1)S(1)}, bf16[256,256]{1,0:T(8,128)(2,1)S(1)}, u32[]{:S(2)}, u32[]{:S(2)}) collective-permute-start(bf16[256,256]{1,0:T(8,128)(2,1)S(1)} %get-tuple-element.872), channel_id=1, source_target_pairs={{0,16},{8,24},{16,0},{24,8},{1,17},{9,25},{17,1},{25,9},{2,18},{10... | collective-permute-start | bytes 393224 | tf_op jit(solution)/shard_map/ppermute | solution.py:845
  167.0 7.6 %collective-permute-start.44 = (bf16[256,256]{1,0:T(8,128)(2,1)S(1)}, bf16[256,256]{1,0:T(8,128)(2,1)S(1)}, u32[]{:S(2)}, u32[]{:S(2)}) collective-permute-start(bf16[256,256]{1,0:T(8,128)(2,1)S(1)} %get-tuple-element.873), channel_id=1, source_target_pairs={{0,24},{8,16},{16,8},{24,0},{1,25},{9,17},{17,9},{25,1},{2,26},{10... | collective-permute-start | bytes 393224 | tf_op jit(solution)/shard_map/ppermute | solution.py:849
  177.5 15.1 %collective-permute-start.47 = (bf16[256,1024]{1,0:T(8,128)(2,1)}, bf16[256,1024]{1,0:T(8,128)(2,1)S(1)}, u32[]{:S(2)}, u32[]{:S(2)}) collective-permute-start(bf16[256,1024]{1,0:T(8,128)(2,1)} %get-tuple-element.965.d0), channel_id=1, source_target_pairs={{0,8},{8,0},{16,24},{24,16},{1,9},{9,1},{17,25},{25,17},{2,10},{10... | collective-permute-start | bytes 1572872 | tf_op jit(solution)/shard_map/ppermute | solution.py:841
  177.5 15.9 %collective-permute-start.48 = (bf16[256,1024]{1,0:T(8,128)(2,1)}, bf16[256,1024]{1,0:T(8,128)(2,1)}, u32[]{:S(2)}, u32[]{:S(2)}) collective-permute-start(bf16[256,1024]{1,0:T(8,128)(2,1)} %get-tuple-element.965.d0), channel_id=1, source_target_pairs={{0,16},{8,24},{16,0},{24,8},{1,17},{9,25},{17,1},{25,9},{2,18},{10... | collective-permute-start | bytes 1572872 | tf_op jit(solution)/shard_map/ppermute | solution.py:845
  178.3 12.7 %collective-permute-start.46 = (bf16[1408,128]{1,0:T(8,128)(2,1)S(1)}, bf16[1408,128]{1,0:T(8,128)(2,1)S(1)}, u32[]{:S(2)}, u32[]{:S(2)}) collective-permute-start(bf16[1408,128]{1,0:T(8,128)(2,1)S(1)} %copy-done.92), channel_id=1, source_target_pairs={{0,1},{1,0},{2,3},{3,2},{4,5},{5,4},{6,7},{7,6},{8,9},{9,8},{10,11... | collective-permute-start | bytes 1081352 | tf_op jit(solution)/shard_map/ppermute | solution.py:873
  179.6 12.9 %collective-permute-start.49 = (bf16[1408,128]{1,0:T(8,128)(2,1)S(1)}, bf16[1408,128]{1,0:T(8,128)(2,1)S(1)}, u32[]{:S(2)}, u32[]{:S(2)}) collective-permute-start(bf16[1408,128]{1,0:T(8,128)(2,1)S(1)} %total.5), channel_id=1, source_target_pairs={{0,2},{1,3},{2,4},{3,5},{4,6},{5,7},{6,0},{7,1},{8,10},{9,11},{10,... | collective-permute-start | bytes 1081352 | tf_op jit(solution)/shard_map/ppermute | solution.py:878
  193.4 20.9 %collective-permute-start.53 = (bf16[2944,128]{1,0:T(8,128)(2,1)}, bf16[2944,128]{1,0:T(8,128)(2,1)S(1)}, u32[]{:S(2)}, u32[]{:S(2)}) collective-permute-start(bf16[2944,128]{1,0:T(8,128)(2,1)} %get-tuple-element.936), channel_id=1, source_target_pairs={{0,1},{1,0},{2,3},{3,2},{4,5},{5,4},{6,7},{7,6},{8,9},{9,8},{10,11... | collective-permute-start | bytes 2261000 | tf_op jit(solution)/shard_map/ppermute | solution.py:873
  193.8 20.5 %collective-permute-start.50 = (bf16[256,1024]{1,0:T(8,128)(2,1)}, bf16[256,1024]{1,0:T(8,128)(2,1)}, u32[]{:S(2)}, u32[]{:S(2)}) collective-permute-start(bf16[256,1024]{1,0:T(8,128)(2,1)} %collective-permute-done.48.d2), channel_id=1, source_target_pairs={{0,8},{8,0},{16,24},{24,16},{1,9},{9,1},{17,25},{25,17},{2,10},{10... | collective-permute-start | bytes 1572872 | tf_op jit(solution)/shard_map/ppermute | solution.py:841
  193.8 20.5 %collective-permute-start.51 = (bf16[256,1024]{1,0:T(8,128)(2,1)}, bf16[256,1024]{1,0:T(8,128)(2,1)}, u32[]{:S(2)}, u32[]{:S(2)}) collective-permute-start(bf16[256,1024]{1,0:T(8,128)(2,1)} %get-tuple-element.925), channel_id=1, source_target_pairs={{0,16},{8,24},{16,0},{24,8},{1,17},{9,25},{17,1},{25,9},{2,18},{10... | collective-permute-start | bytes 1572872 | tf_op jit(solution)/shard_map/ppermute | solution.py:845
  195.8 18.5 %collective-permute-start.52 = (bf16[1408,128]{1,0:T(8,128)(2,1)}, bf16[1408,128]{1,0:T(8,128)(2,1)}, u32[]{:S(2)}, u32[]{:S(2)}) collective-permute-start(bf16[1408,128]{1,0:T(8,128)(2,1)} %total.6), channel_id=1, source_target_pairs={{0,2},{1,3},{2,4},{3,5},{4,6},{5,7},{6,0},{7,1},{8,10},{9,11},{10,... | collective-permute-start | bytes 1081352 | tf_op jit(solution)/shard_map/ppermute | solution.py:878
  196.8 15.6 %collective-permute-start.54 = (bf16[512,128]{1,0:T(8,128)(2,1)S(1)}, bf16[512,128]{1,0:T(8,128)(2,1)S(1)}, u32[]{:S(2)}, u32[]{:S(2)}) collective-permute-start(bf16[512,128]{1,0:T(8,128)(2,1)S(1)} %constant_dynamic-slice_fusion.4), channel_id=1, source_target_pairs={{0,16},{8,24},{16,0},{24,8},{1,17},{9,25},{17,1},{25,9},{2,18},{10... | collective-permute-start | bytes 393224 | tf_op jit(solution)/shard_map/ppermute | solution.py:845
  214.3 8.1 %collective-permute-start.59 = (bf16[512,1024]{1,0:T(8,128)(2,1)S(1)}, bf16[512,1024]{1,0:T(8,128)(2,1)S(1)}, u32[]{:S(2)}, u32[]{:S(2)}) collective-permute-start(bf16[512,1024]{1,0:T(8,128)(2,1)S(1)} %get-tuple-element.961), channel_id=1, source_target_pairs={{0,8},{8,0},{16,24},{24,16},{1,9},{9,1},{17,25},{25,17},{2,10},{10... | collective-permute-start | bytes 3145736 | tf_op jit(solution)/shard_map/ppermute | solution.py:841
  214.4 13.7 %collective-permute-start.58 = (bf16[1536,128]{1,0:T(8,128)(2,1)S(1)}, bf16[1536,128]{1,0:T(8,128)(2,1)S(1)}, u32[]{:S(2)}, u32[]{:S(2)}) collective-permute-start(bf16[1536,128]{1,0:T(8,128)(2,1)S(1)} %copy-done.91), channel_id=1, source_target_pairs={{0,1},{1,0},{2,3},{3,2},{4,5},{5,4},{6,7},{7,6},{8,9},{9,8},{10,11... | collective-permute-start | bytes 1179656 | tf_op jit(solution)/shard_map/ppermute | solution.py:873
  216.1 7.6 %collective-permute-start.55 = (bf16[384,128]{1,0:T(8,128)(2,1)S(1)}, bf16[384,128]{1,0:T(8,128)(2,1)S(1)}, u32[]{:S(2)}, u32[]{:S(2)}) collective-permute-start(bf16[384,128]{1,0:T(8,128)(2,1)S(1)} %get-tuple-element.954), channel_id=1, source_target_pairs={{0,2},{1,3},{2,4},{3,5},{4,6},{5,7},{6,0},{7,1},{8,10},{9,11},{10,... | collective-permute-start | bytes 294920 | tf_op jit(solution)/shard_map/ppermute | solution.py:878
  216.2 10.8 %collective-permute-start.56 = (bf16[384,128]{1,0:T(8,128)(2,1)S(1)}, bf16[384,128]{1,0:T(8,128)(2,1)S(1)}, u32[]{:S(2)}, u32[]{:S(2)}) collective-permute-start(bf16[384,128]{1,0:T(8,128)(2,1)S(1)} %get-tuple-element.955), channel_id=1, source_target_pairs={{0,4},{1,5},{2,6},{3,7},{4,0},{5,1},{6,2},{7,3},{8,12},{9,13},{10,... | collective-permute-start | bytes 294920 | tf_op jit(solution)/shard_map/ppermute | solution.py:878
  218.9 8.1 %collective-permute-start.57 = (bf16[384,128]{1,0:T(8,128)(2,1)S(1)}, bf16[384,128]{1,0:T(8,128)(2,1)S(1)}, u32[]{:S(2)}, u32[]{:S(2)}) collective-permute-start(bf16[384,128]{1,0:T(8,128)(2,1)S(1)} %get-tuple-element.956), channel_id=1, source_target_pairs={{0,6},{1,7},{2,0},{3,1},{4,2},{5,3},{6,4},{7,5},{8,14},{9,15},{10,... | collective-permute-start | bytes 294920 | tf_op jit(solution)/shard_map/ppermute | solution.py:878
  228.1 15.3 %collective-permute-start.63 = (bf16[256,1024]{1,0:T(8,128)(2,1)S(1)}, bf16[256,1024]{1,0:T(8,128)(2,1)S(1)}, u32[]{:S(2)}, u32[]{:S(2)}) collective-permute-start(bf16[256,1024]{1,0:T(8,128)(2,1)S(1)} %get-tuple-element.991), channel_id=1, source_target_pairs={{0,16},{8,24},{16,0},{24,8},{1,17},{9,25},{17,1},{25,9},{2,18},{10... | collective-permute-start | bytes 1572872 | tf_op jit(solution)/shard_map/ppermute | solution.py:845
  229.5 7.7 %collective-permute-start.64 = (bf16[1024,128]{1,0:T(8,128)(2,1)S(1)}, bf16[1024,128]{1,0:T(8,128)(2,1)S(1)}, u32[]{:S(2)}, u32[]{:S(2)}) collective-permute-start(bf16[1024,128]{1,0:T(8,128)(2,1)S(1)} %get-tuple-element.993), channel_id=1, source_target_pairs={{0,1},{1,0},{2,3},{3,2},{4,5},{5,4},{6,7},{7,6},{8,9},{9,8},{10,11... | collective-permute-start | bytes 786440 | tf_op jit(solution)/shard_map/ppermute | solution.py:873
  231.1 7.6 %collective-permute-start.60 = (bf16[384,128]{1,0:T(8,128)(2,1)S(1)}, bf16[384,128]{1,0:T(8,128)(2,1)S(1)}, u32[]{:S(2)}, u32[]{:S(2)}) collective-permute-start(bf16[384,128]{1,0:T(8,128)(2,1)S(1)} %get-tuple-element.985), channel_id=1, source_target_pairs={{0,2},{1,3},{2,4},{3,5},{4,6},{5,7},{6,0},{7,1},{8,10},{9,11},{10,... | collective-permute-start | bytes 294920 | tf_op jit(solution)/shard_map/ppermute | solution.py:878
  231.2 12.2 %collective-permute-start.61 = (bf16[384,128]{1,0:T(8,128)(2,1)S(1)}, bf16[384,128]{1,0:T(8,128)(2,1)S(1)}, u32[]{:S(2)}, u32[]{:S(2)}) collective-permute-start(bf16[384,128]{1,0:T(8,128)(2,1)S(1)} %get-tuple-element.986), channel_id=1, source_target_pairs={{0,4},{1,5},{2,6},{3,7},{4,0},{5,1},{6,2},{7,3},{8,12},{9,13},{10,... | collective-permute-start | bytes 294920 | tf_op jit(solution)/shard_map/ppermute | solution.py:878
  233.4 10.0 %collective-permute-start.62 = (bf16[384,128]{1,0:T(8,128)(2,1)S(1)}, bf16[384,128]{1,0:T(8,128)(2,1)S(1)}, u32[]{:S(2)}, u32[]{:S(2)}) collective-permute-start(bf16[384,128]{1,0:T(8,128)(2,1)S(1)} %get-tuple-element.987), channel_id=1, source_target_pairs={{0,6},{1,7},{2,0},{3,1},{4,2},{5,3},{6,4},{7,5},{8,14},{9,15},{10,... | collective-permute-start | bytes 294920 | tf_op jit(solution)/shard_map/ppermute | solution.py:878
  245.6 9.5 %collective-permute-start.68 = (bf16[1600,128]{1,0:T(8,128)(2,1)}, bf16[1600,128]{1,0:T(8,128)(2,1)S(1)}, u32[]{:S(2)}, u32[]{:S(2)}) collective-permute-start(bf16[1600,128]{1,0:T(8,128)(2,1)} %get-tuple-element.1025), channel_id=1, source_target_pairs={{0,16},{8,24},{16,0},{24,8},{1,17},{9,25},{17,1},{25,9},{2,18},{10... | collective-permute-start | bytes 1228808 | tf_op jit(solution)/shard_map/ppermute | solution.py:845
  245.9 8.6 %collective-permute-start.65 = (bf16[256,128]{1,0:T(8,128)(2,1)}, bf16[256,128]{1,0:T(8,128)(2,1)S(1)}, u32[]{:S(2)}, u32[]{:S(2)}) collective-permute-start(bf16[256,128]{1,0:T(8,128)(2,1)} %get-tuple-element.1008), channel_id=1, source_target_pairs={{0,2},{1,3},{2,4},{3,5},{4,6},{5,7},{6,0},{7,1},{8,10},{9,11},{10,... | collective-permute-start | bytes 196616 | tf_op jit(solution)/shard_map/ppermute | solution.py:878
  248.9 6.1 %collective-permute-start.66 = (bf16[256,128]{1,0:T(8,128)(2,1)}, bf16[256,128]{1,0:T(8,128)(2,1)}, u32[]{:S(2)}, u32[]{:S(2)}) collective-permute-start(bf16[256,128]{1,0:T(8,128)(2,1)} %get-tuple-element.1009), channel_id=1, source_target_pairs={{0,4},{1,5},{2,6},{3,7},{4,0},{5,1},{6,2},{7,3},{8,12},{9,13},{10,... | collective-permute-start | bytes 196616 | tf_op jit(solution)/shard_map/ppermute | solution.py:878
  249.8 5.3 %collective-permute-start.67 = (bf16[256,128]{1,0:T(8,128)(2,1)}, bf16[256,128]{1,0:T(8,128)(2,1)}, u32[]{:S(2)}, u32[]{:S(2)}) collective-permute-start(bf16[256,128]{1,0:T(8,128)(2,1)} %get-tuple-element.1010), channel_id=1, source_target_pairs={{0,6},{1,7},{2,0},{3,1},{4,2},{5,3},{6,4},{7,5},{8,14},{9,15},{10,... | collective-permute-start | bytes 196616 | tf_op jit(solution)/shard_map/ppermute | solution.py:878
  (103 other events, 807.5 us)
Sparse Core Ops, SparseCore 0:
  43.7 59.9 all-gather.2
  180.1 71.1 reduce-scatter.1

commit v2 on v1

--- a/solution.py
+++ b/solution.py
@@ -607,12 +607,20 @@
     )(act, grad)
 
 
-def simple(kernel, name, args, outs, limit=24):
+def simple(kernel, name, args, outs, limit=24, half=()):
+    half = dict(half)
+
+    def spec(i, x):
+        if i not in half:
+            return SMEM if x.dtype == jnp.int32 else fixed(x.shape)
+        shape = (x.shape[0] // 2, x.shape[1])
+        return pl.BlockSpec(shape, lambda _: (half[i], 0), pipeline_mode=pl.Buffered(1))
+
     return pl.pallas_call(
         kernel,
         name=name,
         grid=(1,),
-        in_specs=[SMEM if x.dtype == jnp.int32 else fixed(x.shape) for x in args],
+        in_specs=[spec(i, x) for i, x in enumerate(args)],
         out_specs=[fixed(x.shape) for x in outs],
         out_shape=outs,
         compiler_params=params(limit),
@@ -632,15 +640,9 @@
     return simple(sum_kernel, "total", pieces, [shaped(bf16, *pieces[0].shape)])[0]
 
 
-def halves_kernel(kept_ref, got_ref, near_ref, far_ref):
-    rows = near_ref.shape[0]
-    near_ref[...] = kept_ref[:rows, :].astype(f32) + got_ref[:rows, :].astype(f32)
-    far_ref[...] = (kept_ref[rows:, :].astype(f32) + got_ref[rows:, :].astype(f32)).astype(bf16)
-
-
-def halves(kept, got):
+def lower(kept, got):
     rows, width = kept.shape[0] // 2, kept.shape[1]
-    return simple(halves_kernel, "halves", (kept, got), [shaped(f32, rows, width), shaped(bf16, rows, width)])
+    return simple(sum_kernel, "lower", (kept, got), [shaped(bf16, rows, width)], half=((0, 1), (1, 1)))[0]
 
 
 def slots_kernel(kept_ref, got_ref, *outs):
@@ -664,8 +666,8 @@
     return scale * (pressed - unit * jnp.mean(pressed * unit, axis=-1, keepdims=True))
 
 
-def branch_kernel(near_ref, far_ref, mid_ref, og_ref, gain_ref, w0, w1, w2, w3, d_mid_ref, d_ref, a0, a1, a2, a3):
-    grad = near_ref[...] + far_ref[...].astype(f32)
+def branch_kernel(kept_ref, got_ref, far_ref, mid_ref, og_ref, gain_ref, w0, w1, w2, w3, d_mid_ref, d_ref, a0, a1, a2, a3):
+    grad = kept_ref[...].astype(f32) + got_ref[...].astype(f32) + far_ref[...].astype(f32)
     d_mid = og_ref[...].astype(f32) + back_through_norm(grad, mid_ref[...], gain_ref[...])
     d_mid_ref[...] = d_mid
     d_branch = d_mid.astype(bf16)
@@ -674,8 +676,8 @@
         a[...] = mul(d_branch, w[...], 1, 1).astype(bf16)
 
 
-def token_grad_kernel(near_ref, far_ref, tok_ref, gain_ref, d_mid_ref, out_ref):
-    grad = near_ref[...] + far_ref[...].astype(f32)
+def token_grad_kernel(kept_ref, got_ref, far_ref, tok_ref, gain_ref, d_mid_ref, out_ref):
+    grad = kept_ref[...].astype(f32) + got_ref[...].astype(f32) + far_ref[...].astype(f32)
     out_ref[...] = (d_mid_ref[...] + back_through_norm(grad, tok_ref[...].astype(f32), gain_ref[...])).astype(bf16)
 
 
@@ -980,7 +982,8 @@
     s.nm, s.hidden, s.d_gu, s.mid, s.dnm, dnm_sent, s.lo, s.lo_sent = ffn_call(
         me_arg, s.tok, s.og, s.att, s.wo, s.mlp_gain, ffn_all, s.w_down
     )
-    s.dnm, s.dnm_far = halves(s.dnm, to_core(dnm_sent))
+    s.dnm_got = to_core(dnm_sent)
+    s.dnm_far = lower(s.dnm, s.dnm_got)
     del s.tok, s.att, s.w_down
     s.fence()
     s.dnm_far = to_chip(s.dnm_far)
@@ -991,15 +994,16 @@
     del s.nm, s.d_gu, s.hidden, s.og
     s.fence()
     s.f_sent[3] = to_y(s.f_sent[3])
-    lo_got = to_core(s.lo_sent)
+    s.lo_got = to_core(s.lo_sent)
     s.d_middle, s.d_branch, *s.d_att = simple(
         branch_kernel,
         "branch",
-        (s.dnm, s.dnm_far, s.mid, s.out_grad, s.mlp_gain, *s.wo),
+        (s.dnm, s.dnm_got, s.dnm_far, s.mid, s.out_grad, s.mlp_gain, *s.wo),
         [shaped(f32, rows, width), shaped(bf16, rows, width)] + [shaped(bf16, rows, part)] * SEQ,
+        half=((0, 0), (1, 0)),
     )
-    s.lo, s.lo_far = halves(s.lo, lo_got)
-    del s.dnm, s.dnm_far, s.wo, s.lo_sent, s.g_down
+    s.lo_far = lower(s.lo, s.lo_got)
+    del s.dnm, s.dnm_got, s.dnm_far, s.wo, s.lo_sent, s.g_down
     s.fence()
     s.d_att = exchange_rel(s.d_att)
     s.f_sent[2] = to_y(s.f_sent[2])
@@ -1038,15 +1042,22 @@
 
     s.sent[1] = to_y(s.sent[1])
     s.kept[0] = over_z(*slots(s.kept[0], s.sent[0]))
-    s.dnin, s.dnin_far = halves(s.dnin, to_core(s.dnin_sent))
+    s.dnin_got = to_core(s.dnin_sent)
+    s.dnin_far = lower(s.dnin, s.dnin_got)
     s.out_kept, s.out_sent = out_projection_grad(place, s.attended, s.d_branch, dp)
     del s.d_branch, s.attended, s.dnin_sent
     s.fence()
     s.kept[1] = over_z(*slots(s.kept[1], s.sent[1]))
     s.out_kept = slots(s.out_kept, to_y(s.out_sent))
     s.dnin_far = to_chip(s.dnin_far)
-    s.layer_out = total(s.mid, s.lo, s.lo_far)
-    del s.lo, s.lo_far, s.mid
+    s.layer_out = simple(
+        sum_kernel,
+        "layer_out",
+        (s.mid, s.lo, s.lo_got, s.lo_far),
+        [shaped(bf16, rows, width)],
+        half=((1, 0), (2, 0)),
+    )[0]
+    del s.lo, s.lo_got, s.lo_far, s.mid
     s.fence()
     s.mine, s.near, far = cut(me_arg, s.kept, (s.f_kept[0], s.sent[0], s.f), s.d_qkv[1])
     s.far = to_chip(far)
@@ -1054,12 +1065,13 @@
     s.token_grad = simple(
         token_grad_kernel,
         "token_grad",
-        (s.dnin, s.dnin_far, s.tokens, s.attn_gain, s.d_middle),
+        (s.dnin, s.dnin_got, s.dnin_far, s.tokens, s.attn_gain, s.d_middle),
         [shaped(bf16, rows, width)],
         60,
+        ((0, 0), (1, 0)),
     )[0]
     s.g_down = g_down
-    del s.kept, s.sent, s.out_sent, s.dnin, s.d_middle, s.f, s.f_kept, s.f_sent
+    del s.kept, s.sent, s.out_sent, s.dnin, s.dnin_got, s.d_middle, s.f, s.f_kept, s.f_sent
     s.fence()
     count = s.mine.shape[0]
     args = (me_arg, s.near, s.far, *s.d_qkv, s.values_far)

time: 269 us -> 269 us (level)
    unnamed x202 -> x204, local copies, waits for them, and re-layouts: 15.8 us -> 15.3 us
where the time goes in v2:
time: 269 us; the launch traced here: 267 us
  Pallas kernels  98.3 us (37%)
  waiting for transfers between devices  71.2 us (26%)
  starting transfers between devices  56.5 us (21%)
  local copies, waits for them, and re-layouts  18.3 us (7%)
  between operations  15.3 us (6%)
  other arithmetic  7.61 us (3%)
    ppermute x16, waiting for transfers between devices, to_chip(): return lax.ppermute(value, 'seq', [(i, i ^ 2) for i in range(SEQ)])  26.9 us
    ppermute x18, waiting for transfers between devices, to_z(): lax.ppermute(value, 'dp', [(i, (i + 2 * hops) % dp) for i in range(dp)])  22 us
    pallas_call x2, Pallas kernels, attend_back_call(): pl.pallas_call(functools.partial(attend_back_kernel, dp, pieces), name='a...  21.9 us
    ppermute x18, starting transfers between devices, to_z(): lax.ppermute(value, 'dp', [(i, (i + 2 * hops) % dp) for i in range(dp)])  21.3 us
    pallas_call x1, Pallas kernels, ffn_call(): pl.pallas_call(ffn_kernel, name='ffn', grid_spec=pltpu.PrefetchScalarGrid...  21.2 us
    ppermute x16, starting transfers between devices, to_chip(): return lax.ppermute(value, 'seq', [(i, i ^ 2) for i in range(SEQ)])  17 us
    pallas_call x15, Pallas kernels, simple(): pl.pallas_call(kernel, name=name, grid=(1,), in_specs=[spec(i, x) for i,...  15.4 us
    unnamed x204, local copies, waits for them, and re-layouts  15.3 us
  transfers between devices with their start and end apart: 72, of which 32 were waited for; matrix products, arithmetic and copies ran while one was open for 4% of the time, Pallas kernels for 26%

profile of v2, /device:TPU:0, one launch (start us, length us, event | category | flops | bytes accessed | tf_op | source)
XLA Modules:
  0.0 267.2 jit_solution(10468193037338609499)
XLA Ops:
  7.2 2.3 pack_attn.1
  9.5 3.1 %collective-permute-start.3 = (bf16[704,128]{1,0:T(8,128)(2,1)}, bf16[704,128]{1,0:T(8,128)(2,1)S(1)}, u32[]{:S(2)}, u32[]{:S(2)}) collective-permute-start(bf16[704,128]{1,0:T(8,128)(2,1)} %get-tuple-element.707.refs_0_), channel_id=1, source_target_pairs={{0,2},{1,3},{2,4},{3,5},{4,6},{5,7},{6,0},{7,1},{8,10},{9,11},{10,... | collective-permute-start | bytes 540680 | tf_op jit(solution)/shard_map/ppermute | solution.py:880
  12.6 1.5 collective-permute-start.4
  14.1 1.5 collective-permute-start.1
  16.0 2.6 collective-permute-done.1
  21.4 1.6 collective-permute-start.6
  24.3 1.5 collective-permute-start.5
  25.8 3.0 %fusion = (f32[1024,32]{1,0:T(8,128)S(1)}, f32[1024,32]{1,0:T(8,128)}, f32[1024,32]{1,0:T(8,128)}) fusion(f32[32]{0:T(128)S(1)} %multiply_exponential_fusion, f32[1024]{0:T(1024)S(1)} %iota_convert_fusion), kind=kLoop, calls=%fused_computation.8 | loop fusion | flops 65536 | bytes 397440 | tf_op jit(solution)/shard_map/neg | solution.py:888
  28.9 2.3 pack_ffn.1
  31.2 1.2 collective-permute-done.5
  33.2 1.6 collective-permute-start.8
  34.7 1.3 collective-permute-start.9
  36.1 1.3 collective-permute-start.11
  37.9 3.1 %pad_maximum_fusion = (f32[1024,128]{1,0:T(8,128)S(1)}, f32[1024,128]{1,0:T(8,128)S(1)}) fusion(f32[1024,32]{1,0:T(8,128)} %get-tuple-element.1064, f32[1024,32]{1,0:T(8,128)} %get-tuple-element.1063, f32[1024,32]{1,0:T(8,128)S(1)} %get-tuple-element.1062), kind=kLoop, calls=%fused_computation.2 | loop fusion | flops 786432 | bytes 1441792 | tf_op jit(solution)/shard_map/concatenate | solution.py:888
  41.2 1.5 collective-permute-done.11
  47.0 6.3 %collective-permute-done.13 = bf16[128,1024]{1,0:T(8,128)(2,1)S(1)} collective-permute-done((bf16[128,1024]{1,0:T(8,128)(2,1)}, bf16[128,1024]{1,0:T(8,128)(2,1)S(1)}, u32[]{:S(2)}, u32[]{:S(2)}) %collective-permute-start.13) | collective-permute-done | bytes 262176 | tf_op jit(solution)/shard_map/ppermute | solution.py:847
  53.3 1.4 collective-permute-done.14.refs_3_
  57.7 1.2 constant_dynamic-update-slice_fusion.8
  59.0 1.5 collective-permute-done.19
  60.4 2.1 collective-permute-done.18
  62.7 2.5 collective-permute-done.20.refs_7_
  65.9 1.2 collective-permute-start.23
  68.3 3.3 %qkv.1 = (bf16[1024,1024]{1,0:T(8,128)(2,1)S(1)}, bf16[1024,256]{1,0:T(8,128)(2,1)S(1)}, bf16[1024,256]{1,0:T(8,128)(2,1)S(1)}, bf16[1024,256]{1,0:T(8,128)(2,1)S(1)}) custom-call(s32[1]{0:T(128)} %bitcast.5.me_ref, bf16[1024,1024]{1,0:T(8,128)(2,1)S(1)} %constant_dynamic-update-slice_fusion.5.tok_ref, bf16[1024,256]{1,0:T(8,128)(2,1)S(1)} %pad_maximum_fusion.2.first_ref, ...), custom_call_target="tpu_custom_call" | custom-call | tf_op jit(solution)/shard_map/qkv/pallas_call | solution.py:76
  71.7 1.4 copy-done.5
  73.1 1.5 collective-permute-done.22.refs_2_
  74.6 1.3 collective-permute-start.30
  77.8 9.0 %attend.1 = (bf16[1024,256]{1,0:T(8,128)(2,1)S(1)}, f32[2,2,1024]{2,1,0:T(2,128)S(1)}) custom-call(bf16[1024,256]{1,0:T(8,128)(2,1)S(1)} %get-tuple-element.914.q_ref, bf16[1024,256]{1,0:T(8,128)(2,1)S(1)} %get-tuple-element.915.k_ref, bf16[1024,256]{1,0:T(8,128)(2,1)S(1)} %get-tuple-element.916.v_ref, s32[1,1024]{1,0:T(1,128)S(1)} %copy-done.73), custom_call_target="tpu_custom_call" | custom-call | tf_op jit(solution)/shard_map/attend/pallas_call | solution.py:152
  86.8 2.6 collective-permute-done.26.refs_3_
  89.4 5.2 %collective-permute-done.28 = bf16[128,1024]{1,0:T(8,128)(2,1)S(1)} collective-permute-done((bf16[128,1024]{1,0:T(8,128)(2,1)S(1)}, bf16[128,1024]{1,0:T(8,128)(2,1)S(1)}, u32[]{:S(2)}, u32[]{:S(2)}) %collective-permute-start.28) | collective-permute-done | bytes 262176 | tf_op jit(solution)/shard_map/ppermute | solution.py:847
  95.2 1.3 collective-permute-start.35
  97.6 6.0 %collective-permute-done.33.refs_7_ = bf16[704,128]{1,0:T(8,128)(2,1)S(1)} collective-permute-done((bf16[704,128]{1,0:T(8,128)(2,1)S(1)}, bf16[704,128]{1,0:T(8,128)(2,1)S(1)}, u32[]{:S(2)}, u32[]{:S(2)}) %collective-permute-start.33) | collective-permute-done | bytes 180256 | tf_op jit(solution)/shard_map/ppermute | solution.py:875
  105.7 3.5 %collective-permute-done.35.a2 = bf16[1024,256]{1,0:T(8,128)(2,1)S(1)} collective-permute-done((bf16[1024,256]{1,0:T(8,128)(2,1)S(1)}, bf16[1024,256]{1,0:T(8,128)(2,1)S(1)}, u32[]{:S(2)}, u32[]{:S(2)}) %collective-permute-start.35) | collective-permute-done | bytes 524320 | tf_op jit(solution)/shard_map/ppermute | solution.py:847
  109.2 1.9 collective-permute-done.36.a3
  111.9 21.2 %ffn.1 = (bf16[1024,1024]{1,0:T(8,128)(2,1)}, bf16[1024,704]{1,0:T(8,128)(2,1)}, bf16[1024,1408]{1,0:T(8,128)(2,1)}, f32[256,1024]{1,0:T(8,128)}, bf16[512,1024]...) custom-call(s32[1]{0:T(128)} %bitcast.5.me_ref, ...), custom_call_target="tpu_custom_call" | custom-call | tf_op jit(solution)/shard_map/ffn/pallas_call | solution.py:479
  133.3 2.7 %collective-permute-done.37.refs_1_.got_ref = bf16[512,1024]{1,0:T(8,128)(2,1)S(1)} collective-permute-done((bf16[512,1024]{1,0:T(8,128)(2,1)}, bf16[512,1024]{1,0:T(8,128)(2,1)S(1)}, u32[]{:S(2)}, u32[]{:S(2)}) %collective-permute-start.37) | collective-permute-done | bytes 1048608 | tf_op jit(solution)/shard_map/ppermute | solution.py:843
  136.0 1.2 copy-done.22
  138.1 1.3 collective-permute-start.38
  139.4 8.1 %columns_grad.1 = (bf16[1408,128]{1,0:T(8,128)(2,1)}, bf16[1408,128]{1,0:T(8,128)(2,1)}, bf16[1408,128]{1,0:T(8,128)(2,1)}, bf16[1408,128]{1,0:T(8,128)(2,1)}, b...) custom-call(s32[3]{0:T(128)} %pad_add_fusion.place_ref, ...), custom_call_target="tpu_custom_call" | custom-call | tf_op jit(solution)/shard_map/columns_grad/pallas_call | solution.py:539
  147.5 5.6 %down_grad.1 = bf16[704,1024]{1,0:T(8,128)(2,1)} custom-call(bf16[1024,704]{1,0:T(8,128)(2,1)} %get-tuple-element.807.act_ref, bf16[1024,1024]{1,0:T(8,128)(2,1)} %copy-done.81), custom_call_target="tpu_custom_call" | custom-call | tf_op jit(solution)/shard_map/down_grad/pallas_call | solution.py:599
  154.0 1.2 copy-done.24
  158.4 2.9 %branch.1 = (f32[256,1024]{1,0:T(8,128)S(1)}, bf16[256,1024]{1,0:T(8,128)(2,1)}, bf16[256,256]{1,0:T(8,128)(2,1)S(1)}, bf16[256,256]{1,0:T(8,128)(2,1)S(1)}, bf1...) custom-call(bf16[512,1024]{1,0:T(8,128)(2,1)S(1)} %copy-done.23, ...), custom_call_target="tpu_custom_call" | custom-call | tf_op jit(solution)/shard_map/branch/pallas_call | solution.py:619
  167.1 4.4 %collective-permute-done.43.d2 = bf16[256,256]{1,0:T(8,128)(2,1)S(1)} collective-permute-done((bf16[256,256]{1,0:T(8,128)(2,1)S(1)}, bf16[256,256]{1,0:T(8,128)(2,1)S(1)}, u32[]{:S(2)}, u32[]{:S(2)}) %collective-permute-start.43) | collective-permute-done | bytes 131104 | tf_op jit(solution)/shard_map/ppermute | solution.py:847
  171.5 2.0 collective-permute-done.44.d3
  174.0 2.9 %collective-permute-done.45.refs_2_ = bf16[1408,128]{1,0:T(8,128)(2,1)S(1)} collective-permute-done((bf16[1408,128]{1,0:T(8,128)(2,1)S(1)}, bf16[1408,128]{1,0:T(8,128)(2,1)S(1)}, u32[]{:S(2)}, u32[]{:S(2)}) %collective-permute-start.45) | collective-permute-done | bytes 360480 | tf_op jit(solution)/shard_map/ppermute | solution.py:880
  179.0 11.1 %attend_back.2 = (bf16[1024,384]{1,0:T(8,128)(2,1)}, bf16[4,384,128]{2,1,0:T(8,128)(2,1)}, bf16[2944,128]{1,0:T(8,128)(2,1)}) custom-call(s32[3]{0:T(128)} %pad_add_fusion.place_ref, bf16[1024,256]{1,0:T(8,128)(2,1)} %copy-done.10, bf16[1024,256]{1,0:T(8,128)(2,1)} %copy-done.11, bf16[1024,256]{1,0:T(8,128)(2,1)} %copy-done.12, bf16[256,256]{1,0:T(8,128)(2,1)} %copy-done.42, ...), custom_call_target="tpu_custom_call" | custom-call | tf_op jit(solution)/shard_map/attend_back/pallas_call | solution.py:236
  193.1 1.2 collective-permute-start.51
  197.0 10.9 %attend_back.3 = (bf16[1024,384]{1,0:T(8,128)(2,1)}, bf16[4,384,128]{2,1,0:T(8,128)(2,1)}, bf16[1536,128]{1,0:T(8,128)(2,1)}) custom-call(s32[3]{0:T(128)} %pad_add_fusion.place_ref, bf16[1024,256]{1,0:T(8,128)(2,1)} %copy-done.10, bf16[1024,256]{1,0:T(8,128)(2,1)} %copy-done.11, bf16[1024,256]{1,0:T(8,128)(2,1)} %copy-done.12, bf16[256,256]{1,0:T(8,128)(2,1)} %copy-done.42, ...), custom_call_target="tpu_custom_call" | custom-call | tf_op jit(solution)/shard_map/attend_back/pallas_call | solution.py:236
  209.1 2.7 %input_grad.1 = (bf16[512,1024]{1,0:T(8,128)(2,1)S(1)}, bf16[512,1024]{1,0:T(8,128)(2,1)S(1)}) custom-call(s32[1]{0:T(128)} %bitcast.5.me_ref, bf16[1024,384]{1,0:T(8,128)(2,1)S(1)} %copy-done.6, bf16[1024,384]{1,0:T(8,128)(2,1)S(1)} %copy-done, bf16[1024,768]{1,0:T(8,128)(2,1)S(1)} %copy-done.8), custom_call_target="tpu_custom_call" | custom-call | tf_op jit(solution)/shard_map/input_grad/pallas_call | solution.py:828
  211.8 2.1 collective-permute-done.52.refs_10_
  214.0 1.2 collective-permute-start.58
  215.3 3.1 %collective-permute-start.56 = (bf16[384,128]{1,0:T(8,128)(2,1)S(1)}, bf16[384,128]{1,0:T(8,128)(2,1)S(1)}, u32[]{:S(2)}, u32[]{:S(2)}) collective-permute-start(bf16[384,128]{1,0:T(8,128)(2,1)S(1)} %get-tuple-element.960), channel_id=1, source_target_pairs={{0,4},{1,5},{2,6},{3,7},{4,0},{5,1},{6,2},{7,3},{8,12},{9,13},{10,... | collective-permute-start | bytes 294920 | tf_op jit(solution)/shard_map/ppermute | solution.py:880
  219.3 2.2 out_projection_grad.1
  221.7 1.2 collective-permute-done.55.refs_1_
  222.9 3.4 %collective-permute-done.56.refs_2_ = bf16[384,128]{1,0:T(8,128)(2,1)S(1)} collective-permute-done((bf16[384,128]{1,0:T(8,128)(2,1)S(1)}, bf16[384,128]{1,0:T(8,128)(2,1)S(1)}, u32[]{:S(2)}, u32[]{:S(2)}) %collective-permute-start.56) | collective-permute-done | bytes 98336 | tf_op jit(solution)/shard_map/ppermute | solution.py:880
  226.3 1.4 collective-permute-done.58.got_ref
  230.4 3.0 %collective-permute-start.61 = (bf16[384,128]{1,0:T(8,128)(2,1)S(1)}, bf16[384,128]{1,0:T(8,128)(2,1)S(1)}, u32[]{:S(2)}, u32[]{:S(2)}) collective-permute-start(bf16[384,128]{1,0:T(8,128)(2,1)S(1)} %get-tuple-element.989), channel_id=1, source_target_pairs={{0,4},{1,5},{2,6},{3,7},{4,0},{5,1},{6,2},{7,3},{8,12},{9,13},{10,... | collective-permute-start | bytes 294920 | tf_op jit(solution)/shard_map/ppermute | solution.py:880
  234.4 2.1 layer_out.1
  237.5 4.3 %collective-permute-done.61.refs_6_ = bf16[384,128]{1,0:T(8,128)(2,1)S(1)} collective-permute-done((bf16[384,128]{1,0:T(8,128)(2,1)S(1)}, bf16[384,128]{1,0:T(8,128)(2,1)S(1)}, u32[]{:S(2)}, u32[]{:S(2)}) %collective-permute-start.61) | collective-permute-done | bytes 98336 | tf_op jit(solution)/shard_map/ppermute | solution.py:880
  241.9 2.1 cut.1
  245.0 2.7 %collective-permute-start.65 = (bf16[256,128]{1,0:T(8,128)(2,1)}, bf16[256,128]{1,0:T(8,128)(2,1)S(1)}, u32[]{:S(2)}, u32[]{:S(2)}) collective-permute-start(bf16[256,128]{1,0:T(8,128)(2,1)} %get-tuple-element.1013), channel_id=1, source_target_pairs={{0,2},{1,3},{2,4},{3,5},{4,6},{5,7},{6,0},{7,1},{8,10},{9,11},{10,... | collective-permute-start | bytes 196616 | tf_op jit(solution)/shard_map/ppermute | solution.py:880
  247.7 1.8 collective-permute-start.66
  250.1 3.2 %token_grad.1 = bf16[256,1024]{1,0:T(8,128)(2,1)} custom-call(bf16[512,1024]{1,0:T(8,128)(2,1)} %copy-done.20, bf16[512,1024]{1,0:T(8,128)(2,1)} %copy-done.21, bf16[256,1024]{1,0:T(8,128)(2,1)} %copy-done.90, bf16[256,1024]{1,0:T(8,128)(2,1)} %bitcast.31, f32[1,1024]{1,0:T(1,128)} %bitcast.23, f32[256,1024]{1,0:T(8,128)} %copy-done.39), custom_call_target="tpu_custom_call" | custom-call | tf_op jit(solution)/shard_map/token_grad/pallas_call | solution.py:619
  254.7 1.9 collective-permute-done.69.got_ref
  258.1 2.3 finish.1
  (330 shorter events, 52.2 us)
Async XLA Ops:
  7.2 103.9 %all-gather.3.cloned.1.call-start = ((), (), s32[]{:S(2)}) async-start(), calls=%async_computation.2 | async-start | bytes 3244032 | tf_op jit(solution)/shard_map/all_gather | solution.py:941
  9.5 10.1 %collective-permute-start.3 = (bf16[704,128]{1,0:T(8,128)(2,1)}, bf16[704,128]{1,0:T(8,128)(2,1)S(1)}, u32[]{:S(2)}, u32[]{:S(2)}) collective-permute-start(bf16[704,128]{1,0:T(8,128)(2,1)} %get-tuple-element.707.refs_0_), channel_id=1, source_target_pairs={{0,2},{1,3},{2,4},{3,5},{4,6},{5,7},{6,0},{7,1},{8,10},{9,11},{10,... | collective-permute-start | bytes 540680 | tf_op jit(solution)/shard_map/ppermute | solution.py:880
  12.6 7.0 %collective-permute-start.4 = (bf16[704,128]{1,0:T(8,128)(2,1)}, bf16[704,128]{1,0:T(8,128)(2,1)S(1)}, u32[]{:S(2)}, u32[]{:S(2)}) collective-permute-start(bf16[704,128]{1,0:T(8,128)(2,1)} %get-tuple-element.707.refs_0_), channel_id=1, source_target_pairs={{0,1},{1,0},{2,3},{3,2},{4,5},{5,4},{6,7},{7,6},{8,9},{9,8},{10,11... | collective-permute-start | bytes 540680 | tf_op jit(solution)/shard_map/ppermute | solution.py:875
  21.4 10.9 %collective-permute-start.6 = (bf16[1088,128]{1,0:T(8,128)(2,1)S(1)}, bf16[1088,128]{1,0:T(8,128)(2,1)S(1)}, u32[]{:S(2)}, u32[]{:S(2)}) collective-permute-start(bf16[1088,128]{1,0:T(8,128)(2,1)S(1)} %constant_dynamic-update-slice_fusion.refs_0_), channel_id=1, source_target_pairs={{0,2},{1,3},{2,4},{3,5},{4,6},{5,7},{6,0},{7,1},{8,10},{9,11},{10,... | collective-permute-start | bytes 835592 | tf_op jit(solution)/shard_map/ppermute | solution.py:880
  23.1 9.3 %collective-permute-start.7 = (bf16[1088,128]{1,0:T(8,128)(2,1)S(1)}, bf16[1088,128]{1,0:T(8,128)(2,1)S(1)}, u32[]{:S(2)}, u32[]{:S(2)}) collective-permute-start(bf16[1088,128]{1,0:T(8,128)(2,1)S(1)} %constant_dynamic-update-slice_fusion.refs_0_), channel_id=1, source_target_pairs={{0,1},{1,0},{2,3},{3,2},{4,5},{5,4},{6,7},{7,6},{8,9},{9,8},{10,11... | collective-permute-start | bytes 835592 | tf_op jit(solution)/shard_map/ppermute | solution.py:875
  24.3 8.0 %collective-permute-start.5 = (bf16[128,1024]{1,0:T(8,128)(2,1)}, bf16[128,1024]{1,0:T(8,128)(2,1)S(1)}, u32[]{:S(2)}, u32[]{:S(2)}) collective-permute-start(bf16[128,1024]{1,0:T(8,128)(2,1)} %get-tuple-element.558), channel_id=1, source_target_pairs={{0,16},{8,24},{16,0},{24,8},{1,17},{9,25},{17,1},{25,9},{2,18},{10... | collective-permute-start | bytes 786440 | tf_op jit(solution)/shard_map/ppermute | solution.py:847
  33.2 10.4 %collective-permute-start.8 = (bf16[1088,128]{1,0:T(8,128)(2,1)S(1)}, bf16[1088,128]{1,0:T(8,128)(2,1)S(1)}, u32[]{:S(2)}, u32[]{:S(2)}) collective-permute-start(bf16[1088,128]{1,0:T(8,128)(2,1)S(1)} %collective-permute-done.6.refs_1_), channel_id=1, source_target_pairs={{0,2},{1,3},{2,4},{3,5},{4,6},{5,7},{6,0},{7,1},{8,10},{9,11},{10,... | collective-permute-start | bytes 835592 | tf_op jit(solution)/shard_map/ppermute | solution.py:880
  34.7 8.8 %collective-permute-start.9 = (bf16[1088,128]{1,0:T(8,128)(2,1)S(1)}, bf16[1088,128]{1,0:T(8,128)(2,1)S(1)}, u32[]{:S(2)}, u32[]{:S(2)}) collective-permute-start(bf16[1088,128]{1,0:T(8,128)(2,1)S(1)} %collective-permute-done.6.refs_1_), channel_id=1, source_target_pairs={{0,1},{1,0},{2,3},{3,2},{4,5},{5,4},{6,7},{7,6},{8,9},{9,8},{10,11... | collective-permute-start | bytes 835592 | tf_op jit(solution)/shard_map/ppermute | solution.py:875
  36.1 5.1 %collective-permute-start.12 = (bf16[352,128]{1,0:T(8,128)(2,1)}, bf16[352,128]{1,0:T(8,128)(2,1)S(1)}, u32[]{:S(2)}, u32[]{:S(2)}) collective-permute-start(bf16[352,128]{1,0:T(8,128)(2,1)} %get-tuple-element.591), channel_id=1, source_target_pairs={{0,24},{8,16},{16,8},{24,0},{1,25},{9,17},{17,9},{25,1},{2,26},{10... | collective-permute-start | bytes 270344 | tf_op jit(solution)/shard_map/ppermute | solution.py:851
  36.1 6.7 %collective-permute-start.11 = (bf16[352,128]{1,0:T(8,128)(2,1)}, bf16[352,128]{1,0:T(8,128)(2,1)S(1)}, u32[]{:S(2)}, u32[]{:S(2)}) collective-permute-start(bf16[352,128]{1,0:T(8,128)(2,1)} %get-tuple-element.590), channel_id=1, source_target_pairs={{0,16},{8,24},{16,0},{24,8},{1,17},{9,25},{17,1},{25,9},{2,18},{10... | collective-permute-start | bytes 270344 | tf_op jit(solution)/shard_map/ppermute | solution.py:847
  37.4 5.4 %collective-permute-start.10 = (bf16[352,128]{1,0:T(8,128)(2,1)}, bf16[352,128]{1,0:T(8,128)(2,1)S(1)}, u32[]{:S(2)}, u32[]{:S(2)}) collective-permute-start(bf16[352,128]{1,0:T(8,128)(2,1)} %get-tuple-element.589), channel_id=1, source_target_pairs={{0,8},{8,0},{16,24},{24,16},{1,9},{9,1},{17,25},{25,17},{2,10},{10... | collective-permute-start | bytes 270344 | tf_op jit(solution)/shard_map/ppermute | solution.py:843
  43.6 209.8 %reduce-scatter.2.cloned.1.call-start = ((), (), s32[]{:S(2)}) async-start(), calls=%async_computation.1 | async-start | bytes 1622016 | tf_op jit(solution)/shard_map/reduce_scatter | solution.py:993
  43.6 11.1 %collective-permute-start.16 = (bf16[256,1024]{1,0:T(8,128)(2,1)S(1)}, bf16[256,1024]{1,0:T(8,128)(2,1)}, u32[]{:S(2)}, u32[]{:S(2)}) collective-permute-start(bf16[256,1024]{1,0:T(8,128)(2,1)S(1)} %bitcast.32), channel_id=1, source_target_pairs={{0,8},{8,0},{16,24},{24,16},{1,9},{9,1},{17,25},{25,17},{2,10},{10... | collective-permute-start | bytes 1572872 | tf_op jit(solution)/shard_map/ppermute | solution.py:843
  43.8 10.9 %collective-permute-start.14 = (bf16[1088,128]{1,0:T(8,128)(2,1)S(1)}, bf16[1088,128]{1,0:T(8,128)(2,1)S(1)}, u32[]{:S(2)}, u32[]{:S(2)}) collective-permute-start(bf16[1088,128]{1,0:T(8,128)(2,1)S(1)} %collective-permute-done.8.refs_2_), channel_id=1, source_target_pairs={{0,2},{1,3},{2,4},{3,5},{4,6},{5,7},{6,0},{7,1},{8,10},{9,11},{10,... | collective-permute-start | bytes 835592 | tf_op jit(solution)/shard_map/ppermute | solution.py:880
  44.2 10.5 %collective-permute-start.15 = (bf16[1088,128]{1,0:T(8,128)(2,1)S(1)}, bf16[1088,128]{1,0:T(8,128)(2,1)S(1)}, u32[]{:S(2)}, u32[]{:S(2)}) collective-permute-start(bf16[1088,128]{1,0:T(8,128)(2,1)S(1)} %collective-permute-done.8.refs_2_), channel_id=1, source_target_pairs={{0,1},{1,0},{2,3},{3,2},{4,5},{5,4},{6,7},{7,6},{8,9},{9,8},{10,11... | collective-permute-start | bytes 835592 | tf_op jit(solution)/shard_map/ppermute | solution.py:875
  45.1 8.2 %collective-permute-start.13 = (bf16[128,1024]{1,0:T(8,128)(2,1)}, bf16[128,1024]{1,0:T(8,128)(2,1)S(1)}, u32[]{:S(2)}, u32[]{:S(2)}) collective-permute-start(bf16[128,1024]{1,0:T(8,128)(2,1)} %get-tuple-element.595), channel_id=1, source_target_pairs={{0,16},{8,24},{16,0},{24,8},{1,17},{9,25},{17,1},{25,9},{2,18},{10... | collective-permute-start | bytes 786440 | tf_op jit(solution)/shard_map/ppermute | solution.py:847
  54.7 5.7 %collective-permute-start.19 = (bf16[256,256]{1,0:T(8,128)(2,1)S(1)}, bf16[256,256]{1,0:T(8,128)(2,1)S(1)}, u32[]{:S(2)}, u32[]{:S(2)}) collective-permute-start(bf16[256,256]{1,0:T(8,128)(2,1)S(1)} %get-tuple-element.614), channel_id=1, source_target_pairs={{0,24},{8,16},{16,8},{24,0},{1,25},{9,17},{17,9},{25,1},{2,26},{10... | collective-permute-start | bytes 393224 | tf_op jit(solution)/shard_map/ppermute | solution.py:851
  54.7 7.8 %collective-permute-start.18 = (bf16[256,256]{1,0:T(8,128)(2,1)S(1)}, bf16[256,256]{1,0:T(8,128)(2,1)S(1)}, u32[]{:S(2)}, u32[]{:S(2)}) collective-permute-start(bf16[256,256]{1,0:T(8,128)(2,1)S(1)} %get-tuple-element.613), channel_id=1, source_target_pairs={{0,16},{8,24},{16,0},{24,8},{1,17},{9,25},{17,1},{25,9},{2,18},{10... | collective-permute-start | bytes 393224 | tf_op jit(solution)/shard_map/ppermute | solution.py:847
  55.8 6.8 %collective-permute-start.17 = (bf16[256,256]{1,0:T(8,128)(2,1)S(1)}, bf16[256,256]{1,0:T(8,128)(2,1)S(1)}, u32[]{:S(2)}, u32[]{:S(2)}) collective-permute-start(bf16[256,256]{1,0:T(8,128)(2,1)S(1)} %get-tuple-element.612), channel_id=1, source_target_pairs={{0,8},{8,0},{16,24},{24,16},{1,9},{9,1},{17,25},{25,17},{2,10},{10... | collective-permute-start | bytes 393224 | tf_op jit(solution)/shard_map/ppermute | solution.py:843
  56.6 8.6 %collective-permute-start.20 = (bf16[1088,128]{1,0:T(8,128)(2,1)S(1)}, bf16[1088,128]{1,0:T(8,128)(2,1)S(1)}, u32[]{:S(2)}, u32[]{:S(2)}) collective-permute-start(bf16[1088,128]{1,0:T(8,128)(2,1)S(1)} %collective-permute-done.14.refs_3_), channel_id=1, source_target_pairs={{0,1},{1,0},{2,3},{3,2},{4,5},{5,4},{6,7},{7,6},{8,9},{9,8},{10,11... | collective-permute-start | bytes 835592 | tf_op jit(solution)/shard_map/ppermute | solution.py:875
  57.5 5.1 %collective-permute-start.21 = (bf16[256,1024]{1,0:T(8,128)(2,1)S(1)}, bf16[256,1024]{1,0:T(8,128)(2,1)S(1)}, u32[]{:S(2)}, u32[]{:S(2)}) collective-permute-start(bf16[256,1024]{1,0:T(8,128)(2,1)S(1)} %pad_maximum_fusion.3), channel_id=1, source_target_pairs={{0,8},{8,0},{16,24},{24,16},{1,9},{9,1},{17,25},{25,17},{2,10},{10... | collective-permute-start | bytes 1572872 | tf_op jit(solution)/shard_map/ppermute | solution.py:843
  65.1 9.4 %collective-permute-start.25 = (bf16[256,1024]{1,0:T(8,128)(2,1)S(1)}, bf16[256,1024]{1,0:T(8,128)(2,1)S(1)}, u32[]{:S(2)}, u32[]{:S(2)}) collective-permute-start(bf16[256,1024]{1,0:T(8,128)(2,1)S(1)} %bitcast.18), channel_id=1, source_target_pairs={{0,8},{8,0},{16,24},{24,16},{1,9},{9,1},{17,25},{25,17},{2,10},{10... | collective-permute-start | bytes 1572872 | tf_op jit(solution)/shard_map/ppermute | solution.py:843
  65.2 9.4 %collective-permute-start.24 = (bf16[128,1024]{1,0:T(8,128)(2,1)S(1)}, bf16[128,1024]{1,0:T(8,128)(2,1)S(1)}, u32[]{:S(2)}, u32[]{:S(2)}) collective-permute-start(bf16[128,1024]{1,0:T(8,128)(2,1)S(1)} %get-tuple-element.640), channel_id=1, source_target_pairs={{0,16},{8,24},{16,0},{24,8},{1,17},{9,25},{17,1},{25,9},{2,18},{10... | collective-permute-start | bytes 786440 | tf_op jit(solution)/shard_map/ppermute | solution.py:847
  65.9 8.6 %collective-permute-start.22 = (bf16[704,128]{1,0:T(8,128)(2,1)S(1)}, bf16[704,128]{1,0:T(8,128)(2,1)S(1)}, u32[]{:S(2)}, u32[]{:S(2)}) collective-permute-start(bf16[704,128]{1,0:T(8,128)(2,1)S(1)} %copy-done.64), channel_id=1, source_target_pairs={{0,2},{1,3},{2,4},{3,5},{4,6},{5,7},{6,0},{7,1},{8,10},{9,11},{10,... | collective-permute-start | bytes 540680 | tf_op jit(solution)/shard_map/ppermute | solution.py:880
  65.9 8.6 %collective-permute-start.23 = (bf16[704,128]{1,0:T(8,128)(2,1)S(1)}, bf16[704,128]{1,0:T(8,128)(2,1)S(1)}, u32[]{:S(2)}, u32[]{:S(2)}) collective-permute-start(bf16[704,128]{1,0:T(8,128)(2,1)S(1)} %copy-done.64), channel_id=1, source_target_pairs={{0,1},{1,0},{2,3},{3,2},{4,5},{5,4},{6,7},{7,6},{8,9},{9,8},{10,11... | collective-permute-start | bytes 540680 | tf_op jit(solution)/shard_map/ppermute | solution.py:875
  74.5 20.0 %collective-permute-start.29 = (bf16[256,1024]{1,0:T(8,128)(2,1)S(1)}, bf16[256,1024]{1,0:T(8,128)(2,1)S(1)}, u32[]{:S(2)}, u32[]{:S(2)}) collective-permute-start(bf16[256,1024]{1,0:T(8,128)(2,1)S(1)} %get-tuple-element.837.wo0.w0), channel_id=1, source_target_pairs={{0,8},{8,0},{16,24},{24,16},{1,9},{9,1},{17,25},{25,17},{2,10},{10... | collective-permute-start | bytes 1572872 | tf_op jit(solution)/shard_map/ppermute | solution.py:843
  74.6 20.0 %collective-permute-start.30 = (bf16[256,1024]{1,0:T(8,128)(2,1)S(1)}, bf16[256,1024]{1,0:T(8,128)(2,1)S(1)}, u32[]{:S(2)}, u32[]{:S(2)}) collective-permute-start(bf16[256,1024]{1,0:T(8,128)(2,1)S(1)} %get-tuple-element.837.wo0.w0), channel_id=1, source_target_pairs={{0,16},{8,24},{16,0},{24,8},{1,17},{9,25},{17,1},{25,9},{2,18},{10... | collective-permute-start | bytes 1572872 | tf_op jit(solution)/shard_map/ppermute | solution.py:847
  75.9 18.6 %collective-permute-start.28 = (bf16[128,1024]{1,0:T(8,128)(2,1)S(1)}, bf16[128,1024]{1,0:T(8,128)(2,1)S(1)}, u32[]{:S(2)}, u32[]{:S(2)}) collective-permute-start(bf16[128,1024]{1,0:T(8,128)(2,1)S(1)} %get-tuple-element.671), channel_id=1, source_target_pairs={{0,16},{8,24},{16,0},{24,8},{1,17},{9,25},{17,1},{25,9},{2,18},{10... | collective-permute-start | bytes 786440 | tf_op jit(solution)/shard_map/ppermute | solution.py:847
  76.7 12.7 %collective-permute-start.26 = (bf16[704,128]{1,0:T(8,128)(2,1)S(1)}, bf16[704,128]{1,0:T(8,128)(2,1)S(1)}, u32[]{:S(2)}, u32[]{:S(2)}) collective-permute-start(bf16[704,128]{1,0:T(8,128)(2,1)S(1)} %collective-permute-done.22.refs_2_), channel_id=1, source_target_pairs={{0,2},{1,3},{2,4},{3,5},{4,6},{5,7},{6,0},{7,1},{8,10},{9,11},{10,... | collective-permute-start | bytes 540680 | tf_op jit(solution)/shard_map/ppermute | solution.py:880
  76.9 12.5 %collective-permute-start.27 = (bf16[704,128]{1,0:T(8,128)(2,1)S(1)}, bf16[704,128]{1,0:T(8,128)(2,1)S(1)}, u32[]{:S(2)}, u32[]{:S(2)}) collective-permute-start(bf16[704,128]{1,0:T(8,128)(2,1)S(1)} %collective-permute-done.22.refs_2_), channel_id=1, source_target_pairs={{0,1},{1,0},{2,3},{3,2},{4,5},{5,4},{6,7},{7,6},{8,9},{9,8},{10,11... | collective-permute-start | bytes 540680 | tf_op jit(solution)/shard_map/ppermute | solution.py:875
  94.7 10.9 %collective-permute-start.31 = (bf16[256,1024]{1,0:T(8,128)(2,1)S(1)}, bf16[256,1024]{1,0:T(8,128)(2,1)S(1)}, u32[]{:S(2)}, u32[]{:S(2)}) collective-permute-start(bf16[256,1024]{1,0:T(8,128)(2,1)S(1)} %pad_maximum_fusion.4), channel_id=1, source_target_pairs={{0,8},{8,0},{16,24},{24,16},{1,9},{9,1},{17,25},{25,17},{2,10},{10... | collective-permute-start | bytes 1572872 | tf_op jit(solution)/shard_map/ppermute | solution.py:843
  94.7 10.9 %collective-permute-start.34 = (bf16[1024,256]{1,0:T(8,128)(2,1)S(1)}, bf16[1024,256]{1,0:T(8,128)(2,1)S(1)}, u32[]{:S(2)}, u32[]{:S(2)}) collective-permute-start(bf16[1024,256]{1,0:T(8,128)(2,1)S(1)} %get-tuple-element.967.a0.act_ref), channel_id=1, source_target_pairs={{0,8},{8,0},{16,24},{24,16},{1,9},{9,1},{17,25},{25,17},{2,10},{10... | collective-permute-start | bytes 1572872 | tf_op jit(solution)/shard_map/ppermute | solution.py:843
  95.2 13.9 %collective-permute-start.35 = (bf16[1024,256]{1,0:T(8,128)(2,1)S(1)}, bf16[1024,256]{1,0:T(8,128)(2,1)S(1)}, u32[]{:S(2)}, u32[]{:S(2)}) collective-permute-start(bf16[1024,256]{1,0:T(8,128)(2,1)S(1)} %get-tuple-element.967.a0.act_ref), channel_id=1, source_target_pairs={{0,16},{8,24},{16,0},{24,8},{1,17},{9,25},{17,1},{25,9},{2,18},{10... | collective-permute-start | bytes 1572872 | tf_op jit(solution)/shard_map/ppermute | solution.py:847
  96.5 9.1 %collective-permute-start.32 = (bf16[256,1024]{1,0:T(8,128)(2,1)S(1)}, bf16[256,1024]{1,0:T(8,128)(2,1)S(1)}, u32[]{:S(2)}, u32[]{:S(2)}) collective-permute-start(bf16[256,1024]{1,0:T(8,128)(2,1)S(1)} %collective-permute-done.30.wo2.w2), channel_id=1, source_target_pairs={{0,8},{8,0},{16,24},{24,16},{1,9},{9,1},{17,25},{25,17},{2,10},{10... | collective-permute-start | bytes 1572872 | tf_op jit(solution)/shard_map/ppermute | solution.py:843
  96.5 7.0 %collective-permute-start.33 = (bf16[704,128]{1,0:T(8,128)(2,1)S(1)}, bf16[704,128]{1,0:T(8,128)(2,1)S(1)}, u32[]{:S(2)}, u32[]{:S(2)}) collective-permute-start(bf16[704,128]{1,0:T(8,128)(2,1)S(1)} %collective-permute-done.26.refs_3_), channel_id=1, source_target_pairs={{0,1},{1,0},{2,3},{3,2},{4,5},{5,4},{6,7},{7,6},{8,9},{9,8},{10,11... | collective-permute-start | bytes 540680 | tf_op jit(solution)/shard_map/ppermute | solution.py:875
  138.1 15.0 %collective-permute-start.38 = (bf16[256,1024]{1,0:T(8,128)(2,1)}, bf16[256,1024]{1,0:T(8,128)(2,1)}, u32[]{:S(2)}, u32[]{:S(2)}) collective-permute-start(bf16[256,1024]{1,0:T(8,128)(2,1)} %lower.3), channel_id=1, source_target_pairs={{0,16},{8,24},{16,0},{24,8},{1,17},{9,25},{17,1},{25,9},{2,18},{10... | collective-permute-start | bytes 1572872 | tf_op jit(solution)/shard_map/ppermute | solution.py:847
  153.1 9.2 %collective-permute-start.40 = (bf16[512,1024]{1,0:T(8,128)(2,1)}, bf16[512,1024]{1,0:T(8,128)(2,1)S(1)}, u32[]{:S(2)}, u32[]{:S(2)}) collective-permute-start(bf16[512,1024]{1,0:T(8,128)(2,1)} %get-tuple-element.833), channel_id=1, source_target_pairs={{0,8},{8,0},{16,24},{24,16},{1,9},{9,1},{17,25},{25,17},{2,10},{10... | collective-permute-start | bytes 3145736 | tf_op jit(solution)/shard_map/ppermute | solution.py:843
  153.2 10.8 %collective-permute-start.39 = (bf16[1408,128]{1,0:T(8,128)(2,1)S(1)}, bf16[1408,128]{1,0:T(8,128)(2,1)S(1)}, u32[]{:S(2)}, u32[]{:S(2)}) collective-permute-start(bf16[1408,128]{1,0:T(8,128)(2,1)S(1)} %copy-done.95), channel_id=1, source_target_pairs={{0,1},{1,0},{2,3},{3,2},{4,5},{5,4},{6,7},{7,6},{8,9},{9,8},{10,11... | collective-permute-start | bytes 1081352 | tf_op jit(solution)/shard_map/ppermute | solution.py:875
  164.0 10.0 %collective-permute-start.41 = (bf16[1408,128]{1,0:T(8,128)(2,1)S(1)}, bf16[1408,128]{1,0:T(8,128)(2,1)S(1)}, u32[]{:S(2)}, u32[]{:S(2)}) collective-permute-start(bf16[1408,128]{1,0:T(8,128)(2,1)S(1)} %copy-done.94), channel_id=1, source_target_pairs={{0,1},{1,0},{2,3},{3,2},{4,5},{5,4},{6,7},{7,6},{8,9},{9,8},{10,11... | collective-permute-start | bytes 1081352 | tf_op jit(solution)/shard_map/ppermute | solution.py:875
  164.9 12.0 %collective-permute-start.45 = (bf16[1408,128]{1,0:T(8,128)(2,1)S(1)}, bf16[1408,128]{1,0:T(8,128)(2,1)S(1)}, u32[]{:S(2)}, u32[]{:S(2)}) collective-permute-start(bf16[1408,128]{1,0:T(8,128)(2,1)S(1)} %total.3), channel_id=1, source_target_pairs={{0,2},{1,3},{2,4},{3,5},{4,6},{5,7},{6,0},{7,1},{8,10},{9,11},{10,... | collective-permute-start | bytes 1081352 | tf_op jit(solution)/shard_map/ppermute | solution.py:880
  165.2 6.3 %collective-permute-start.43 = (bf16[256,256]{1,0:T(8,128)(2,1)S(1)}, bf16[256,256]{1,0:T(8,128)(2,1)S(1)}, u32[]{:S(2)}, u32[]{:S(2)}) collective-permute-start(bf16[256,256]{1,0:T(8,128)(2,1)S(1)} %get-tuple-element.874), channel_id=1, source_target_pairs={{0,16},{8,24},{16,0},{24,8},{1,17},{9,25},{17,1},{25,9},{2,18},{10... | collective-permute-start | bytes 393224 | tf_op jit(solution)/shard_map/ppermute | solution.py:847
  166.0 7.6 %collective-permute-start.44 = (bf16[256,256]{1,0:T(8,128)(2,1)S(1)}, bf16[256,256]{1,0:T(8,128)(2,1)S(1)}, u32[]{:S(2)}, u32[]{:S(2)}) collective-permute-start(bf16[256,256]{1,0:T(8,128)(2,1)S(1)} %get-tuple-element.875), channel_id=1, source_target_pairs={{0,24},{8,16},{16,8},{24,0},{1,25},{9,17},{17,9},{25,1},{2,26},{10... | collective-permute-start | bytes 393224 | tf_op jit(solution)/shard_map/ppermute | solution.py:851
  176.9 14.3 %collective-permute-start.47 = (bf16[256,1024]{1,0:T(8,128)(2,1)}, bf16[256,1024]{1,0:T(8,128)(2,1)S(1)}, u32[]{:S(2)}, u32[]{:S(2)}) collective-permute-start(bf16[256,1024]{1,0:T(8,128)(2,1)} %get-tuple-element.968.d0), channel_id=1, source_target_pairs={{0,8},{8,0},{16,24},{24,16},{1,9},{9,1},{17,25},{25,17},{2,10},{10... | collective-permute-start | bytes 1572872 | tf_op jit(solution)/shard_map/ppermute | solution.py:843
  176.9 15.1 %collective-permute-start.48 = (bf16[256,1024]{1,0:T(8,128)(2,1)}, bf16[256,1024]{1,0:T(8,128)(2,1)}, u32[]{:S(2)}, u32[]{:S(2)}) collective-permute-start(bf16[256,1024]{1,0:T(8,128)(2,1)} %get-tuple-element.968.d0), channel_id=1, source_target_pairs={{0,16},{8,24},{16,0},{24,8},{1,17},{9,25},{17,1},{25,9},{2,18},{10... | collective-permute-start | bytes 1572872 | tf_op jit(solution)/shard_map/ppermute | solution.py:847
  177.7 12.4 %collective-permute-start.46 = (bf16[1408,128]{1,0:T(8,128)(2,1)S(1)}, bf16[1408,128]{1,0:T(8,128)(2,1)S(1)}, u32[]{:S(2)}, u32[]{:S(2)}) collective-permute-start(bf16[1408,128]{1,0:T(8,128)(2,1)S(1)} %copy-done.93), channel_id=1, source_target_pairs={{0,1},{1,0},{2,3},{3,2},{4,5},{5,4},{6,7},{7,6},{8,9},{9,8},{10,11... | collective-permute-start | bytes 1081352 | tf_op jit(solution)/shard_map/ppermute | solution.py:875
  178.6 12.5 %collective-permute-start.49 = (bf16[1408,128]{1,0:T(8,128)(2,1)S(1)}, bf16[1408,128]{1,0:T(8,128)(2,1)S(1)}, u32[]{:S(2)}, u32[]{:S(2)}) collective-permute-start(bf16[1408,128]{1,0:T(8,128)(2,1)S(1)} %total.4), channel_id=1, source_target_pairs={{0,2},{1,3},{2,4},{3,5},{4,6},{5,7},{6,0},{7,1},{8,10},{9,11},{10,... | collective-permute-start | bytes 1081352 | tf_op jit(solution)/shard_map/ppermute | solution.py:880
  192.0 21.9 %collective-permute-start.53 = (bf16[2944,128]{1,0:T(8,128)(2,1)}, bf16[2944,128]{1,0:T(8,128)(2,1)S(1)}, u32[]{:S(2)}, u32[]{:S(2)}) collective-permute-start(bf16[2944,128]{1,0:T(8,128)(2,1)} %get-tuple-element.940), channel_id=1, source_target_pairs={{0,1},{1,0},{2,3},{3,2},{4,5},{5,4},{6,7},{7,6},{8,9},{9,8},{10,11... | collective-permute-start | bytes 2261000 | tf_op jit(solution)/shard_map/ppermute | solution.py:875
  193.1 20.7 %collective-permute-start.50 = (bf16[256,1024]{1,0:T(8,128)(2,1)}, bf16[256,1024]{1,0:T(8,128)(2,1)}, u32[]{:S(2)}, u32[]{:S(2)}) collective-permute-start(bf16[256,1024]{1,0:T(8,128)(2,1)} %collective-permute-done.48.d2), channel_id=1, source_target_pairs={{0,8},{8,0},{16,24},{24,16},{1,9},{9,1},{17,25},{25,17},{2,10},{10... | collective-permute-start | bytes 1572872 | tf_op jit(solution)/shard_map/ppermute | solution.py:843
  193.1 20.7 %collective-permute-start.51 = (bf16[256,1024]{1,0:T(8,128)(2,1)}, bf16[256,1024]{1,0:T(8,128)(2,1)}, u32[]{:S(2)}, u32[]{:S(2)}) collective-permute-start(bf16[256,1024]{1,0:T(8,128)(2,1)} %lower.4), channel_id=1, source_target_pairs={{0,16},{8,24},{16,0},{24,8},{1,17},{9,25},{17,1},{25,9},{2,18},{10... | collective-permute-start | bytes 1572872 | tf_op jit(solution)/shard_map/ppermute | solution.py:847
  195.2 18.6 %collective-permute-start.52 = (bf16[1408,128]{1,0:T(8,128)(2,1)}, bf16[1408,128]{1,0:T(8,128)(2,1)}, u32[]{:S(2)}, u32[]{:S(2)}) collective-permute-start(bf16[1408,128]{1,0:T(8,128)(2,1)} %total.5), channel_id=1, source_target_pairs={{0,2},{1,3},{2,4},{3,5},{4,6},{5,7},{6,0},{7,1},{8,10},{9,11},{10,... | collective-permute-start | bytes 1081352 | tf_op jit(solution)/shard_map/ppermute | solution.py:880
  196.2 15.6 %collective-permute-start.54 = (bf16[512,128]{1,0:T(8,128)(2,1)S(1)}, bf16[512,128]{1,0:T(8,128)(2,1)S(1)}, u32[]{:S(2)}, u32[]{:S(2)}) collective-permute-start(bf16[512,128]{1,0:T(8,128)(2,1)S(1)} %constant_dynamic-slice_fusion.4), channel_id=1, source_target_pairs={{0,16},{8,24},{16,0},{24,8},{1,17},{9,25},{17,1},{25,9},{2,18},{10... | collective-permute-start | bytes 393224 | tf_op jit(solution)/shard_map/ppermute | solution.py:847
  213.9 7.7 %collective-permute-start.59 = (bf16[512,1024]{1,0:T(8,128)(2,1)S(1)}, bf16[512,1024]{1,0:T(8,128)(2,1)S(1)}, u32[]{:S(2)}, u32[]{:S(2)}) collective-permute-start(bf16[512,1024]{1,0:T(8,128)(2,1)S(1)} %get-tuple-element.966), channel_id=1, source_target_pairs={{0,8},{8,0},{16,24},{24,16},{1,9},{9,1},{17,25},{25,17},{2,10},{10... | collective-permute-start | bytes 3145736 | tf_op jit(solution)/shard_map/ppermute | solution.py:843
  214.0 13.7 %collective-permute-start.58 = (bf16[1536,128]{1,0:T(8,128)(2,1)S(1)}, bf16[1536,128]{1,0:T(8,128)(2,1)S(1)}, u32[]{:S(2)}, u32[]{:S(2)}) collective-permute-start(bf16[1536,128]{1,0:T(8,128)(2,1)S(1)} %copy-done.92), channel_id=1, source_target_pairs={{0,1},{1,0},{2,3},{3,2},{4,5},{5,4},{6,7},{7,6},{8,9},{9,8},{10,11... | collective-permute-start | bytes 1179656 | tf_op jit(solution)/shard_map/ppermute | solution.py:875
  215.3 7.6 %collective-permute-start.55 = (bf16[384,128]{1,0:T(8,128)(2,1)S(1)}, bf16[384,128]{1,0:T(8,128)(2,1)S(1)}, u32[]{:S(2)}, u32[]{:S(2)}) collective-permute-start(bf16[384,128]{1,0:T(8,128)(2,1)S(1)} %get-tuple-element.959), channel_id=1, source_target_pairs={{0,2},{1,3},{2,4},{3,5},{4,6},{5,7},{6,0},{7,1},{8,10},{9,11},{10,... | collective-permute-start | bytes 294920 | tf_op jit(solution)/shard_map/ppermute | solution.py:880
  215.3 10.9 %collective-permute-start.56 = (bf16[384,128]{1,0:T(8,128)(2,1)S(1)}, bf16[384,128]{1,0:T(8,128)(2,1)S(1)}, u32[]{:S(2)}, u32[]{:S(2)}) collective-permute-start(bf16[384,128]{1,0:T(8,128)(2,1)S(1)} %get-tuple-element.960), channel_id=1, source_target_pairs={{0,4},{1,5},{2,6},{3,7},{4,0},{5,1},{6,2},{7,3},{8,12},{9,13},{10,... | collective-permute-start | bytes 294920 | tf_op jit(solution)/shard_map/ppermute | solution.py:880
  218.4 7.8 %collective-permute-start.57 = (bf16[384,128]{1,0:T(8,128)(2,1)S(1)}, bf16[384,128]{1,0:T(8,128)(2,1)S(1)}, u32[]{:S(2)}, u32[]{:S(2)}) collective-permute-start(bf16[384,128]{1,0:T(8,128)(2,1)S(1)} %get-tuple-element.961), channel_id=1, source_target_pairs={{0,6},{1,7},{2,0},{3,1},{4,2},{5,3},{6,4},{7,5},{8,14},{9,15},{10,... | collective-permute-start | bytes 294920 | tf_op jit(solution)/shard_map/ppermute | solution.py:880
  227.6 14.2 %collective-permute-start.63 = (bf16[256,1024]{1,0:T(8,128)(2,1)S(1)}, bf16[256,1024]{1,0:T(8,128)(2,1)S(1)}, u32[]{:S(2)}, u32[]{:S(2)}) collective-permute-start(bf16[256,1024]{1,0:T(8,128)(2,1)S(1)} %lower.5), channel_id=1, source_target_pairs={{0,16},{8,24},{16,0},{24,8},{1,17},{9,25},{17,1},{25,9},{2,18},{10... | collective-permute-start | bytes 1572872 | tf_op jit(solution)/shard_map/ppermute | solution.py:847
  228.6 7.9 %collective-permute-start.64 = (bf16[1024,128]{1,0:T(8,128)(2,1)S(1)}, bf16[1024,128]{1,0:T(8,128)(2,1)S(1)}, u32[]{:S(2)}, u32[]{:S(2)}) collective-permute-start(bf16[1024,128]{1,0:T(8,128)(2,1)S(1)} %get-tuple-element.997), channel_id=1, source_target_pairs={{0,1},{1,0},{2,3},{3,2},{4,5},{5,4},{6,7},{7,6},{8,9},{9,8},{10,11... | collective-permute-start | bytes 786440 | tf_op jit(solution)/shard_map/ppermute | solution.py:875
  229.6 7.9 %collective-permute-start.60 = (bf16[384,128]{1,0:T(8,128)(2,1)S(1)}, bf16[384,128]{1,0:T(8,128)(2,1)S(1)}, u32[]{:S(2)}, u32[]{:S(2)}) collective-permute-start(bf16[384,128]{1,0:T(8,128)(2,1)S(1)} %get-tuple-element.988), channel_id=1, source_target_pairs={{0,2},{1,3},{2,4},{3,5},{4,6},{5,7},{6,0},{7,1},{8,10},{9,11},{10,... | collective-permute-start | bytes 294920 | tf_op jit(solution)/shard_map/ppermute | solution.py:880
  230.4 11.5 %collective-permute-start.61 = (bf16[384,128]{1,0:T(8,128)(2,1)S(1)}, bf16[384,128]{1,0:T(8,128)(2,1)S(1)}, u32[]{:S(2)}, u32[]{:S(2)}) collective-permute-start(bf16[384,128]{1,0:T(8,128)(2,1)S(1)} %get-tuple-element.989), channel_id=1, source_target_pairs={{0,4},{1,5},{2,6},{3,7},{4,0},{5,1},{6,2},{7,3},{8,12},{9,13},{10,... | collective-permute-start | bytes 294920 | tf_op jit(solution)/shard_map/ppermute | solution.py:880
  233.3 8.5 %collective-permute-start.62 = (bf16[384,128]{1,0:T(8,128)(2,1)S(1)}, bf16[384,128]{1,0:T(8,128)(2,1)S(1)}, u32[]{:S(2)}, u32[]{:S(2)}) collective-permute-start(bf16[384,128]{1,0:T(8,128)(2,1)S(1)} %get-tuple-element.990), channel_id=1, source_target_pairs={{0,6},{1,7},{2,0},{3,1},{4,2},{5,3},{6,4},{7,5},{8,14},{9,15},{10,... | collective-permute-start | bytes 294920 | tf_op jit(solution)/shard_map/ppermute | solution.py:880
  244.0 10.7 %collective-permute-start.68 = (bf16[1600,128]{1,0:T(8,128)(2,1)}, bf16[1600,128]{1,0:T(8,128)(2,1)S(1)}, u32[]{:S(2)}, u32[]{:S(2)}) collective-permute-start(bf16[1600,128]{1,0:T(8,128)(2,1)} %get-tuple-element.1030), channel_id=1, source_target_pairs={{0,16},{8,24},{16,0},{24,8},{1,17},{9,25},{17,1},{25,9},{2,18},{10... | collective-permute-start | bytes 1228808 | tf_op jit(solution)/shard_map/ppermute | solution.py:847
  245.0 8.3 %collective-permute-start.65 = (bf16[256,128]{1,0:T(8,128)(2,1)}, bf16[256,128]{1,0:T(8,128)(2,1)S(1)}, u32[]{:S(2)}, u32[]{:S(2)}) collective-permute-start(bf16[256,128]{1,0:T(8,128)(2,1)} %get-tuple-element.1013), channel_id=1, source_target_pairs={{0,2},{1,3},{2,4},{3,5},{4,6},{5,7},{6,0},{7,1},{8,10},{9,11},{10,... | collective-permute-start | bytes 196616 | tf_op jit(solution)/shard_map/ppermute | solution.py:880
  247.7 6.4 %collective-permute-start.66 = (bf16[256,128]{1,0:T(8,128)(2,1)}, bf16[256,128]{1,0:T(8,128)(2,1)}, u32[]{:S(2)}, u32[]{:S(2)}) collective-permute-start(bf16[256,128]{1,0:T(8,128)(2,1)} %get-tuple-element.1014), channel_id=1, source_target_pairs={{0,4},{1,5},{2,6},{3,7},{4,0},{5,1},{6,2},{7,3},{8,12},{9,13},{10,... | collective-permute-start | bytes 196616 | tf_op jit(solution)/shard_map/ppermute | solution.py:880
  (104 other events, 808.8 us)
Sparse Core Ops, SparseCore 0:
  43.7 59.9 all-gather.2
  179.1 70.8 reduce-scatter.1

commit v3 on v1

--- a/solution.py
+++ b/solution.py
@@ -919,9 +919,11 @@
     s.gate, s.up = gate_weight, up_weight
     s.fence()
     s.cols = exchange_rel(s.cols)
-    s.ry = [to_y(s.r[0])]
-    s.r.append(to_z(s.r[0]))
-    s.fence()
+    down = after(s.r[0], s.cols[1])
+    down_near, down_next = to_y(down), to_z(down)
+    s.fence()
+    s.ry = [down_near]
+    s.r.append(down_next)
     s.a = [jnp.concatenate([*s.cols, s.orows])]
     del s.cols, s.orows
     s.tok_far[0] = to_chip(s.tok_far[0])

time: 269 us -> 268 us (level)
  waiting for transfers between devices: 71.3 us -> 62.2 us
  starting transfers between devices: 56.5 us -> 61.8 us
    ppermute x14, starting transfers between devices: 14.6 us -> 18.8 us  [to_y(): return lax.ppermute(value, 'dp', [(i, i ^ 1) for i in range(dp)])]
    ppermute x16, waiting for transfers between devices: 26.9 us -> 22.7 us  [to_chip(): return lax.ppermute(value, 'seq', [(i, i ^ 2) for i in range(SEQ)])]
  transfers between devices with their start and end apart: 72 -> 72, of which waited for: 32 -> 31; matrix products, arithmetic and copies ran while one was open for 4% -> 5% of each run, Pallas kernels for 26% -> 26%
where the time goes in v3:
time: 268 us; the launch traced here: 265 us
  Pallas kernels  98.1 us (37%)
  waiting for transfers between devices  62.2 us (23%)
  starting transfers between devices  61.8 us (23%)
  local copies, waits for them, and re-layouts  19.3 us (7%)
  between operations  15.3 us (6%)
  other arithmetic  8.06 us (3%)
    ppermute x16, waiting for transfers between devices, to_chip(): return lax.ppermute(value, 'seq', [(i, i ^ 2) for i in range(SEQ)])  22.7 us
    pallas_call x2, Pallas kernels, attend_back_call(): pl.pallas_call(functools.partial(attend_back_kernel, dp, pieces), name='a...  21.9 us
    ppermute x18, starting transfers between devices, to_z(): lax.ppermute(value, 'dp', [(i, (i + 2 * hops) % dp) for i in range(dp)])  21.2 us
    pallas_call x1, Pallas kernels, ffn_call(): pl.pallas_call(ffn_kernel, name='ffn', grid_spec=pltpu.PrefetchScalarGrid...  21.1 us
    ppermute x14, starting transfers between devices, to_y(): return lax.ppermute(value, 'dp', [(i, i ^ 1) for i in range(dp)])  18.8 us
    ppermute x18, waiting for transfers between devices, to_z(): lax.ppermute(value, 'dp', [(i, (i + 2 * hops) % dp) for i in range(dp)])  18.2 us
    ppermute x16, starting transfers between devices, to_chip(): return lax.ppermute(value, 'seq', [(i, i ^ 2) for i in range(SEQ)])  17.4 us
    unnamed x202, local copies, waits for them, and re-layouts  16.3 us
  transfers between devices with their start and end apart: 72, of which 31 were waited for; matrix products, arithmetic and copies ran while one was open for 5% of the time, Pallas kernels for 26%

profile of v3, /device:TPU:0, one launch (start us, length us, event | category | flops | bytes accessed | tf_op | source)
XLA Modules:
  0.0 264.8 jit_solution(3848749839751666363)
XLA Ops:
  7.2 2.3 pack_attn.1
  10.0 2.6 collective-permute-start.1
  12.7 1.9 collective-permute-start.3
  14.6 1.5 collective-permute-start.5
  18.4 1.6 collective-permute-start.6
  20.1 1.5 collective-permute-start.7
  22.6 3.1 %fusion = (f32[1024,32]{1,0:T(8,128)}, f32[1024,32]{1,0:T(8,128)}, f32[1024,32]{1,0:T(8,128)}) fusion(f32[32]{0:T(128)S(1)} %multiply_exponential_fusion, f32[1024]{0:T(1024)S(1)} %iota_convert_fusion), kind=kLoop, calls=%fused_computation.8 | loop fusion | flops 65536 | bytes 397440 | tf_op jit(solution)/shard_map/neg | solution.py:886
  26.3 2.2 pack_ffn.1
  30.6 1.6 collective-permute-start.8
  34.5 3.4 %pad_maximum_fusion = (f32[1024,128]{1,0:T(8,128)S(1)}, f32[1024,128]{1,0:T(8,128)S(1)}) fusion(f32[1024,32]{1,0:T(8,128)} %get-tuple-element.1056, f32[1024,32]{1,0:T(8,128)} %get-tuple-element.1055, f32[1024,32]{1,0:T(8,128)} %get-tuple-element.1054), kind=kLoop, calls=%fused_computation.2 | loop fusion | flops 786432 | bytes 1441792 | tf_op jit(solution)/shard_map/concatenate | solution.py:886
  40.2 1.6 collective-permute-start.14
  41.8 1.2 collective-permute-start.15
  45.4 5.7 %collective-permute-done.13 = bf16[128,1024]{1,0:T(8,128)(2,1)S(1)} collective-permute-done((bf16[128,1024]{1,0:T(8,128)(2,1)}, bf16[128,1024]{1,0:T(8,128)(2,1)S(1)}, u32[]{:S(2)}, u32[]{:S(2)}) %collective-permute-start.13) | collective-permute-done | bytes 262176 | tf_op jit(solution)/shard_map/ppermute | solution.py:845
  51.2 1.3 collective-permute-start.18
  53.0 2.3 collective-permute-start.20
  55.6 1.2 constant_dynamic-update-slice_fusion.8
  57.0 2.4 collective-permute-done.18
  59.5 2.6 collective-permute-done.20.refs_7_
  63.2 1.4 collective-permute-start.23
  65.7 3.4 %qkv.1 = (bf16[1024,1024]{1,0:T(8,128)(2,1)S(1)}, bf16[1024,256]{1,0:T(8,128)(2,1)S(1)}, bf16[1024,256]{1,0:T(8,128)(2,1)S(1)}, bf16[1024,256]{1,0:T(8,128)(2,1)S(1)}) custom-call(s32[1]{0:T(128)} %bitcast.5.me_ref, bf16[1024,1024]{1,0:T(8,128)(2,1)S(1)} %constant_dynamic-update-slice_fusion.5.tok_ref, bf16[1024,256]{1,0:T(8,128)(2,1)S(1)} %pad_maximum_fusion.2.first_ref, ...), custom_call_target="tpu_custom_call" | custom-call | tf_op jit(solution)/shard_map/qkv/pallas_call | solution.py:76
  69.2 1.4 copy-done.5
  71.6 1.4 collective-permute-start.30
  73.8 1.6 collective-permute-start.27
  75.4 9.0 %attend.1 = (bf16[1024,256]{1,0:T(8,128)(2,1)S(1)}, f32[2,2,1024]{2,1,0:T(2,128)S(1)}) custom-call(bf16[1024,256]{1,0:T(8,128)(2,1)S(1)} %get-tuple-element.909.q_ref, bf16[1024,256]{1,0:T(8,128)(2,1)S(1)} %get-tuple-element.910.k_ref, bf16[1024,256]{1,0:T(8,128)(2,1)S(1)} %get-tuple-element.911.v_ref, s32[1,1024]{1,0:T(1,128)S(1)} %copy-done.72), custom_call_target="tpu_custom_call" | custom-call | tf_op jit(solution)/shard_map/attend/pallas_call | solution.py:152
  85.0 1.3 collective-permute-done.26.refs_3_
  86.4 5.2 %collective-permute-done.28 = bf16[128,1024]{1,0:T(8,128)(2,1)S(1)} collective-permute-done((bf16[128,1024]{1,0:T(8,128)(2,1)S(1)}, bf16[128,1024]{1,0:T(8,128)(2,1)S(1)}, u32[]{:S(2)}, u32[]{:S(2)}) %collective-permute-start.28) | collective-permute-done | bytes 262176 | tf_op jit(solution)/shard_map/ppermute | solution.py:845
  92.2 1.3 collective-permute-start.35
  93.5 1.8 collective-permute-start.33
  95.5 5.1 %collective-permute-done.33.refs_7_ = bf16[704,128]{1,0:T(8,128)(2,1)S(1)} collective-permute-done((bf16[704,128]{1,0:T(8,128)(2,1)S(1)}, bf16[704,128]{1,0:T(8,128)(2,1)S(1)}, u32[]{:S(2)}, u32[]{:S(2)}) %collective-permute-start.33) | collective-permute-done | bytes 180256 | tf_op jit(solution)/shard_map/ppermute | solution.py:873
  102.7 3.4 %collective-permute-done.35.a2 = bf16[1024,256]{1,0:T(8,128)(2,1)S(1)} collective-permute-done((bf16[1024,256]{1,0:T(8,128)(2,1)S(1)}, bf16[1024,256]{1,0:T(8,128)(2,1)S(1)}, u32[]{:S(2)}, u32[]{:S(2)}) %collective-permute-start.35) | collective-permute-done | bytes 524320 | tf_op jit(solution)/shard_map/ppermute | solution.py:845
  106.1 1.9 collective-permute-done.36.a3
  108.8 21.1 %ffn.1 = (bf16[1024,1024]{1,0:T(8,128)(2,1)}, bf16[1024,704]{1,0:T(8,128)(2,1)}, bf16[1024,1408]{1,0:T(8,128)(2,1)}, f32[256,1024]{1,0:T(8,128)}, bf16[512,1024]...) custom-call(s32[1]{0:T(128)} %bitcast.5.me_ref, ...), custom_call_target="tpu_custom_call" | custom-call | tf_op jit(solution)/shard_map/ffn/pallas_call | solution.py:479
  130.2 2.7 %collective-permute-done.37.got_ref = bf16[512,1024]{1,0:T(8,128)(2,1)S(1)} collective-permute-done((bf16[512,1024]{1,0:T(8,128)(2,1)}, bf16[512,1024]{1,0:T(8,128)(2,1)S(1)}, u32[]{:S(2)}, u32[]{:S(2)}) %collective-permute-start.37) | collective-permute-done | bytes 1048608 | tf_op jit(solution)/shard_map/ppermute | solution.py:841
  132.9 1.2 copy-done.34
  136.1 1.3 collective-permute-start.38
  137.3 8.1 %columns_grad.1 = (bf16[1408,128]{1,0:T(8,128)(2,1)}, bf16[1408,128]{1,0:T(8,128)(2,1)}, bf16[1408,128]{1,0:T(8,128)(2,1)}, bf16[1408,128]{1,0:T(8,128)(2,1)}, b...) custom-call(s32[3]{0:T(128)} %pad_add_fusion.place_ref, ...), custom_call_target="tpu_custom_call" | custom-call | tf_op jit(solution)/shard_map/columns_grad/pallas_call | solution.py:539
  145.5 5.6 %down_grad.1 = bf16[704,1024]{1,0:T(8,128)(2,1)} custom-call(bf16[1024,704]{1,0:T(8,128)(2,1)} %get-tuple-element.803.act_ref, bf16[1024,1024]{1,0:T(8,128)(2,1)} %copy-done.80), custom_call_target="tpu_custom_call" | custom-call | tf_op jit(solution)/shard_map/down_grad/pallas_call | solution.py:599
  151.2 1.8 collective-permute-start.40
  154.1 1.2 copy-done.38
  155.3 2.8 %branch.1 = (f32[256,1024]{1,0:T(8,128)S(1)}, bf16[256,1024]{1,0:T(8,128)(2,1)}, bf16[256,256]{1,0:T(8,128)(2,1)S(1)}, bf16[256,256]{1,0:T(8,128)(2,1)S(1)}, bf1...) custom-call(f32[256,1024]{1,0:T(8,128)S(1)} %copy-done.38, bf16[256,1024]{1,0:T(8,128)(2,1)} %collective-permute-done.38.far_ref, ...), custom_call_target="tpu_custom_call" | custom-call | tf_op jit(solution)/shard_map/branch/pallas_call | solution.py:611
  160.1 1.9 collective-permute-done.40.refs_1_
  162.0 1.8 collective-permute-start.41
  165.9 4.5 %collective-permute-done.43.d2 = bf16[256,256]{1,0:T(8,128)(2,1)S(1)} collective-permute-done((bf16[256,256]{1,0:T(8,128)(2,1)S(1)}, bf16[256,256]{1,0:T(8,128)(2,1)S(1)}, u32[]{:S(2)}, u32[]{:S(2)}) %collective-permute-start.43) | collective-permute-done | bytes 131104 | tf_op jit(solution)/shard_map/ppermute | solution.py:845
  170.4 1.9 collective-permute-done.44.d3
  172.3 3.1 %collective-permute-done.45.refs_2_ = bf16[1408,128]{1,0:T(8,128)(2,1)S(1)} collective-permute-done((bf16[1408,128]{1,0:T(8,128)(2,1)S(1)}, bf16[1408,128]{1,0:T(8,128)(2,1)S(1)}, u32[]{:S(2)}, u32[]{:S(2)}) %collective-permute-start.45) | collective-permute-done | bytes 360480 | tf_op jit(solution)/shard_map/ppermute | solution.py:878
  176.9 11.0 %attend_back.2 = (bf16[1024,384]{1,0:T(8,128)(2,1)}, bf16[4,384,128]{2,1,0:T(8,128)(2,1)}, bf16[2944,128]{1,0:T(8,128)(2,1)}) custom-call(s32[3]{0:T(128)} %pad_add_fusion.place_ref, bf16[1024,256]{1,0:T(8,128)(2,1)} %copy-done.10, bf16[1024,256]{1,0:T(8,128)(2,1)} %copy-done.11, bf16[1024,256]{1,0:T(8,128)(2,1)} %copy-done.12, bf16[256,256]{1,0:T(8,128)(2,1)} %copy-done.41, ...), custom_call_target="tpu_custom_call" | custom-call | tf_op jit(solution)/shard_map/attend_back/pallas_call | solution.py:236
  190.1 1.6 collective-permute-start.53
  191.6 1.3 collective-permute-start.51
  195.5 10.9 %attend_back.3 = (bf16[1024,384]{1,0:T(8,128)(2,1)}, bf16[4,384,128]{2,1,0:T(8,128)(2,1)}, bf16[1536,128]{1,0:T(8,128)(2,1)}) custom-call(s32[3]{0:T(128)} %pad_add_fusion.place_ref, bf16[1024,256]{1,0:T(8,128)(2,1)} %copy-done.10, bf16[1024,256]{1,0:T(8,128)(2,1)} %copy-done.11, bf16[1024,256]{1,0:T(8,128)(2,1)} %copy-done.12, bf16[256,256]{1,0:T(8,128)(2,1)} %copy-done.41, ...), custom_call_target="tpu_custom_call" | custom-call | tf_op jit(solution)/shard_map/attend_back/pallas_call | solution.py:236
  207.6 2.7 %input_grad.1 = (bf16[512,1024]{1,0:T(8,128)(2,1)S(1)}, bf16[512,1024]{1,0:T(8,128)(2,1)S(1)}) custom-call(s32[1]{0:T(128)} %bitcast.5.me_ref, bf16[1024,384]{1,0:T(8,128)(2,1)S(1)} %copy-done.6, bf16[1024,384]{1,0:T(8,128)(2,1)S(1)} %copy-done, bf16[1024,768]{1,0:T(8,128)(2,1)S(1)} %copy-done.8), custom_call_target="tpu_custom_call" | custom-call | tf_op jit(solution)/shard_map/input_grad/pallas_call | solution.py:826
  210.3 2.2 collective-permute-done.52.refs_10_
  213.3 3.5 %collective-permute-start.56 = (bf16[384,128]{1,0:T(8,128)(2,1)S(1)}, bf16[384,128]{1,0:T(8,128)(2,1)S(1)}, u32[]{:S(2)}, u32[]{:S(2)}) collective-permute-start(bf16[384,128]{1,0:T(8,128)(2,1)S(1)} %get-tuple-element.953), channel_id=1, source_target_pairs={{0,4},{1,5},{2,6},{3,7},{4,0},{5,1},{6,2},{7,3},{8,12},{9,13},{10,... | collective-permute-start | bytes 294920 | tf_op jit(solution)/shard_map/ppermute | solution.py:878
  217.2 2.2 out_projection_grad.1
  220.9 3.4 %collective-permute-done.56.refs_2_ = bf16[384,128]{1,0:T(8,128)(2,1)S(1)} collective-permute-done((bf16[384,128]{1,0:T(8,128)(2,1)S(1)}, bf16[384,128]{1,0:T(8,128)(2,1)S(1)}, u32[]{:S(2)}, u32[]{:S(2)}) %collective-permute-start.56) | collective-permute-done | bytes 98336 | tf_op jit(solution)/shard_map/ppermute | solution.py:878
  224.3 1.7 collective-permute-done.58.got_ref
  228.6 3.1 %collective-permute-start.61 = (bf16[384,128]{1,0:T(8,128)(2,1)S(1)}, bf16[384,128]{1,0:T(8,128)(2,1)S(1)}, u32[]{:S(2)}, u32[]{:S(2)}) collective-permute-start(bf16[384,128]{1,0:T(8,128)(2,1)S(1)} %get-tuple-element.984), channel_id=1, source_target_pairs={{0,4},{1,5},{2,6},{3,7},{4,0},{5,1},{6,2},{7,3},{8,12},{9,13},{10,... | collective-permute-start | bytes 294920 | tf_op jit(solution)/shard_map/ppermute | solution.py:878
  232.2 2.0 total.7
  235.7 4.6 %collective-permute-done.61.refs_6_ = bf16[384,128]{1,0:T(8,128)(2,1)S(1)} collective-permute-done((bf16[384,128]{1,0:T(8,128)(2,1)S(1)}, bf16[384,128]{1,0:T(8,128)(2,1)S(1)}, u32[]{:S(2)}, u32[]{:S(2)}) %collective-permute-start.61) | collective-permute-done | bytes 98336 | tf_op jit(solution)/shard_map/ppermute | solution.py:878
  240.4 2.1 cut.1
  242.9 3.3 %collective-permute-start.65 = (bf16[256,128]{1,0:T(8,128)(2,1)}, bf16[256,128]{1,0:T(8,128)(2,1)S(1)}, u32[]{:S(2)}, u32[]{:S(2)}) collective-permute-start(bf16[256,128]{1,0:T(8,128)(2,1)} %get-tuple-element.1006), channel_id=1, source_target_pairs={{0,2},{1,3},{2,4},{3,5},{4,6},{5,7},{6,0},{7,1},{8,10},{9,11},{10,... | collective-permute-start | bytes 196616 | tf_op jit(solution)/shard_map/ppermute | solution.py:878
  246.4 2.2 collective-permute-start.67
  248.6 3.1 %token_grad.1 = bf16[256,1024]{1,0:T(8,128)(2,1)} custom-call(f32[256,1024]{1,0:T(8,128)} %copy-done.36, bf16[256,1024]{1,0:T(8,128)(2,1)} %copy-done.89, bf16[256,1024]{1,0:T(8,128)(2,1)} %bitcast.31, f32[1,1024]{1,0:T(1,128)} %bitcast.23, f32[256,1024]{1,0:T(8,128)} %copy-done.35), custom_call_target="tpu_custom_call" | custom-call | tf_op jit(solution)/shard_map/token_grad/pallas_call | solution.py:611
  252.3 1.9 collective-permute-done.69.got_ref
  255.7 2.3 finish.1
  (328 shorter events, 46.9 us)
Async XLA Ops:
  7.2 100.8 %all-gather.3.cloned.1.call-start = ((), (), s32[]{:S(2)}) async-start(), calls=%async_computation.2 | async-start | bytes 3244032 | tf_op jit(solution)/shard_map/all_gather | solution.py:941
  10.0 6.0 %collective-permute-start.1 = (bf16[208,128]{1,0:T(8,128)(2,1)}, bf16[208,128]{1,0:T(8,128)(2,1)S(1)}, u32[]{:S(2)}, u32[]{:S(2)}) collective-permute-start(bf16[208,128]{1,0:T(8,128)(2,1)} %get-tuple-element.540), channel_id=1, source_target_pairs={{0,16},{8,24},{16,0},{24,8},{1,17},{9,25},{17,1},{25,9},{2,18},{10... | collective-permute-start | bytes 159752 | tf_op jit(solution)/shard_map/ppermute | solution.py:845
  12.7 15.8 %collective-permute-start.3 = (bf16[704,128]{1,0:T(8,128)(2,1)}, bf16[704,128]{1,0:T(8,128)(2,1)S(1)}, u32[]{:S(2)}, u32[]{:S(2)}) collective-permute-start(bf16[704,128]{1,0:T(8,128)(2,1)} %get-tuple-element.702.refs_0_), channel_id=1, source_target_pairs={{0,2},{1,3},{2,4},{3,5},{4,6},{5,7},{6,0},{7,1},{8,10},{9,11},{10,... | collective-permute-start | bytes 540680 | tf_op jit(solution)/shard_map/ppermute | solution.py:878
  14.6 14.0 %collective-permute-start.5 = (bf16[704,128]{1,0:T(8,128)(2,1)}, bf16[704,128]{1,0:T(8,128)(2,1)S(1)}, u32[]{:S(2)}, u32[]{:S(2)}) collective-permute-start(bf16[704,128]{1,0:T(8,128)(2,1)} %get-tuple-element.702.refs_0_), channel_id=1, source_target_pairs={{0,1},{1,0},{2,3},{3,2},{4,5},{5,4},{6,7},{7,6},{8,9},{9,8},{10,11... | collective-permute-start | bytes 540680 | tf_op jit(solution)/shard_map/ppermute | solution.py:873
  18.4 11.4 %collective-permute-start.6 = (bf16[1088,128]{1,0:T(8,128)(2,1)S(1)}, bf16[1088,128]{1,0:T(8,128)(2,1)S(1)}, u32[]{:S(2)}, u32[]{:S(2)}) collective-permute-start(bf16[1088,128]{1,0:T(8,128)(2,1)S(1)} %constant_dynamic-update-slice_fusion.refs_0_), channel_id=1, source_target_pairs={{0,2},{1,3},{2,4},{3,5},{4,6},{5,7},{6,0},{7,1},{8,10},{9,11},{10,... | collective-permute-start | bytes 835592 | tf_op jit(solution)/shard_map/ppermute | solution.py:878
  20.1 9.7 %collective-permute-start.7 = (bf16[1088,128]{1,0:T(8,128)(2,1)S(1)}, bf16[1088,128]{1,0:T(8,128)(2,1)S(1)}, u32[]{:S(2)}, u32[]{:S(2)}) collective-permute-start(bf16[1088,128]{1,0:T(8,128)(2,1)S(1)} %constant_dynamic-update-slice_fusion.refs_0_), channel_id=1, source_target_pairs={{0,1},{1,0},{2,3},{3,2},{4,5},{5,4},{6,7},{7,6},{8,9},{9,8},{10,11... | collective-permute-start | bytes 835592 | tf_op jit(solution)/shard_map/ppermute | solution.py:873
  21.6 8.2 %collective-permute-start.4 = (bf16[128,1024]{1,0:T(8,128)(2,1)}, bf16[128,1024]{1,0:T(8,128)(2,1)S(1)}, u32[]{:S(2)}, u32[]{:S(2)}) collective-permute-start(bf16[128,1024]{1,0:T(8,128)(2,1)} %get-tuple-element.554), channel_id=1, source_target_pairs={{0,16},{8,24},{16,0},{24,8},{1,17},{9,25},{17,1},{25,9},{2,18},{10... | collective-permute-start | bytes 786440 | tf_op jit(solution)/shard_map/ppermute | solution.py:845
  30.6 9.5 %collective-permute-start.8 = (bf16[1088,128]{1,0:T(8,128)(2,1)S(1)}, bf16[1088,128]{1,0:T(8,128)(2,1)S(1)}, u32[]{:S(2)}, u32[]{:S(2)}) collective-permute-start(bf16[1088,128]{1,0:T(8,128)(2,1)S(1)} %collective-permute-done.6.refs_1_), channel_id=1, source_target_pairs={{0,2},{1,3},{2,4},{3,5},{4,6},{5,7},{6,0},{7,1},{8,10},{9,11},{10,... | collective-permute-start | bytes 835592 | tf_op jit(solution)/shard_map/ppermute | solution.py:878
  32.1 7.9 %collective-permute-start.9 = (bf16[1088,128]{1,0:T(8,128)(2,1)S(1)}, bf16[1088,128]{1,0:T(8,128)(2,1)S(1)}, u32[]{:S(2)}, u32[]{:S(2)}) collective-permute-start(bf16[1088,128]{1,0:T(8,128)(2,1)S(1)} %collective-permute-done.6.refs_1_), channel_id=1, source_target_pairs={{0,1},{1,0},{2,3},{3,2},{4,5},{5,4},{6,7},{7,6},{8,9},{9,8},{10,11... | collective-permute-start | bytes 835592 | tf_op jit(solution)/shard_map/ppermute | solution.py:873
  32.6 5.3 %collective-permute-start.12 = (bf16[352,128]{1,0:T(8,128)(2,1)}, bf16[352,128]{1,0:T(8,128)(2,1)S(1)}, u32[]{:S(2)}, u32[]{:S(2)}) collective-permute-start(bf16[352,128]{1,0:T(8,128)(2,1)} %get-tuple-element.586), channel_id=1, source_target_pairs={{0,24},{8,16},{16,8},{24,0},{1,25},{9,17},{17,9},{25,1},{2,26},{10... | collective-permute-start | bytes 270344 | tf_op jit(solution)/shard_map/ppermute | solution.py:849
  32.6 6.0 %collective-permute-start.11 = (bf16[352,128]{1,0:T(8,128)(2,1)}, bf16[352,128]{1,0:T(8,128)(2,1)S(1)}, u32[]{:S(2)}, u32[]{:S(2)}) collective-permute-start(bf16[352,128]{1,0:T(8,128)(2,1)} %get-tuple-element.585), channel_id=1, source_target_pairs={{0,16},{8,24},{16,0},{24,8},{1,17},{9,25},{17,1},{25,9},{2,18},{10... | collective-permute-start | bytes 270344 | tf_op jit(solution)/shard_map/ppermute | solution.py:845
  40.1 211.7 %reduce-scatter.2.cloned.1.call-start = ((), (), s32[]{:S(2)}) async-start(), calls=%async_computation.1 | async-start | bytes 1622016 | tf_op jit(solution)/shard_map/reduce_scatter | solution.py:992
  40.1 11.0 %collective-permute-start.16 = (bf16[256,1024]{1,0:T(8,128)(2,1)S(1)}, bf16[256,1024]{1,0:T(8,128)(2,1)}, u32[]{:S(2)}, u32[]{:S(2)}) collective-permute-start(bf16[256,1024]{1,0:T(8,128)(2,1)S(1)} %bitcast.32), channel_id=1, source_target_pairs={{0,8},{8,0},{16,24},{24,16},{1,9},{9,1},{17,25},{25,17},{2,10},{10... | collective-permute-start | bytes 1572872 | tf_op jit(solution)/shard_map/ppermute | solution.py:841
  40.2 10.9 %collective-permute-start.14 = (bf16[1088,128]{1,0:T(8,128)(2,1)S(1)}, bf16[1088,128]{1,0:T(8,128)(2,1)S(1)}, u32[]{:S(2)}, u32[]{:S(2)}) collective-permute-start(bf16[1088,128]{1,0:T(8,128)(2,1)S(1)} %collective-permute-done.8.refs_2_), channel_id=1, source_target_pairs={{0,2},{1,3},{2,4},{3,5},{4,6},{5,7},{6,0},{7,1},{8,10},{9,11},{10,... | collective-permute-start | bytes 835592 | tf_op jit(solution)/shard_map/ppermute | solution.py:878
  41.8 9.4 %collective-permute-start.15 = (bf16[1088,128]{1,0:T(8,128)(2,1)S(1)}, bf16[1088,128]{1,0:T(8,128)(2,1)S(1)}, u32[]{:S(2)}, u32[]{:S(2)}) collective-permute-start(bf16[1088,128]{1,0:T(8,128)(2,1)S(1)} %collective-permute-done.8.refs_2_), channel_id=1, source_target_pairs={{0,1},{1,0},{2,3},{3,2},{4,5},{5,4},{6,7},{7,6},{8,9},{9,8},{10,11... | collective-permute-start | bytes 835592 | tf_op jit(solution)/shard_map/ppermute | solution.py:873
  43.0 8.1 %collective-permute-start.13 = (bf16[128,1024]{1,0:T(8,128)(2,1)}, bf16[128,1024]{1,0:T(8,128)(2,1)S(1)}, u32[]{:S(2)}, u32[]{:S(2)}) collective-permute-start(bf16[128,1024]{1,0:T(8,128)(2,1)} %get-tuple-element.590), channel_id=1, source_target_pairs={{0,16},{8,24},{16,0},{24,8},{1,17},{9,25},{17,1},{25,9},{2,18},{10... | collective-permute-start | bytes 786440 | tf_op jit(solution)/shard_map/ppermute | solution.py:845
  51.2 5.8 %collective-permute-start.19 = (bf16[256,256]{1,0:T(8,128)(2,1)S(1)}, bf16[256,256]{1,0:T(8,128)(2,1)S(1)}, u32[]{:S(2)}, u32[]{:S(2)}) collective-permute-start(bf16[256,256]{1,0:T(8,128)(2,1)S(1)} %get-tuple-element.609), channel_id=1, source_target_pairs={{0,24},{8,16},{16,8},{24,0},{1,25},{9,17},{17,9},{25,1},{2,26},{10... | collective-permute-start | bytes 393224 | tf_op jit(solution)/shard_map/ppermute | solution.py:849
  51.2 8.2 %collective-permute-start.18 = (bf16[256,256]{1,0:T(8,128)(2,1)S(1)}, bf16[256,256]{1,0:T(8,128)(2,1)S(1)}, u32[]{:S(2)}, u32[]{:S(2)}) collective-permute-start(bf16[256,256]{1,0:T(8,128)(2,1)S(1)} %get-tuple-element.608), channel_id=1, source_target_pairs={{0,16},{8,24},{16,0},{24,8},{1,17},{9,25},{17,1},{25,9},{2,18},{10... | collective-permute-start | bytes 393224 | tf_op jit(solution)/shard_map/ppermute | solution.py:845
  52.5 6.9 %collective-permute-start.17 = (bf16[256,256]{1,0:T(8,128)(2,1)S(1)}, bf16[256,256]{1,0:T(8,128)(2,1)S(1)}, u32[]{:S(2)}, u32[]{:S(2)}) collective-permute-start(bf16[256,256]{1,0:T(8,128)(2,1)S(1)} %get-tuple-element.607), channel_id=1, source_target_pairs={{0,8},{8,0},{16,24},{24,16},{1,9},{9,1},{17,25},{25,17},{2,10},{10... | collective-permute-start | bytes 393224 | tf_op jit(solution)/shard_map/ppermute | solution.py:841
  53.0 9.1 %collective-permute-start.20 = (bf16[1088,128]{1,0:T(8,128)(2,1)S(1)}, bf16[1088,128]{1,0:T(8,128)(2,1)S(1)}, u32[]{:S(2)}, u32[]{:S(2)}) collective-permute-start(bf16[1088,128]{1,0:T(8,128)(2,1)S(1)} %collective-permute-done.14.refs_3_), channel_id=1, source_target_pairs={{0,1},{1,0},{2,3},{3,2},{4,5},{5,4},{6,7},{7,6},{8,9},{9,8},{10,11... | collective-permute-start | bytes 835592 | tf_op jit(solution)/shard_map/ppermute | solution.py:873
  62.2 9.3 %collective-permute-start.25 = (bf16[256,1024]{1,0:T(8,128)(2,1)S(1)}, bf16[256,1024]{1,0:T(8,128)(2,1)S(1)}, u32[]{:S(2)}, u32[]{:S(2)}) collective-permute-start(bf16[256,1024]{1,0:T(8,128)(2,1)S(1)} %bitcast.18), channel_id=1, source_target_pairs={{0,8},{8,0},{16,24},{24,16},{1,9},{9,1},{17,25},{25,17},{2,10},{10... | collective-permute-start | bytes 1572872 | tf_op jit(solution)/shard_map/ppermute | solution.py:841
  62.2 9.3 %collective-permute-start.24 = (bf16[128,1024]{1,0:T(8,128)(2,1)S(1)}, bf16[128,1024]{1,0:T(8,128)(2,1)S(1)}, u32[]{:S(2)}, u32[]{:S(2)}) collective-permute-start(bf16[128,1024]{1,0:T(8,128)(2,1)S(1)} %get-tuple-element.635), channel_id=1, source_target_pairs={{0,16},{8,24},{16,0},{24,8},{1,17},{9,25},{17,1},{25,9},{2,18},{10... | collective-permute-start | bytes 786440 | tf_op jit(solution)/shard_map/ppermute | solution.py:845
  62.9 8.6 %collective-permute-start.22 = (bf16[704,128]{1,0:T(8,128)(2,1)S(1)}, bf16[704,128]{1,0:T(8,128)(2,1)S(1)}, u32[]{:S(2)}, u32[]{:S(2)}) collective-permute-start(bf16[704,128]{1,0:T(8,128)(2,1)S(1)} %copy-done.63), channel_id=1, source_target_pairs={{0,2},{1,3},{2,4},{3,5},{4,6},{5,7},{6,0},{7,1},{8,10},{9,11},{10,... | collective-permute-start | bytes 540680 | tf_op jit(solution)/shard_map/ppermute | solution.py:878
  63.2 8.2 %collective-permute-start.23 = (bf16[704,128]{1,0:T(8,128)(2,1)S(1)}, bf16[704,128]{1,0:T(8,128)(2,1)S(1)}, u32[]{:S(2)}, u32[]{:S(2)}) collective-permute-start(bf16[704,128]{1,0:T(8,128)(2,1)S(1)} %copy-done.63), channel_id=1, source_target_pairs={{0,1},{1,0},{2,3},{3,2},{4,5},{5,4},{6,7},{7,6},{8,9},{9,8},{10,11... | collective-permute-start | bytes 540680 | tf_op jit(solution)/shard_map/ppermute | solution.py:873
  71.5 20.0 %collective-permute-start.29 = (bf16[256,1024]{1,0:T(8,128)(2,1)S(1)}, bf16[256,1024]{1,0:T(8,128)(2,1)S(1)}, u32[]{:S(2)}, u32[]{:S(2)}) collective-permute-start(bf16[256,1024]{1,0:T(8,128)(2,1)S(1)} %get-tuple-element.833.wo0.w0), channel_id=1, source_target_pairs={{0,8},{8,0},{16,24},{24,16},{1,9},{9,1},{17,25},{25,17},{2,10},{10... | collective-permute-start | bytes 1572872 | tf_op jit(solution)/shard_map/ppermute | solution.py:841
  71.6 20.0 %collective-permute-start.30 = (bf16[256,1024]{1,0:T(8,128)(2,1)S(1)}, bf16[256,1024]{1,0:T(8,128)(2,1)S(1)}, u32[]{:S(2)}, u32[]{:S(2)}) collective-permute-start(bf16[256,1024]{1,0:T(8,128)(2,1)S(1)} %get-tuple-element.833.wo0.w0), channel_id=1, source_target_pairs={{0,16},{8,24},{16,0},{24,8},{1,17},{9,25},{17,1},{25,9},{2,18},{10... | collective-permute-start | bytes 1572872 | tf_op jit(solution)/shard_map/ppermute | solution.py:845
  72.9 18.6 %collective-permute-start.28 = (bf16[128,1024]{1,0:T(8,128)(2,1)S(1)}, bf16[128,1024]{1,0:T(8,128)(2,1)S(1)}, u32[]{:S(2)}, u32[]{:S(2)}) collective-permute-start(bf16[128,1024]{1,0:T(8,128)(2,1)S(1)} %get-tuple-element.666), channel_id=1, source_target_pairs={{0,16},{8,24},{16,0},{24,8},{1,17},{9,25},{17,1},{25,9},{2,18},{10... | collective-permute-start | bytes 786440 | tf_op jit(solution)/shard_map/ppermute | solution.py:845
  73.7 12.7 %collective-permute-start.26 = (bf16[704,128]{1,0:T(8,128)(2,1)S(1)}, bf16[704,128]{1,0:T(8,128)(2,1)S(1)}, u32[]{:S(2)}, u32[]{:S(2)}) collective-permute-start(bf16[704,128]{1,0:T(8,128)(2,1)S(1)} %collective-permute-done.22.refs_2_), channel_id=1, source_target_pairs={{0,2},{1,3},{2,4},{3,5},{4,6},{5,7},{6,0},{7,1},{8,10},{9,11},{10,... | collective-permute-start | bytes 540680 | tf_op jit(solution)/shard_map/ppermute | solution.py:878
  73.8 12.5 %collective-permute-start.27 = (bf16[704,128]{1,0:T(8,128)(2,1)S(1)}, bf16[704,128]{1,0:T(8,128)(2,1)S(1)}, u32[]{:S(2)}, u32[]{:S(2)}) collective-permute-start(bf16[704,128]{1,0:T(8,128)(2,1)S(1)} %collective-permute-done.22.refs_2_), channel_id=1, source_target_pairs={{0,1},{1,0},{2,3},{3,2},{4,5},{5,4},{6,7},{7,6},{8,9},{9,8},{10,11... | collective-permute-start | bytes 540680 | tf_op jit(solution)/shard_map/ppermute | solution.py:873
  91.6 11.0 %collective-permute-start.31 = (bf16[256,1024]{1,0:T(8,128)(2,1)S(1)}, bf16[256,1024]{1,0:T(8,128)(2,1)S(1)}, u32[]{:S(2)}, u32[]{:S(2)}) collective-permute-start(bf16[256,1024]{1,0:T(8,128)(2,1)S(1)} %pad_maximum_fusion.4), channel_id=1, source_target_pairs={{0,8},{8,0},{16,24},{24,16},{1,9},{9,1},{17,25},{25,17},{2,10},{10... | collective-permute-start | bytes 1572872 | tf_op jit(solution)/shard_map/ppermute | solution.py:841
  91.7 11.0 %collective-permute-start.34 = (bf16[1024,256]{1,0:T(8,128)(2,1)S(1)}, bf16[1024,256]{1,0:T(8,128)(2,1)S(1)}, u32[]{:S(2)}, u32[]{:S(2)}) collective-permute-start(bf16[1024,256]{1,0:T(8,128)(2,1)S(1)} %get-tuple-element.962.a0.act_ref), channel_id=1, source_target_pairs={{0,8},{8,0},{16,24},{24,16},{1,9},{9,1},{17,25},{25,17},{2,10},{10... | collective-permute-start | bytes 1572872 | tf_op jit(solution)/shard_map/ppermute | solution.py:841
  92.2 13.9 %collective-permute-start.35 = (bf16[1024,256]{1,0:T(8,128)(2,1)S(1)}, bf16[1024,256]{1,0:T(8,128)(2,1)S(1)}, u32[]{:S(2)}, u32[]{:S(2)}) collective-permute-start(bf16[1024,256]{1,0:T(8,128)(2,1)S(1)} %get-tuple-element.962.a0.act_ref), channel_id=1, source_target_pairs={{0,16},{8,24},{16,0},{24,8},{1,17},{9,25},{17,1},{25,9},{2,18},{10... | collective-permute-start | bytes 1572872 | tf_op jit(solution)/shard_map/ppermute | solution.py:845
  93.5 9.2 %collective-permute-start.32 = (bf16[256,1024]{1,0:T(8,128)(2,1)S(1)}, bf16[256,1024]{1,0:T(8,128)(2,1)S(1)}, u32[]{:S(2)}, u32[]{:S(2)}) collective-permute-start(bf16[256,1024]{1,0:T(8,128)(2,1)S(1)} %collective-permute-done.30.wo2.w2), channel_id=1, source_target_pairs={{0,8},{8,0},{16,24},{24,16},{1,9},{9,1},{17,25},{25,17},{2,10},{10... | collective-permute-start | bytes 1572872 | tf_op jit(solution)/shard_map/ppermute | solution.py:841
  93.5 7.1 %collective-permute-start.33 = (bf16[704,128]{1,0:T(8,128)(2,1)S(1)}, bf16[704,128]{1,0:T(8,128)(2,1)S(1)}, u32[]{:S(2)}, u32[]{:S(2)}) collective-permute-start(bf16[704,128]{1,0:T(8,128)(2,1)S(1)} %collective-permute-done.26.refs_3_), channel_id=1, source_target_pairs={{0,1},{1,0},{2,3},{3,2},{4,5},{5,4},{6,7},{7,6},{8,9},{9,8},{10,11... | collective-permute-start | bytes 540680 | tf_op jit(solution)/shard_map/ppermute | solution.py:873
  136.1 15.1 %collective-permute-start.38 = (bf16[256,1024]{1,0:T(8,128)(2,1)}, bf16[256,1024]{1,0:T(8,128)(2,1)}, u32[]{:S(2)}, u32[]{:S(2)}) collective-permute-start(bf16[256,1024]{1,0:T(8,128)(2,1)} %get-tuple-element.791), channel_id=1, source_target_pairs={{0,16},{8,24},{16,0},{24,8},{1,17},{9,25},{17,1},{25,9},{2,18},{10... | collective-permute-start | bytes 1572872 | tf_op jit(solution)/shard_map/ppermute | solution.py:845
  151.1 7.0 %collective-permute-start.39 = (bf16[512,1024]{1,0:T(8,128)(2,1)}, bf16[512,1024]{1,0:T(8,128)(2,1)S(1)}, u32[]{:S(2)}, u32[]{:S(2)}) collective-permute-start(bf16[512,1024]{1,0:T(8,128)(2,1)} %get-tuple-element.821), channel_id=1, source_target_pairs={{0,8},{8,0},{16,24},{24,16},{1,9},{9,1},{17,25},{25,17},{2,10},{10... | collective-permute-start | bytes 3145736 | tf_op jit(solution)/shard_map/ppermute | solution.py:841
  151.2 10.8 %collective-permute-start.40 = (bf16[1408,128]{1,0:T(8,128)(2,1)S(1)}, bf16[1408,128]{1,0:T(8,128)(2,1)S(1)}, u32[]{:S(2)}, u32[]{:S(2)}) collective-permute-start(bf16[1408,128]{1,0:T(8,128)(2,1)S(1)} %copy-done.94), channel_id=1, source_target_pairs={{0,1},{1,0},{2,3},{3,2},{4,5},{5,4},{6,7},{7,6},{8,9},{9,8},{10,11... | collective-permute-start | bytes 1081352 | tf_op jit(solution)/shard_map/ppermute | solution.py:873
  162.0 10.3 %collective-permute-start.41 = (bf16[1408,128]{1,0:T(8,128)(2,1)S(1)}, bf16[1408,128]{1,0:T(8,128)(2,1)S(1)}, u32[]{:S(2)}, u32[]{:S(2)}) collective-permute-start(bf16[1408,128]{1,0:T(8,128)(2,1)S(1)} %copy-done.93), channel_id=1, source_target_pairs={{0,1},{1,0},{2,3},{3,2},{4,5},{5,4},{6,7},{7,6},{8,9},{9,8},{10,11... | collective-permute-start | bytes 1081352 | tf_op jit(solution)/shard_map/ppermute | solution.py:873
  163.8 11.5 %collective-permute-start.45 = (bf16[1408,128]{1,0:T(8,128)(2,1)S(1)}, bf16[1408,128]{1,0:T(8,128)(2,1)S(1)}, u32[]{:S(2)}, u32[]{:S(2)}) collective-permute-start(bf16[1408,128]{1,0:T(8,128)(2,1)S(1)} %total.4), channel_id=1, source_target_pairs={{0,2},{1,3},{2,4},{3,5},{4,6},{5,7},{6,0},{7,1},{8,10},{9,11},{10,... | collective-permute-start | bytes 1081352 | tf_op jit(solution)/shard_map/ppermute | solution.py:878
  164.0 6.4 %collective-permute-start.43 = (bf16[256,256]{1,0:T(8,128)(2,1)S(1)}, bf16[256,256]{1,0:T(8,128)(2,1)S(1)}, u32[]{:S(2)}, u32[]{:S(2)}) collective-permute-start(bf16[256,256]{1,0:T(8,128)(2,1)S(1)} %get-tuple-element.870), channel_id=1, source_target_pairs={{0,16},{8,24},{16,0},{24,8},{1,17},{9,25},{17,1},{25,9},{2,18},{10... | collective-permute-start | bytes 393224 | tf_op jit(solution)/shard_map/ppermute | solution.py:845
  164.8 7.5 %collective-permute-start.44 = (bf16[256,256]{1,0:T(8,128)(2,1)S(1)}, bf16[256,256]{1,0:T(8,128)(2,1)S(1)}, u32[]{:S(2)}, u32[]{:S(2)}) collective-permute-start(bf16[256,256]{1,0:T(8,128)(2,1)S(1)} %get-tuple-element.871), channel_id=1, source_target_pairs={{0,24},{8,16},{16,8},{24,0},{1,25},{9,17},{17,9},{25,1},{2,26},{10... | collective-permute-start | bytes 393224 | tf_op jit(solution)/shard_map/ppermute | solution.py:849
  175.4 13.6 %collective-permute-start.47 = (bf16[256,1024]{1,0:T(8,128)(2,1)}, bf16[256,1024]{1,0:T(8,128)(2,1)S(1)}, u32[]{:S(2)}, u32[]{:S(2)}) collective-permute-start(bf16[256,1024]{1,0:T(8,128)(2,1)} %get-tuple-element.963.d0), channel_id=1, source_target_pairs={{0,8},{8,0},{16,24},{24,16},{1,9},{9,1},{17,25},{25,17},{2,10},{10... | collective-permute-start | bytes 1572872 | tf_op jit(solution)/shard_map/ppermute | solution.py:841
  175.4 14.7 %collective-permute-start.48 = (bf16[256,1024]{1,0:T(8,128)(2,1)}, bf16[256,1024]{1,0:T(8,128)(2,1)}, u32[]{:S(2)}, u32[]{:S(2)}) collective-permute-start(bf16[256,1024]{1,0:T(8,128)(2,1)} %get-tuple-element.963.d0), channel_id=1, source_target_pairs={{0,16},{8,24},{16,0},{24,8},{1,17},{9,25},{17,1},{25,9},{2,18},{10... | collective-permute-start | bytes 1572872 | tf_op jit(solution)/shard_map/ppermute | solution.py:845
  176.1 11.8 %collective-permute-start.46 = (bf16[1408,128]{1,0:T(8,128)(2,1)S(1)}, bf16[1408,128]{1,0:T(8,128)(2,1)S(1)}, u32[]{:S(2)}, u32[]{:S(2)}) collective-permute-start(bf16[1408,128]{1,0:T(8,128)(2,1)S(1)} %copy-done.92), channel_id=1, source_target_pairs={{0,1},{1,0},{2,3},{3,2},{4,5},{5,4},{6,7},{7,6},{8,9},{9,8},{10,11... | collective-permute-start | bytes 1081352 | tf_op jit(solution)/shard_map/ppermute | solution.py:873
  176.6 12.5 %collective-permute-start.49 = (bf16[1408,128]{1,0:T(8,128)(2,1)S(1)}, bf16[1408,128]{1,0:T(8,128)(2,1)S(1)}, u32[]{:S(2)}, u32[]{:S(2)}) collective-permute-start(bf16[1408,128]{1,0:T(8,128)(2,1)S(1)} %total.5), channel_id=1, source_target_pairs={{0,2},{1,3},{2,4},{3,5},{4,6},{5,7},{6,0},{7,1},{8,10},{9,11},{10,... | collective-permute-start | bytes 1081352 | tf_op jit(solution)/shard_map/ppermute | solution.py:878
  190.1 22.4 %collective-permute-start.53 = (bf16[2944,128]{1,0:T(8,128)(2,1)}, bf16[2944,128]{1,0:T(8,128)(2,1)S(1)}, u32[]{:S(2)}, u32[]{:S(2)}) collective-permute-start(bf16[2944,128]{1,0:T(8,128)(2,1)} %get-tuple-element.934), channel_id=1, source_target_pairs={{0,1},{1,0},{2,3},{3,2},{4,5},{5,4},{6,7},{7,6},{8,9},{9,8},{10,11... | collective-permute-start | bytes 2261000 | tf_op jit(solution)/shard_map/ppermute | solution.py:873
  191.6 20.8 %collective-permute-start.50 = (bf16[256,1024]{1,0:T(8,128)(2,1)}, bf16[256,1024]{1,0:T(8,128)(2,1)}, u32[]{:S(2)}, u32[]{:S(2)}) collective-permute-start(bf16[256,1024]{1,0:T(8,128)(2,1)} %collective-permute-done.48.d2), channel_id=1, source_target_pairs={{0,8},{8,0},{16,24},{24,16},{1,9},{9,1},{17,25},{25,17},{2,10},{10... | collective-permute-start | bytes 1572872 | tf_op jit(solution)/shard_map/ppermute | solution.py:841
  191.6 20.8 %collective-permute-start.51 = (bf16[256,1024]{1,0:T(8,128)(2,1)}, bf16[256,1024]{1,0:T(8,128)(2,1)}, u32[]{:S(2)}, u32[]{:S(2)}) collective-permute-start(bf16[256,1024]{1,0:T(8,128)(2,1)} %get-tuple-element.923), channel_id=1, source_target_pairs={{0,16},{8,24},{16,0},{24,8},{1,17},{9,25},{17,1},{25,9},{2,18},{10... | collective-permute-start | bytes 1572872 | tf_op jit(solution)/shard_map/ppermute | solution.py:845
  193.8 18.7 %collective-permute-start.52 = (bf16[1408,128]{1,0:T(8,128)(2,1)}, bf16[1408,128]{1,0:T(8,128)(2,1)}, u32[]{:S(2)}, u32[]{:S(2)}) collective-permute-start(bf16[1408,128]{1,0:T(8,128)(2,1)} %total.6), channel_id=1, source_target_pairs={{0,2},{1,3},{2,4},{3,5},{4,6},{5,7},{6,0},{7,1},{8,10},{9,11},{10,... | collective-permute-start | bytes 1081352 | tf_op jit(solution)/shard_map/ppermute | solution.py:878
  194.7 15.5 %collective-permute-start.54 = (bf16[512,128]{1,0:T(8,128)(2,1)S(1)}, bf16[512,128]{1,0:T(8,128)(2,1)S(1)}, u32[]{:S(2)}, u32[]{:S(2)}) collective-permute-start(bf16[512,128]{1,0:T(8,128)(2,1)S(1)} %constant_dynamic-slice_fusion.4), channel_id=1, source_target_pairs={{0,16},{8,24},{16,0},{24,8},{1,17},{9,25},{17,1},{25,9},{2,18},{10... | collective-permute-start | bytes 393224 | tf_op jit(solution)/shard_map/ppermute | solution.py:845
  212.5 6.9 %collective-permute-start.59 = (bf16[512,1024]{1,0:T(8,128)(2,1)S(1)}, bf16[512,1024]{1,0:T(8,128)(2,1)S(1)}, u32[]{:S(2)}, u32[]{:S(2)}) collective-permute-start(bf16[512,1024]{1,0:T(8,128)(2,1)S(1)} %get-tuple-element.959), channel_id=1, source_target_pairs={{0,8},{8,0},{16,24},{24,16},{1,9},{9,1},{17,25},{25,17},{2,10},{10... | collective-permute-start | bytes 3145736 | tf_op jit(solution)/shard_map/ppermute | solution.py:841
  212.6 13.5 %collective-permute-start.58 = (bf16[1536,128]{1,0:T(8,128)(2,1)S(1)}, bf16[1536,128]{1,0:T(8,128)(2,1)S(1)}, u32[]{:S(2)}, u32[]{:S(2)}) collective-permute-start(bf16[1536,128]{1,0:T(8,128)(2,1)S(1)} %copy-done.91), channel_id=1, source_target_pairs={{0,1},{1,0},{2,3},{3,2},{4,5},{5,4},{6,7},{7,6},{8,9},{9,8},{10,11... | collective-permute-start | bytes 1179656 | tf_op jit(solution)/shard_map/ppermute | solution.py:873
  213.3 7.6 %collective-permute-start.55 = (bf16[384,128]{1,0:T(8,128)(2,1)S(1)}, bf16[384,128]{1,0:T(8,128)(2,1)S(1)}, u32[]{:S(2)}, u32[]{:S(2)}) collective-permute-start(bf16[384,128]{1,0:T(8,128)(2,1)S(1)} %get-tuple-element.952), channel_id=1, source_target_pairs={{0,2},{1,3},{2,4},{3,5},{4,6},{5,7},{6,0},{7,1},{8,10},{9,11},{10,... | collective-permute-start | bytes 294920 | tf_op jit(solution)/shard_map/ppermute | solution.py:878
  213.3 10.9 %collective-permute-start.56 = (bf16[384,128]{1,0:T(8,128)(2,1)S(1)}, bf16[384,128]{1,0:T(8,128)(2,1)S(1)}, u32[]{:S(2)}, u32[]{:S(2)}) collective-permute-start(bf16[384,128]{1,0:T(8,128)(2,1)S(1)} %get-tuple-element.953), channel_id=1, source_target_pairs={{0,4},{1,5},{2,6},{3,7},{4,0},{5,1},{6,2},{7,3},{8,12},{9,13},{10,... | collective-permute-start | bytes 294920 | tf_op jit(solution)/shard_map/ppermute | solution.py:878
  216.9 7.4 %collective-permute-start.57 = (bf16[384,128]{1,0:T(8,128)(2,1)S(1)}, bf16[384,128]{1,0:T(8,128)(2,1)S(1)}, u32[]{:S(2)}, u32[]{:S(2)}) collective-permute-start(bf16[384,128]{1,0:T(8,128)(2,1)S(1)} %get-tuple-element.954), channel_id=1, source_target_pairs={{0,6},{1,7},{2,0},{3,1},{4,2},{5,3},{6,4},{7,5},{8,14},{9,15},{10,... | collective-permute-start | bytes 294920 | tf_op jit(solution)/shard_map/ppermute | solution.py:878
  226.0 14.4 %collective-permute-start.63 = (bf16[256,1024]{1,0:T(8,128)(2,1)S(1)}, bf16[256,1024]{1,0:T(8,128)(2,1)S(1)}, u32[]{:S(2)}, u32[]{:S(2)}) collective-permute-start(bf16[256,1024]{1,0:T(8,128)(2,1)S(1)} %get-tuple-element.989), channel_id=1, source_target_pairs={{0,16},{8,24},{16,0},{24,8},{1,17},{9,25},{17,1},{25,9},{2,18},{10... | collective-permute-start | bytes 1572872 | tf_op jit(solution)/shard_map/ppermute | solution.py:845
  227.1 7.8 %collective-permute-start.64 = (bf16[1024,128]{1,0:T(8,128)(2,1)S(1)}, bf16[1024,128]{1,0:T(8,128)(2,1)S(1)}, u32[]{:S(2)}, u32[]{:S(2)}) collective-permute-start(bf16[1024,128]{1,0:T(8,128)(2,1)S(1)} %get-tuple-element.991), channel_id=1, source_target_pairs={{0,1},{1,0},{2,3},{3,2},{4,5},{5,4},{6,7},{7,6},{8,9},{9,8},{10,11... | collective-permute-start | bytes 786440 | tf_op jit(solution)/shard_map/ppermute | solution.py:873
  228.1 7.6 %collective-permute-start.60 = (bf16[384,128]{1,0:T(8,128)(2,1)S(1)}, bf16[384,128]{1,0:T(8,128)(2,1)S(1)}, u32[]{:S(2)}, u32[]{:S(2)}) collective-permute-start(bf16[384,128]{1,0:T(8,128)(2,1)S(1)} %get-tuple-element.983), channel_id=1, source_target_pairs={{0,2},{1,3},{2,4},{3,5},{4,6},{5,7},{6,0},{7,1},{8,10},{9,11},{10,... | collective-permute-start | bytes 294920 | tf_op jit(solution)/shard_map/ppermute | solution.py:878
  228.6 11.8 %collective-permute-start.61 = (bf16[384,128]{1,0:T(8,128)(2,1)S(1)}, bf16[384,128]{1,0:T(8,128)(2,1)S(1)}, u32[]{:S(2)}, u32[]{:S(2)}) collective-permute-start(bf16[384,128]{1,0:T(8,128)(2,1)S(1)} %get-tuple-element.984), channel_id=1, source_target_pairs={{0,4},{1,5},{2,6},{3,7},{4,0},{5,1},{6,2},{7,3},{8,12},{9,13},{10,... | collective-permute-start | bytes 294920 | tf_op jit(solution)/shard_map/ppermute | solution.py:878
  231.7 8.7 %collective-permute-start.62 = (bf16[384,128]{1,0:T(8,128)(2,1)S(1)}, bf16[384,128]{1,0:T(8,128)(2,1)S(1)}, u32[]{:S(2)}, u32[]{:S(2)}) collective-permute-start(bf16[384,128]{1,0:T(8,128)(2,1)S(1)} %get-tuple-element.985), channel_id=1, source_target_pairs={{0,6},{1,7},{2,0},{3,1},{4,2},{5,3},{6,4},{7,5},{8,14},{9,15},{10,... | collective-permute-start | bytes 294920 | tf_op jit(solution)/shard_map/ppermute | solution.py:878
  242.5 9.7 %collective-permute-start.68 = (bf16[1600,128]{1,0:T(8,128)(2,1)}, bf16[1600,128]{1,0:T(8,128)(2,1)S(1)}, u32[]{:S(2)}, u32[]{:S(2)}) collective-permute-start(bf16[1600,128]{1,0:T(8,128)(2,1)} %get-tuple-element.1023), channel_id=1, source_target_pairs={{0,16},{8,24},{16,0},{24,8},{1,17},{9,25},{17,1},{25,9},{2,18},{10... | collective-permute-start | bytes 1228808 | tf_op jit(solution)/shard_map/ppermute | solution.py:845
  242.9 8.9 %collective-permute-start.65 = (bf16[256,128]{1,0:T(8,128)(2,1)}, bf16[256,128]{1,0:T(8,128)(2,1)S(1)}, u32[]{:S(2)}, u32[]{:S(2)}) collective-permute-start(bf16[256,128]{1,0:T(8,128)(2,1)} %get-tuple-element.1006), channel_id=1, source_target_pairs={{0,2},{1,3},{2,4},{3,5},{4,6},{5,7},{6,0},{7,1},{8,10},{9,11},{10,... | collective-permute-start | bytes 196616 | tf_op jit(solution)/shard_map/ppermute | solution.py:878
  246.2 6.0 %collective-permute-start.66 = (bf16[256,128]{1,0:T(8,128)(2,1)}, bf16[256,128]{1,0:T(8,128)(2,1)}, u32[]{:S(2)}, u32[]{:S(2)}) collective-permute-start(bf16[256,128]{1,0:T(8,128)(2,1)} %get-tuple-element.1007), channel_id=1, source_target_pairs={{0,4},{1,5},{2,6},{3,7},{4,0},{5,1},{6,2},{7,3},{8,12},{9,13},{10,... | collective-permute-start | bytes 196616 | tf_op jit(solution)/shard_map/ppermute | solution.py:878
  246.4 5.8 %collective-permute-start.67 = (bf16[256,128]{1,0:T(8,128)(2,1)}, bf16[256,128]{1,0:T(8,128)(2,1)}, u32[]{:S(2)}, u32[]{:S(2)}) collective-permute-start(bf16[256,128]{1,0:T(8,128)(2,1)} %get-tuple-element.1008), channel_id=1, source_target_pairs={{0,6},{1,7},{2,0},{3,1},{4,2},{5,3},{6,4},{7,5},{8,14},{9,15},{10,... | collective-permute-start | bytes 196616 | tf_op jit(solution)/shard_map/ppermute | solution.py:878
  (103 other events, 776.3 us)
Sparse Core Ops, SparseCore 0:
  40.2 60.7 all-gather.2
  177.0 73.1 reduce-scatter.1

commit v4 on v2

--- a/solution.py
+++ b/solution.py
@@ -921,9 +921,11 @@
     s.gate, s.up = gate_weight, up_weight
     s.fence()
     s.cols = exchange_rel(s.cols)
-    s.ry = [to_y(s.r[0])]
-    s.r.append(to_z(s.r[0]))
-    s.fence()
+    down = after(s.r[0], s.cols[1])
+    down_near, down_next = to_y(down), to_z(down)
+    s.fence()
+    s.ry = [down_near]
+    s.r.append(down_next)
     s.a = [jnp.concatenate([*s.cols, s.orows])]
     del s.cols, s.orows
     s.tok_far[0] = to_chip(s.tok_far[0])

time: 269 us -> 266 us (0.989)
  waiting for transfers between devices: 71.2 us -> 61.2 us
  starting transfers between devices: 56.5 us -> 63.2 us
    ppermute x14, starting transfers between devices: 14.1 us -> 20 us  [to_y(): return lax.ppermute(value, 'dp', [(i, i ^ 1) for i in range(dp)])]
    ppermute x16, waiting for transfers between devices: 26.9 us -> 22.5 us  [to_chip(): return lax.ppermute(value, 'seq', [(i, i ^ 2) for i in range(SEQ)])]
  transfers between devices with their start and end apart: 72 -> 72, of which waited for: 32 -> 30; matrix products, arithmetic and copies ran while one was open for 4% -> 5% of each run, Pallas kernels for 26% -> 27%
where the time goes in v4:
time: 266 us; the launch traced here: 265 us
  Pallas kernels  98.3 us (37%)
  starting transfers between devices  63.2 us (24%)
  waiting for transfers between devices  61.2 us (23%)
  local copies, waits for them, and re-layouts  19.1 us (7%)
  between operations  15.3 us (6%)
  other arithmetic  8.05 us (3%)
    ppermute x16, waiting for transfers between devices, to_chip(): return lax.ppermute(value, 'seq', [(i, i ^ 2) for i in range(SEQ)])  22.5 us
    pallas_call x2, Pallas kernels, attend_back_call(): pl.pallas_call(functools.partial(attend_back_kernel, dp, pieces), name='a...  21.9 us
    pallas_call x1, Pallas kernels, ffn_call(): pl.pallas_call(ffn_kernel, name='ffn', grid_spec=pltpu.PrefetchScalarGrid...  21.2 us
    ppermute x18, starting transfers between devices, to_z(): lax.ppermute(value, 'dp', [(i, (i + 2 * hops) % dp) for i in range(dp)])  21 us
    ppermute x18, waiting for transfers between devices, to_z(): lax.ppermute(value, 'dp', [(i, (i + 2 * hops) % dp) for i in range(dp)])  20 us
    ppermute x14, starting transfers between devices, to_y(): return lax.ppermute(value, 'dp', [(i, i ^ 1) for i in range(dp)])  20 us
    ppermute x16, starting transfers between devices, to_chip(): return lax.ppermute(value, 'seq', [(i, i ^ 2) for i in range(SEQ)])  17.8 us
    unnamed x204, local copies, waits for them, and re-layouts  16.1 us
  transfers between devices with their start and end apart: 72, of which 30 were waited for; matrix products, arithmetic and copies ran while one was open for 5% of the time, Pallas kernels for 27%

profile of v4, /device:TPU:0, one launch (start us, length us, event | category | flops | bytes accessed | tf_op | source)
XLA Modules:
  0.0 265.2 jit_solution(17982834817986869166)
XLA Ops:
  7.2 2.3 pack_attn.1
  10.0 2.6 collective-permute-start.1
  12.7 1.9 collective-permute-start.3
  14.6 1.5 collective-permute-start.5
  18.4 1.6 collective-permute-start.6
  20.1 1.5 collective-permute-start.7
  22.6 3.1 %fusion = (f32[1024,32]{1,0:T(8,128)}, f32[1024,32]{1,0:T(8,128)}, f32[1024,32]{1,0:T(8,128)}) fusion(f32[32]{0:T(128)S(1)} %multiply_exponential_fusion, f32[1024]{0:T(1024)S(1)} %iota_convert_fusion), kind=kLoop, calls=%fused_computation.8 | loop fusion | flops 65536 | bytes 397440 | tf_op jit(solution)/shard_map/neg | solution.py:888
  26.3 2.2 pack_ffn.1
  30.6 1.6 collective-permute-start.8
  34.5 3.4 %pad_maximum_fusion = (f32[1024,128]{1,0:T(8,128)S(1)}, f32[1024,128]{1,0:T(8,128)S(1)}) fusion(f32[1024,32]{1,0:T(8,128)} %get-tuple-element.1062, f32[1024,32]{1,0:T(8,128)} %get-tuple-element.1061, f32[1024,32]{1,0:T(8,128)} %get-tuple-element.1060), kind=kLoop, calls=%fused_computation.2 | loop fusion | flops 786432 | bytes 1441792 | tf_op jit(solution)/shard_map/concatenate | solution.py:888
  40.2 1.6 collective-permute-start.14
  45.4 5.7 %collective-permute-done.13 = bf16[128,1024]{1,0:T(8,128)(2,1)S(1)} collective-permute-done((bf16[128,1024]{1,0:T(8,128)(2,1)}, bf16[128,1024]{1,0:T(8,128)(2,1)S(1)}, u32[]{:S(2)}, u32[]{:S(2)}) %collective-permute-start.13) | collective-permute-done | bytes 262176 | tf_op jit(solution)/shard_map/ppermute | solution.py:847
  51.2 1.3 collective-permute-start.18
  53.0 2.3 collective-permute-start.20
  57.0 2.4 collective-permute-done.18
  59.5 2.6 collective-permute-done.20.refs_7_
  63.2 1.4 collective-permute-start.23
  65.8 3.4 %qkv.1 = (bf16[1024,1024]{1,0:T(8,128)(2,1)S(1)}, bf16[1024,256]{1,0:T(8,128)(2,1)S(1)}, bf16[1024,256]{1,0:T(8,128)(2,1)S(1)}, bf16[1024,256]{1,0:T(8,128)(2,1)S(1)}) custom-call(s32[1]{0:T(128)} %bitcast.5.me_ref, bf16[1024,1024]{1,0:T(8,128)(2,1)S(1)} %constant_dynamic-update-slice_fusion.5.tok_ref, bf16[1024,256]{1,0:T(8,128)(2,1)S(1)} %pad_maximum_fusion.2.first_ref, ...), custom_call_target="tpu_custom_call" | custom-call | tf_op jit(solution)/shard_map/qkv/pallas_call | solution.py:76
  69.2 1.4 copy-done.5
  71.6 1.4 collective-permute-start.30
  73.8 1.6 collective-permute-start.27
  75.4 9.0 %attend.1 = (bf16[1024,256]{1,0:T(8,128)(2,1)S(1)}, f32[2,2,1024]{2,1,0:T(2,128)S(1)}) custom-call(bf16[1024,256]{1,0:T(8,128)(2,1)S(1)} %get-tuple-element.912.q_ref, bf16[1024,256]{1,0:T(8,128)(2,1)S(1)} %get-tuple-element.913.k_ref, bf16[1024,256]{1,0:T(8,128)(2,1)S(1)} %get-tuple-element.914.v_ref, s32[1,1024]{1,0:T(1,128)S(1)} %copy-done.73), custom_call_target="tpu_custom_call" | custom-call | tf_op jit(solution)/shard_map/attend/pallas_call | solution.py:152
  84.5 1.9 collective-permute-done.26.refs_3_
  86.4 5.2 %collective-permute-done.28 = bf16[128,1024]{1,0:T(8,128)(2,1)S(1)} collective-permute-done((bf16[128,1024]{1,0:T(8,128)(2,1)S(1)}, bf16[128,1024]{1,0:T(8,128)(2,1)S(1)}, u32[]{:S(2)}, u32[]{:S(2)}) %collective-permute-start.28) | collective-permute-done | bytes 262176 | tf_op jit(solution)/shard_map/ppermute | solution.py:847
  92.2 1.3 collective-permute-start.35
  93.5 1.8 collective-permute-start.33
  95.5 5.1 %collective-permute-done.33.refs_7_ = bf16[704,128]{1,0:T(8,128)(2,1)S(1)} collective-permute-done((bf16[704,128]{1,0:T(8,128)(2,1)S(1)}, bf16[704,128]{1,0:T(8,128)(2,1)S(1)}, u32[]{:S(2)}, u32[]{:S(2)}) %collective-permute-start.33) | collective-permute-done | bytes 180256 | tf_op jit(solution)/shard_map/ppermute | solution.py:875
  102.7 3.4 %collective-permute-done.35.a2 = bf16[1024,256]{1,0:T(8,128)(2,1)S(1)} collective-permute-done((bf16[1024,256]{1,0:T(8,128)(2,1)S(1)}, bf16[1024,256]{1,0:T(8,128)(2,1)S(1)}, u32[]{:S(2)}, u32[]{:S(2)}) %collective-permute-start.35) | collective-permute-done | bytes 524320 | tf_op jit(solution)/shard_map/ppermute | solution.py:847
  106.1 1.9 collective-permute-done.36.a3
  108.8 21.2 %ffn.1 = (bf16[1024,1024]{1,0:T(8,128)(2,1)}, bf16[1024,704]{1,0:T(8,128)(2,1)}, bf16[1024,1408]{1,0:T(8,128)(2,1)}, f32[256,1024]{1,0:T(8,128)}, bf16[512,1024]...) custom-call(s32[1]{0:T(128)} %bitcast.5.me_ref, ...), custom_call_target="tpu_custom_call" | custom-call | tf_op jit(solution)/shard_map/ffn/pallas_call | solution.py:479
  130.2 2.7 %collective-permute-done.37.refs_1_.got_ref = bf16[512,1024]{1,0:T(8,128)(2,1)S(1)} collective-permute-done((bf16[512,1024]{1,0:T(8,128)(2,1)}, bf16[512,1024]{1,0:T(8,128)(2,1)S(1)}, u32[]{:S(2)}, u32[]{:S(2)}) %collective-permute-start.37) | collective-permute-done | bytes 1048608 | tf_op jit(solution)/shard_map/ppermute | solution.py:843
  135.1 1.3 collective-permute-start.38
  136.4 8.1 %columns_grad.1 = (bf16[1408,128]{1,0:T(8,128)(2,1)}, bf16[1408,128]{1,0:T(8,128)(2,1)}, bf16[1408,128]{1,0:T(8,128)(2,1)}, bf16[1408,128]{1,0:T(8,128)(2,1)}, b...) custom-call(s32[3]{0:T(128)} %pad_add_fusion.place_ref, ...), custom_call_target="tpu_custom_call" | custom-call | tf_op jit(solution)/shard_map/columns_grad/pallas_call | solution.py:539
  144.5 5.6 %down_grad.1 = bf16[704,1024]{1,0:T(8,128)(2,1)} custom-call(bf16[1024,704]{1,0:T(8,128)(2,1)} %get-tuple-element.805.act_ref, bf16[1024,1024]{1,0:T(8,128)(2,1)} %copy-done.81), custom_call_target="tpu_custom_call" | custom-call | tf_op jit(solution)/shard_map/down_grad/pallas_call | solution.py:599
  150.1 1.8 collective-permute-start.39
  156.3 2.9 %branch.1 = (f32[256,1024]{1,0:T(8,128)S(1)}, bf16[256,1024]{1,0:T(8,128)(2,1)}, bf16[256,256]{1,0:T(8,128)(2,1)S(1)}, bf16[256,256]{1,0:T(8,128)(2,1)S(1)}, bf1...) custom-call(bf16[512,1024]{1,0:T(8,128)(2,1)S(1)} %copy-done.23, ...), custom_call_target="tpu_custom_call" | custom-call | tf_op jit(solution)/shard_map/branch/pallas_call | solution.py:619
  161.5 1.3 collective-permute-start.41
  164.8 4.5 %collective-permute-done.43.d2 = bf16[256,256]{1,0:T(8,128)(2,1)S(1)} collective-permute-done((bf16[256,256]{1,0:T(8,128)(2,1)S(1)}, bf16[256,256]{1,0:T(8,128)(2,1)S(1)}, u32[]{:S(2)}, u32[]{:S(2)}) %collective-permute-start.43) | collective-permute-done | bytes 131104 | tf_op jit(solution)/shard_map/ppermute | solution.py:847
  169.3 1.9 collective-permute-done.44.d3
  171.9 2.4 collective-permute-done.45.refs_2_
  175.1 1.2 collective-permute-start.46
  176.9 11.1 %attend_back.2 = (bf16[1024,384]{1,0:T(8,128)(2,1)}, bf16[4,384,128]{2,1,0:T(8,128)(2,1)}, bf16[2944,128]{1,0:T(8,128)(2,1)}) custom-call(s32[3]{0:T(128)} %pad_add_fusion.place_ref, bf16[1024,256]{1,0:T(8,128)(2,1)} %copy-done.10, bf16[1024,256]{1,0:T(8,128)(2,1)} %copy-done.11, bf16[1024,256]{1,0:T(8,128)(2,1)} %copy-done.12, bf16[256,256]{1,0:T(8,128)(2,1)} %copy-done.42, ...), custom_call_target="tpu_custom_call" | custom-call | tf_op jit(solution)/shard_map/attend_back/pallas_call | solution.py:236
  187.9 1.5 collective-permute-done.49.refs_2_
  190.6 1.3 collective-permute-start.51
  194.5 10.9 %attend_back.3 = (bf16[1024,384]{1,0:T(8,128)(2,1)}, bf16[4,384,128]{2,1,0:T(8,128)(2,1)}, bf16[1536,128]{1,0:T(8,128)(2,1)}) custom-call(s32[3]{0:T(128)} %pad_add_fusion.place_ref, bf16[1024,256]{1,0:T(8,128)(2,1)} %copy-done.10, bf16[1024,256]{1,0:T(8,128)(2,1)} %copy-done.11, bf16[1024,256]{1,0:T(8,128)(2,1)} %copy-done.12, bf16[256,256]{1,0:T(8,128)(2,1)} %copy-done.42, ...), custom_call_target="tpu_custom_call" | custom-call | tf_op jit(solution)/shard_map/attend_back/pallas_call | solution.py:236
  206.5 2.7 %input_grad.1 = (bf16[512,1024]{1,0:T(8,128)(2,1)S(1)}, bf16[512,1024]{1,0:T(8,128)(2,1)S(1)}) custom-call(s32[1]{0:T(128)} %bitcast.5.me_ref, bf16[1024,384]{1,0:T(8,128)(2,1)S(1)} %copy-done.6, bf16[1024,384]{1,0:T(8,128)(2,1)S(1)} %copy-done, bf16[1024,768]{1,0:T(8,128)(2,1)S(1)} %copy-done.8), custom_call_target="tpu_custom_call" | custom-call | tf_op jit(solution)/shard_map/input_grad/pallas_call | solution.py:828
  209.2 2.0 collective-permute-done.52.refs_10_
  211.3 1.6 collective-permute-start.58
  213.1 2.6 collective-permute-start.56
  215.7 1.4 collective-permute-start.57
  217.2 2.2 out_projection_grad.1
  220.7 3.3 %collective-permute-done.56.refs_2_ = bf16[384,128]{1,0:T(8,128)(2,1)S(1)} collective-permute-done((bf16[384,128]{1,0:T(8,128)(2,1)S(1)}, bf16[384,128]{1,0:T(8,128)(2,1)S(1)}, u32[]{:S(2)}, u32[]{:S(2)}) %collective-permute-start.56) | collective-permute-done | bytes 98336 | tf_op jit(solution)/shard_map/ppermute | solution.py:880
  225.0 1.3 collective-permute-start.63
  226.3 1.7 collective-permute-start.64
  228.5 2.1 collective-permute-start.61
  230.7 1.9 collective-permute-start.62
  232.6 2.1 layer_out.1
  235.9 4.6 %collective-permute-done.61.refs_6_ = bf16[384,128]{1,0:T(8,128)(2,1)S(1)} collective-permute-done((bf16[384,128]{1,0:T(8,128)(2,1)S(1)}, bf16[384,128]{1,0:T(8,128)(2,1)S(1)}, u32[]{:S(2)}, u32[]{:S(2)}) %collective-permute-start.61) | collective-permute-done | bytes 98336 | tf_op jit(solution)/shard_map/ppermute | solution.py:880
  240.6 2.1 cut.1
  243.2 2.6 collective-permute-start.65
  245.8 1.7 collective-permute-start.66
  248.2 3.2 %token_grad.1 = bf16[256,1024]{1,0:T(8,128)(2,1)} custom-call(bf16[512,1024]{1,0:T(8,128)(2,1)} %copy-done.20, bf16[512,1024]{1,0:T(8,128)(2,1)} %copy-done.21, bf16[256,1024]{1,0:T(8,128)(2,1)} %copy-done.90, bf16[256,1024]{1,0:T(8,128)(2,1)} %bitcast.31, f32[1,1024]{1,0:T(1,128)} %bitcast.23, f32[256,1024]{1,0:T(8,128)} %copy-done.39), custom_call_target="tpu_custom_call" | custom-call | tf_op jit(solution)/shard_map/token_grad/pallas_call | solution.py:619
  252.7 1.9 collective-permute-done.69.got_ref
  256.0 2.3 finish.1
  (330 shorter events, 50.5 us)
Async XLA Ops:
  7.2 100.8 %all-gather.3.cloned.1.call-start = ((), (), s32[]{:S(2)}) async-start(), calls=%async_computation.2 | async-start | bytes 3244032 | tf_op jit(solution)/shard_map/all_gather | solution.py:943
  10.0 6.0 %collective-permute-start.1 = (bf16[208,128]{1,0:T(8,128)(2,1)}, bf16[208,128]{1,0:T(8,128)(2,1)S(1)}, u32[]{:S(2)}, u32[]{:S(2)}) collective-permute-start(bf16[208,128]{1,0:T(8,128)(2,1)} %get-tuple-element.543), channel_id=1, source_target_pairs={{0,16},{8,24},{16,0},{24,8},{1,17},{9,25},{17,1},{25,9},{2,18},{10... | collective-permute-start | bytes 159752 | tf_op jit(solution)/shard_map/ppermute | solution.py:847
  12.7 15.8 %collective-permute-start.3 = (bf16[704,128]{1,0:T(8,128)(2,1)}, bf16[704,128]{1,0:T(8,128)(2,1)S(1)}, u32[]{:S(2)}, u32[]{:S(2)}) collective-permute-start(bf16[704,128]{1,0:T(8,128)(2,1)} %get-tuple-element.705.refs_0_), channel_id=1, source_target_pairs={{0,2},{1,3},{2,4},{3,5},{4,6},{5,7},{6,0},{7,1},{8,10},{9,11},{10,... | collective-permute-start | bytes 540680 | tf_op jit(solution)/shard_map/ppermute | solution.py:880
  14.6 14.0 %collective-permute-start.5 = (bf16[704,128]{1,0:T(8,128)(2,1)}, bf16[704,128]{1,0:T(8,128)(2,1)S(1)}, u32[]{:S(2)}, u32[]{:S(2)}) collective-permute-start(bf16[704,128]{1,0:T(8,128)(2,1)} %get-tuple-element.705.refs_0_), channel_id=1, source_target_pairs={{0,1},{1,0},{2,3},{3,2},{4,5},{5,4},{6,7},{7,6},{8,9},{9,8},{10,11... | collective-permute-start | bytes 540680 | tf_op jit(solution)/shard_map/ppermute | solution.py:875
  18.4 11.4 %collective-permute-start.6 = (bf16[1088,128]{1,0:T(8,128)(2,1)S(1)}, bf16[1088,128]{1,0:T(8,128)(2,1)S(1)}, u32[]{:S(2)}, u32[]{:S(2)}) collective-permute-start(bf16[1088,128]{1,0:T(8,128)(2,1)S(1)} %constant_dynamic-update-slice_fusion.refs_0_), channel_id=1, source_target_pairs={{0,2},{1,3},{2,4},{3,5},{4,6},{5,7},{6,0},{7,1},{8,10},{9,11},{10,... | collective-permute-start | bytes 835592 | tf_op jit(solution)/shard_map/ppermute | solution.py:880
  20.1 9.7 %collective-permute-start.7 = (bf16[1088,128]{1,0:T(8,128)(2,1)S(1)}, bf16[1088,128]{1,0:T(8,128)(2,1)S(1)}, u32[]{:S(2)}, u32[]{:S(2)}) collective-permute-start(bf16[1088,128]{1,0:T(8,128)(2,1)S(1)} %constant_dynamic-update-slice_fusion.refs_0_), channel_id=1, source_target_pairs={{0,1},{1,0},{2,3},{3,2},{4,5},{5,4},{6,7},{7,6},{8,9},{9,8},{10,11... | collective-permute-start | bytes 835592 | tf_op jit(solution)/shard_map/ppermute | solution.py:875
  21.6 8.2 %collective-permute-start.4 = (bf16[128,1024]{1,0:T(8,128)(2,1)}, bf16[128,1024]{1,0:T(8,128)(2,1)S(1)}, u32[]{:S(2)}, u32[]{:S(2)}) collective-permute-start(bf16[128,1024]{1,0:T(8,128)(2,1)} %get-tuple-element.557), channel_id=1, source_target_pairs={{0,16},{8,24},{16,0},{24,8},{1,17},{9,25},{17,1},{25,9},{2,18},{10... | collective-permute-start | bytes 786440 | tf_op jit(solution)/shard_map/ppermute | solution.py:847
  30.6 9.5 %collective-permute-start.8 = (bf16[1088,128]{1,0:T(8,128)(2,1)S(1)}, bf16[1088,128]{1,0:T(8,128)(2,1)S(1)}, u32[]{:S(2)}, u32[]{:S(2)}) collective-permute-start(bf16[1088,128]{1,0:T(8,128)(2,1)S(1)} %collective-permute-done.6.refs_1_), channel_id=1, source_target_pairs={{0,2},{1,3},{2,4},{3,5},{4,6},{5,7},{6,0},{7,1},{8,10},{9,11},{10,... | collective-permute-start | bytes 835592 | tf_op jit(solution)/shard_map/ppermute | solution.py:880
  32.1 7.9 %collective-permute-start.9 = (bf16[1088,128]{1,0:T(8,128)(2,1)S(1)}, bf16[1088,128]{1,0:T(8,128)(2,1)S(1)}, u32[]{:S(2)}, u32[]{:S(2)}) collective-permute-start(bf16[1088,128]{1,0:T(8,128)(2,1)S(1)} %collective-permute-done.6.refs_1_), channel_id=1, source_target_pairs={{0,1},{1,0},{2,3},{3,2},{4,5},{5,4},{6,7},{7,6},{8,9},{9,8},{10,11... | collective-permute-start | bytes 835592 | tf_op jit(solution)/shard_map/ppermute | solution.py:875
  32.6 5.3 %collective-permute-start.12 = (bf16[352,128]{1,0:T(8,128)(2,1)}, bf16[352,128]{1,0:T(8,128)(2,1)S(1)}, u32[]{:S(2)}, u32[]{:S(2)}) collective-permute-start(bf16[352,128]{1,0:T(8,128)(2,1)} %get-tuple-element.589), channel_id=1, source_target_pairs={{0,24},{8,16},{16,8},{24,0},{1,25},{9,17},{17,9},{25,1},{2,26},{10... | collective-permute-start | bytes 270344 | tf_op jit(solution)/shard_map/ppermute | solution.py:851
  32.6 6.0 %collective-permute-start.11 = (bf16[352,128]{1,0:T(8,128)(2,1)}, bf16[352,128]{1,0:T(8,128)(2,1)S(1)}, u32[]{:S(2)}, u32[]{:S(2)}) collective-permute-start(bf16[352,128]{1,0:T(8,128)(2,1)} %get-tuple-element.588), channel_id=1, source_target_pairs={{0,16},{8,24},{16,0},{24,8},{1,17},{9,25},{17,1},{25,9},{2,18},{10... | collective-permute-start | bytes 270344 | tf_op jit(solution)/shard_map/ppermute | solution.py:847
  33.6 5.1 %collective-permute-start.10 = (bf16[352,128]{1,0:T(8,128)(2,1)}, bf16[352,128]{1,0:T(8,128)(2,1)S(1)}, u32[]{:S(2)}, u32[]{:S(2)}) collective-permute-start(bf16[352,128]{1,0:T(8,128)(2,1)} %get-tuple-element.587), channel_id=1, source_target_pairs={{0,8},{8,0},{16,24},{24,16},{1,9},{9,1},{17,25},{25,17},{2,10},{10... | collective-permute-start | bytes 270344 | tf_op jit(solution)/shard_map/ppermute | solution.py:843
  40.1 211.4 %reduce-scatter.2.cloned.1.call-start = ((), (), s32[]{:S(2)}) async-start(), calls=%async_computation.1 | async-start | bytes 1622016 | tf_op jit(solution)/shard_map/reduce_scatter | solution.py:995
  40.1 11.0 %collective-permute-start.16 = (bf16[256,1024]{1,0:T(8,128)(2,1)S(1)}, bf16[256,1024]{1,0:T(8,128)(2,1)}, u32[]{:S(2)}, u32[]{:S(2)}) collective-permute-start(bf16[256,1024]{1,0:T(8,128)(2,1)S(1)} %bitcast.32), channel_id=1, source_target_pairs={{0,8},{8,0},{16,24},{24,16},{1,9},{9,1},{17,25},{25,17},{2,10},{10... | collective-permute-start | bytes 1572872 | tf_op jit(solution)/shard_map/ppermute | solution.py:843
  40.2 10.9 %collective-permute-start.14 = (bf16[1088,128]{1,0:T(8,128)(2,1)S(1)}, bf16[1088,128]{1,0:T(8,128)(2,1)S(1)}, u32[]{:S(2)}, u32[]{:S(2)}) collective-permute-start(bf16[1088,128]{1,0:T(8,128)(2,1)S(1)} %collective-permute-done.8.refs_2_), channel_id=1, source_target_pairs={{0,2},{1,3},{2,4},{3,5},{4,6},{5,7},{6,0},{7,1},{8,10},{9,11},{10,... | collective-permute-start | bytes 835592 | tf_op jit(solution)/shard_map/ppermute | solution.py:880
  41.8 9.4 %collective-permute-start.15 = (bf16[1088,128]{1,0:T(8,128)(2,1)S(1)}, bf16[1088,128]{1,0:T(8,128)(2,1)S(1)}, u32[]{:S(2)}, u32[]{:S(2)}) collective-permute-start(bf16[1088,128]{1,0:T(8,128)(2,1)S(1)} %collective-permute-done.8.refs_2_), channel_id=1, source_target_pairs={{0,1},{1,0},{2,3},{3,2},{4,5},{5,4},{6,7},{7,6},{8,9},{9,8},{10,11... | collective-permute-start | bytes 835592 | tf_op jit(solution)/shard_map/ppermute | solution.py:875
  43.0 8.1 %collective-permute-start.13 = (bf16[128,1024]{1,0:T(8,128)(2,1)}, bf16[128,1024]{1,0:T(8,128)(2,1)S(1)}, u32[]{:S(2)}, u32[]{:S(2)}) collective-permute-start(bf16[128,1024]{1,0:T(8,128)(2,1)} %get-tuple-element.593), channel_id=1, source_target_pairs={{0,16},{8,24},{16,0},{24,8},{1,17},{9,25},{17,1},{25,9},{2,18},{10... | collective-permute-start | bytes 786440 | tf_op jit(solution)/shard_map/ppermute | solution.py:847
  51.2 5.8 %collective-permute-start.19 = (bf16[256,256]{1,0:T(8,128)(2,1)S(1)}, bf16[256,256]{1,0:T(8,128)(2,1)S(1)}, u32[]{:S(2)}, u32[]{:S(2)}) collective-permute-start(bf16[256,256]{1,0:T(8,128)(2,1)S(1)} %get-tuple-element.612), channel_id=1, source_target_pairs={{0,24},{8,16},{16,8},{24,0},{1,25},{9,17},{17,9},{25,1},{2,26},{10... | collective-permute-start | bytes 393224 | tf_op jit(solution)/shard_map/ppermute | solution.py:851
  51.2 8.2 %collective-permute-start.18 = (bf16[256,256]{1,0:T(8,128)(2,1)S(1)}, bf16[256,256]{1,0:T(8,128)(2,1)S(1)}, u32[]{:S(2)}, u32[]{:S(2)}) collective-permute-start(bf16[256,256]{1,0:T(8,128)(2,1)S(1)} %get-tuple-element.611), channel_id=1, source_target_pairs={{0,16},{8,24},{16,0},{24,8},{1,17},{9,25},{17,1},{25,9},{2,18},{10... | collective-permute-start | bytes 393224 | tf_op jit(solution)/shard_map/ppermute | solution.py:847
  52.5 6.9 %collective-permute-start.17 = (bf16[256,256]{1,0:T(8,128)(2,1)S(1)}, bf16[256,256]{1,0:T(8,128)(2,1)S(1)}, u32[]{:S(2)}, u32[]{:S(2)}) collective-permute-start(bf16[256,256]{1,0:T(8,128)(2,1)S(1)} %get-tuple-element.610), channel_id=1, source_target_pairs={{0,8},{8,0},{16,24},{24,16},{1,9},{9,1},{17,25},{25,17},{2,10},{10... | collective-permute-start | bytes 393224 | tf_op jit(solution)/shard_map/ppermute | solution.py:843
  53.0 9.1 %collective-permute-start.20 = (bf16[1088,128]{1,0:T(8,128)(2,1)S(1)}, bf16[1088,128]{1,0:T(8,128)(2,1)S(1)}, u32[]{:S(2)}, u32[]{:S(2)}) collective-permute-start(bf16[1088,128]{1,0:T(8,128)(2,1)S(1)} %collective-permute-done.14.refs_3_), channel_id=1, source_target_pairs={{0,1},{1,0},{2,3},{3,2},{4,5},{5,4},{6,7},{7,6},{8,9},{9,8},{10,11... | collective-permute-start | bytes 835592 | tf_op jit(solution)/shard_map/ppermute | solution.py:875
  62.2 9.3 %collective-permute-start.25 = (bf16[256,1024]{1,0:T(8,128)(2,1)S(1)}, bf16[256,1024]{1,0:T(8,128)(2,1)S(1)}, u32[]{:S(2)}, u32[]{:S(2)}) collective-permute-start(bf16[256,1024]{1,0:T(8,128)(2,1)S(1)} %bitcast.18), channel_id=1, source_target_pairs={{0,8},{8,0},{16,24},{24,16},{1,9},{9,1},{17,25},{25,17},{2,10},{10... | collective-permute-start | bytes 1572872 | tf_op jit(solution)/shard_map/ppermute | solution.py:843
  62.2 9.3 %collective-permute-start.24 = (bf16[128,1024]{1,0:T(8,128)(2,1)S(1)}, bf16[128,1024]{1,0:T(8,128)(2,1)S(1)}, u32[]{:S(2)}, u32[]{:S(2)}) collective-permute-start(bf16[128,1024]{1,0:T(8,128)(2,1)S(1)} %get-tuple-element.638), channel_id=1, source_target_pairs={{0,16},{8,24},{16,0},{24,8},{1,17},{9,25},{17,1},{25,9},{2,18},{10... | collective-permute-start | bytes 786440 | tf_op jit(solution)/shard_map/ppermute | solution.py:847
  62.9 8.6 %collective-permute-start.22 = (bf16[704,128]{1,0:T(8,128)(2,1)S(1)}, bf16[704,128]{1,0:T(8,128)(2,1)S(1)}, u32[]{:S(2)}, u32[]{:S(2)}) collective-permute-start(bf16[704,128]{1,0:T(8,128)(2,1)S(1)} %copy-done.64), channel_id=1, source_target_pairs={{0,2},{1,3},{2,4},{3,5},{4,6},{5,7},{6,0},{7,1},{8,10},{9,11},{10,... | collective-permute-start | bytes 540680 | tf_op jit(solution)/shard_map/ppermute | solution.py:880
  63.2 8.2 %collective-permute-start.23 = (bf16[704,128]{1,0:T(8,128)(2,1)S(1)}, bf16[704,128]{1,0:T(8,128)(2,1)S(1)}, u32[]{:S(2)}, u32[]{:S(2)}) collective-permute-start(bf16[704,128]{1,0:T(8,128)(2,1)S(1)} %copy-done.64), channel_id=1, source_target_pairs={{0,1},{1,0},{2,3},{3,2},{4,5},{5,4},{6,7},{7,6},{8,9},{9,8},{10,11... | collective-permute-start | bytes 540680 | tf_op jit(solution)/shard_map/ppermute | solution.py:875
  71.5 20.0 %collective-permute-start.29 = (bf16[256,1024]{1,0:T(8,128)(2,1)S(1)}, bf16[256,1024]{1,0:T(8,128)(2,1)S(1)}, u32[]{:S(2)}, u32[]{:S(2)}) collective-permute-start(bf16[256,1024]{1,0:T(8,128)(2,1)S(1)} %get-tuple-element.835.wo0.w0), channel_id=1, source_target_pairs={{0,8},{8,0},{16,24},{24,16},{1,9},{9,1},{17,25},{25,17},{2,10},{10... | collective-permute-start | bytes 1572872 | tf_op jit(solution)/shard_map/ppermute | solution.py:843
  71.6 20.0 %collective-permute-start.30 = (bf16[256,1024]{1,0:T(8,128)(2,1)S(1)}, bf16[256,1024]{1,0:T(8,128)(2,1)S(1)}, u32[]{:S(2)}, u32[]{:S(2)}) collective-permute-start(bf16[256,1024]{1,0:T(8,128)(2,1)S(1)} %get-tuple-element.835.wo0.w0), channel_id=1, source_target_pairs={{0,16},{8,24},{16,0},{24,8},{1,17},{9,25},{17,1},{25,9},{2,18},{10... | collective-permute-start | bytes 1572872 | tf_op jit(solution)/shard_map/ppermute | solution.py:847
  72.9 18.6 %collective-permute-start.28 = (bf16[128,1024]{1,0:T(8,128)(2,1)S(1)}, bf16[128,1024]{1,0:T(8,128)(2,1)S(1)}, u32[]{:S(2)}, u32[]{:S(2)}) collective-permute-start(bf16[128,1024]{1,0:T(8,128)(2,1)S(1)} %get-tuple-element.669), channel_id=1, source_target_pairs={{0,16},{8,24},{16,0},{24,8},{1,17},{9,25},{17,1},{25,9},{2,18},{10... | collective-permute-start | bytes 786440 | tf_op jit(solution)/shard_map/ppermute | solution.py:847
  73.7 12.7 %collective-permute-start.26 = (bf16[704,128]{1,0:T(8,128)(2,1)S(1)}, bf16[704,128]{1,0:T(8,128)(2,1)S(1)}, u32[]{:S(2)}, u32[]{:S(2)}) collective-permute-start(bf16[704,128]{1,0:T(8,128)(2,1)S(1)} %collective-permute-done.22.refs_2_), channel_id=1, source_target_pairs={{0,2},{1,3},{2,4},{3,5},{4,6},{5,7},{6,0},{7,1},{8,10},{9,11},{10,... | collective-permute-start | bytes 540680 | tf_op jit(solution)/shard_map/ppermute | solution.py:880
  73.8 12.5 %collective-permute-start.27 = (bf16[704,128]{1,0:T(8,128)(2,1)S(1)}, bf16[704,128]{1,0:T(8,128)(2,1)S(1)}, u32[]{:S(2)}, u32[]{:S(2)}) collective-permute-start(bf16[704,128]{1,0:T(8,128)(2,1)S(1)} %collective-permute-done.22.refs_2_), channel_id=1, source_target_pairs={{0,1},{1,0},{2,3},{3,2},{4,5},{5,4},{6,7},{7,6},{8,9},{9,8},{10,11... | collective-permute-start | bytes 540680 | tf_op jit(solution)/shard_map/ppermute | solution.py:875
  91.6 11.0 %collective-permute-start.31 = (bf16[256,1024]{1,0:T(8,128)(2,1)S(1)}, bf16[256,1024]{1,0:T(8,128)(2,1)S(1)}, u32[]{:S(2)}, u32[]{:S(2)}) collective-permute-start(bf16[256,1024]{1,0:T(8,128)(2,1)S(1)} %pad_maximum_fusion.4), channel_id=1, source_target_pairs={{0,8},{8,0},{16,24},{24,16},{1,9},{9,1},{17,25},{25,17},{2,10},{10... | collective-permute-start | bytes 1572872 | tf_op jit(solution)/shard_map/ppermute | solution.py:843
  91.7 11.0 %collective-permute-start.34 = (bf16[1024,256]{1,0:T(8,128)(2,1)S(1)}, bf16[1024,256]{1,0:T(8,128)(2,1)S(1)}, u32[]{:S(2)}, u32[]{:S(2)}) collective-permute-start(bf16[1024,256]{1,0:T(8,128)(2,1)S(1)} %get-tuple-element.965.a0.act_ref), channel_id=1, source_target_pairs={{0,8},{8,0},{16,24},{24,16},{1,9},{9,1},{17,25},{25,17},{2,10},{10... | collective-permute-start | bytes 1572872 | tf_op jit(solution)/shard_map/ppermute | solution.py:843
  92.2 13.9 %collective-permute-start.35 = (bf16[1024,256]{1,0:T(8,128)(2,1)S(1)}, bf16[1024,256]{1,0:T(8,128)(2,1)S(1)}, u32[]{:S(2)}, u32[]{:S(2)}) collective-permute-start(bf16[1024,256]{1,0:T(8,128)(2,1)S(1)} %get-tuple-element.965.a0.act_ref), channel_id=1, source_target_pairs={{0,16},{8,24},{16,0},{24,8},{1,17},{9,25},{17,1},{25,9},{2,18},{10... | collective-permute-start | bytes 1572872 | tf_op jit(solution)/shard_map/ppermute | solution.py:847
  93.5 9.2 %collective-permute-start.32 = (bf16[256,1024]{1,0:T(8,128)(2,1)S(1)}, bf16[256,1024]{1,0:T(8,128)(2,1)S(1)}, u32[]{:S(2)}, u32[]{:S(2)}) collective-permute-start(bf16[256,1024]{1,0:T(8,128)(2,1)S(1)} %collective-permute-done.30.wo2.w2), channel_id=1, source_target_pairs={{0,8},{8,0},{16,24},{24,16},{1,9},{9,1},{17,25},{25,17},{2,10},{10... | collective-permute-start | bytes 1572872 | tf_op jit(solution)/shard_map/ppermute | solution.py:843
  93.5 7.1 %collective-permute-start.33 = (bf16[704,128]{1,0:T(8,128)(2,1)S(1)}, bf16[704,128]{1,0:T(8,128)(2,1)S(1)}, u32[]{:S(2)}, u32[]{:S(2)}) collective-permute-start(bf16[704,128]{1,0:T(8,128)(2,1)S(1)} %collective-permute-done.26.refs_3_), channel_id=1, source_target_pairs={{0,1},{1,0},{2,3},{3,2},{4,5},{5,4},{6,7},{7,6},{8,9},{9,8},{10,11... | collective-permute-start | bytes 540680 | tf_op jit(solution)/shard_map/ppermute | solution.py:875
  135.1 15.0 %collective-permute-start.38 = (bf16[256,1024]{1,0:T(8,128)(2,1)}, bf16[256,1024]{1,0:T(8,128)(2,1)}, u32[]{:S(2)}, u32[]{:S(2)}) collective-permute-start(bf16[256,1024]{1,0:T(8,128)(2,1)} %lower.3), channel_id=1, source_target_pairs={{0,16},{8,24},{16,0},{24,8},{1,17},{9,25},{17,1},{25,9},{2,18},{10... | collective-permute-start | bytes 1572872 | tf_op jit(solution)/shard_map/ppermute | solution.py:847
  150.1 10.1 %collective-permute-start.40 = (bf16[512,1024]{1,0:T(8,128)(2,1)}, bf16[512,1024]{1,0:T(8,128)(2,1)S(1)}, u32[]{:S(2)}, u32[]{:S(2)}) collective-permute-start(bf16[512,1024]{1,0:T(8,128)(2,1)} %get-tuple-element.831), channel_id=1, source_target_pairs={{0,8},{8,0},{16,24},{24,16},{1,9},{9,1},{17,25},{25,17},{2,10},{10... | collective-permute-start | bytes 3145736 | tf_op jit(solution)/shard_map/ppermute | solution.py:843
  150.1 11.1 %collective-permute-start.39 = (bf16[1408,128]{1,0:T(8,128)(2,1)S(1)}, bf16[1408,128]{1,0:T(8,128)(2,1)S(1)}, u32[]{:S(2)}, u32[]{:S(2)}) collective-permute-start(bf16[1408,128]{1,0:T(8,128)(2,1)S(1)} %copy-done.95), channel_id=1, source_target_pairs={{0,1},{1,0},{2,3},{3,2},{4,5},{5,4},{6,7},{7,6},{8,9},{9,8},{10,11... | collective-permute-start | bytes 1081352 | tf_op jit(solution)/shard_map/ppermute | solution.py:875
  161.5 10.5 %collective-permute-start.41 = (bf16[1408,128]{1,0:T(8,128)(2,1)S(1)}, bf16[1408,128]{1,0:T(8,128)(2,1)S(1)}, u32[]{:S(2)}, u32[]{:S(2)}) collective-permute-start(bf16[1408,128]{1,0:T(8,128)(2,1)S(1)} %copy-done.94), channel_id=1, source_target_pairs={{0,1},{1,0},{2,3},{3,2},{4,5},{5,4},{6,7},{7,6},{8,9},{9,8},{10,11... | collective-permute-start | bytes 1081352 | tf_op jit(solution)/shard_map/ppermute | solution.py:875
  162.8 11.5 %collective-permute-start.45 = (bf16[1408,128]{1,0:T(8,128)(2,1)S(1)}, bf16[1408,128]{1,0:T(8,128)(2,1)S(1)}, u32[]{:S(2)}, u32[]{:S(2)}) collective-permute-start(bf16[1408,128]{1,0:T(8,128)(2,1)S(1)} %total.3), channel_id=1, source_target_pairs={{0,2},{1,3},{2,4},{3,5},{4,6},{5,7},{6,0},{7,1},{8,10},{9,11},{10,... | collective-permute-start | bytes 1081352 | tf_op jit(solution)/shard_map/ppermute | solution.py:880
  163.0 6.4 %collective-permute-start.43 = (bf16[256,256]{1,0:T(8,128)(2,1)S(1)}, bf16[256,256]{1,0:T(8,128)(2,1)S(1)}, u32[]{:S(2)}, u32[]{:S(2)}) collective-permute-start(bf16[256,256]{1,0:T(8,128)(2,1)S(1)} %get-tuple-element.872), channel_id=1, source_target_pairs={{0,16},{8,24},{16,0},{24,8},{1,17},{9,25},{17,1},{25,9},{2,18},{10... | collective-permute-start | bytes 393224 | tf_op jit(solution)/shard_map/ppermute | solution.py:847
  163.8 7.5 %collective-permute-start.44 = (bf16[256,256]{1,0:T(8,128)(2,1)S(1)}, bf16[256,256]{1,0:T(8,128)(2,1)S(1)}, u32[]{:S(2)}, u32[]{:S(2)}) collective-permute-start(bf16[256,256]{1,0:T(8,128)(2,1)S(1)} %get-tuple-element.873), channel_id=1, source_target_pairs={{0,24},{8,16},{16,8},{24,0},{1,25},{9,17},{17,9},{25,1},{2,26},{10... | collective-permute-start | bytes 393224 | tf_op jit(solution)/shard_map/ppermute | solution.py:851
  174.4 15.0 %collective-permute-start.47 = (bf16[256,1024]{1,0:T(8,128)(2,1)}, bf16[256,1024]{1,0:T(8,128)(2,1)S(1)}, u32[]{:S(2)}, u32[]{:S(2)}) collective-permute-start(bf16[256,1024]{1,0:T(8,128)(2,1)} %get-tuple-element.966.d0), channel_id=1, source_target_pairs={{0,8},{8,0},{16,24},{24,16},{1,9},{9,1},{17,25},{25,17},{2,10},{10... | collective-permute-start | bytes 1572872 | tf_op jit(solution)/shard_map/ppermute | solution.py:843
  174.4 15.8 %collective-permute-start.48 = (bf16[256,1024]{1,0:T(8,128)(2,1)}, bf16[256,1024]{1,0:T(8,128)(2,1)}, u32[]{:S(2)}, u32[]{:S(2)}) collective-permute-start(bf16[256,1024]{1,0:T(8,128)(2,1)} %get-tuple-element.966.d0), channel_id=1, source_target_pairs={{0,16},{8,24},{16,0},{24,8},{1,17},{9,25},{17,1},{25,9},{2,18},{10... | collective-permute-start | bytes 1572872 | tf_op jit(solution)/shard_map/ppermute | solution.py:847
  175.1 12.8 %collective-permute-start.46 = (bf16[1408,128]{1,0:T(8,128)(2,1)S(1)}, bf16[1408,128]{1,0:T(8,128)(2,1)S(1)}, u32[]{:S(2)}, u32[]{:S(2)}) collective-permute-start(bf16[1408,128]{1,0:T(8,128)(2,1)S(1)} %copy-done.93), channel_id=1, source_target_pairs={{0,1},{1,0},{2,3},{3,2},{4,5},{5,4},{6,7},{7,6},{8,9},{9,8},{10,11... | collective-permute-start | bytes 1081352 | tf_op jit(solution)/shard_map/ppermute | solution.py:875
  176.5 12.9 %collective-permute-start.49 = (bf16[1408,128]{1,0:T(8,128)(2,1)S(1)}, bf16[1408,128]{1,0:T(8,128)(2,1)S(1)}, u32[]{:S(2)}, u32[]{:S(2)}) collective-permute-start(bf16[1408,128]{1,0:T(8,128)(2,1)S(1)} %total.4), channel_id=1, source_target_pairs={{0,2},{1,3},{2,4},{3,5},{4,6},{5,7},{6,0},{7,1},{8,10},{9,11},{10,... | collective-permute-start | bytes 1081352 | tf_op jit(solution)/shard_map/ppermute | solution.py:880
  190.2 21.0 %collective-permute-start.53 = (bf16[2944,128]{1,0:T(8,128)(2,1)}, bf16[2944,128]{1,0:T(8,128)(2,1)S(1)}, u32[]{:S(2)}, u32[]{:S(2)}) collective-permute-start(bf16[2944,128]{1,0:T(8,128)(2,1)} %get-tuple-element.938), channel_id=1, source_target_pairs={{0,1},{1,0},{2,3},{3,2},{4,5},{5,4},{6,7},{7,6},{8,9},{9,8},{10,11... | collective-permute-start | bytes 2261000 | tf_op jit(solution)/shard_map/ppermute | solution.py:875
  190.6 20.6 %collective-permute-start.50 = (bf16[256,1024]{1,0:T(8,128)(2,1)}, bf16[256,1024]{1,0:T(8,128)(2,1)}, u32[]{:S(2)}, u32[]{:S(2)}) collective-permute-start(bf16[256,1024]{1,0:T(8,128)(2,1)} %collective-permute-done.48.d2), channel_id=1, source_target_pairs={{0,8},{8,0},{16,24},{24,16},{1,9},{9,1},{17,25},{25,17},{2,10},{10... | collective-permute-start | bytes 1572872 | tf_op jit(solution)/shard_map/ppermute | solution.py:843
  190.6 20.6 %collective-permute-start.51 = (bf16[256,1024]{1,0:T(8,128)(2,1)}, bf16[256,1024]{1,0:T(8,128)(2,1)}, u32[]{:S(2)}, u32[]{:S(2)}) collective-permute-start(bf16[256,1024]{1,0:T(8,128)(2,1)} %lower.4), channel_id=1, source_target_pairs={{0,16},{8,24},{16,0},{24,8},{1,17},{9,25},{17,1},{25,9},{2,18},{10... | collective-permute-start | bytes 1572872 | tf_op jit(solution)/shard_map/ppermute | solution.py:847
  192.7 18.5 %collective-permute-start.52 = (bf16[1408,128]{1,0:T(8,128)(2,1)}, bf16[1408,128]{1,0:T(8,128)(2,1)}, u32[]{:S(2)}, u32[]{:S(2)}) collective-permute-start(bf16[1408,128]{1,0:T(8,128)(2,1)} %total.5), channel_id=1, source_target_pairs={{0,2},{1,3},{2,4},{3,5},{4,6},{5,7},{6,0},{7,1},{8,10},{9,11},{10,... | collective-permute-start | bytes 1081352 | tf_op jit(solution)/shard_map/ppermute | solution.py:880
  193.7 15.6 %collective-permute-start.54 = (bf16[512,128]{1,0:T(8,128)(2,1)S(1)}, bf16[512,128]{1,0:T(8,128)(2,1)S(1)}, u32[]{:S(2)}, u32[]{:S(2)}) collective-permute-start(bf16[512,128]{1,0:T(8,128)(2,1)S(1)} %constant_dynamic-slice_fusion.4), channel_id=1, source_target_pairs={{0,16},{8,24},{16,0},{24,8},{1,17},{9,25},{17,1},{25,9},{2,18},{10... | collective-permute-start | bytes 393224 | tf_op jit(solution)/shard_map/ppermute | solution.py:847
  211.2 8.2 %collective-permute-start.59 = (bf16[512,1024]{1,0:T(8,128)(2,1)S(1)}, bf16[512,1024]{1,0:T(8,128)(2,1)S(1)}, u32[]{:S(2)}, u32[]{:S(2)}) collective-permute-start(bf16[512,1024]{1,0:T(8,128)(2,1)S(1)} %get-tuple-element.964), channel_id=1, source_target_pairs={{0,8},{8,0},{16,24},{24,16},{1,9},{9,1},{17,25},{25,17},{2,10},{10... | collective-permute-start | bytes 3145736 | tf_op jit(solution)/shard_map/ppermute | solution.py:843
  211.3 13.7 %collective-permute-start.58 = (bf16[1536,128]{1,0:T(8,128)(2,1)S(1)}, bf16[1536,128]{1,0:T(8,128)(2,1)S(1)}, u32[]{:S(2)}, u32[]{:S(2)}) collective-permute-start(bf16[1536,128]{1,0:T(8,128)(2,1)S(1)} %copy-done.92), channel_id=1, source_target_pairs={{0,1},{1,0},{2,3},{3,2},{4,5},{5,4},{6,7},{7,6},{8,9},{9,8},{10,11... | collective-permute-start | bytes 1179656 | tf_op jit(solution)/shard_map/ppermute | solution.py:875
  213.1 7.6 %collective-permute-start.55 = (bf16[384,128]{1,0:T(8,128)(2,1)S(1)}, bf16[384,128]{1,0:T(8,128)(2,1)S(1)}, u32[]{:S(2)}, u32[]{:S(2)}) collective-permute-start(bf16[384,128]{1,0:T(8,128)(2,1)S(1)} %get-tuple-element.957), channel_id=1, source_target_pairs={{0,2},{1,3},{2,4},{3,5},{4,6},{5,7},{6,0},{7,1},{8,10},{9,11},{10,... | collective-permute-start | bytes 294920 | tf_op jit(solution)/shard_map/ppermute | solution.py:880
  213.1 10.8 %collective-permute-start.56 = (bf16[384,128]{1,0:T(8,128)(2,1)S(1)}, bf16[384,128]{1,0:T(8,128)(2,1)S(1)}, u32[]{:S(2)}, u32[]{:S(2)}) collective-permute-start(bf16[384,128]{1,0:T(8,128)(2,1)S(1)} %get-tuple-element.958), channel_id=1, source_target_pairs={{0,4},{1,5},{2,6},{3,7},{4,0},{5,1},{6,2},{7,3},{8,12},{9,13},{10,... | collective-permute-start | bytes 294920 | tf_op jit(solution)/shard_map/ppermute | solution.py:880
  215.7 8.2 %collective-permute-start.57 = (bf16[384,128]{1,0:T(8,128)(2,1)S(1)}, bf16[384,128]{1,0:T(8,128)(2,1)S(1)}, u32[]{:S(2)}, u32[]{:S(2)}) collective-permute-start(bf16[384,128]{1,0:T(8,128)(2,1)S(1)} %get-tuple-element.959), channel_id=1, source_target_pairs={{0,6},{1,7},{2,0},{3,1},{4,2},{5,3},{6,4},{7,5},{8,14},{9,15},{10,... | collective-permute-start | bytes 294920 | tf_op jit(solution)/shard_map/ppermute | solution.py:880
  225.0 15.5 %collective-permute-start.63 = (bf16[256,1024]{1,0:T(8,128)(2,1)S(1)}, bf16[256,1024]{1,0:T(8,128)(2,1)S(1)}, u32[]{:S(2)}, u32[]{:S(2)}) collective-permute-start(bf16[256,1024]{1,0:T(8,128)(2,1)S(1)} %lower.5), channel_id=1, source_target_pairs={{0,16},{8,24},{16,0},{24,8},{1,17},{9,25},{17,1},{25,9},{2,18},{10... | collective-permute-start | bytes 1572872 | tf_op jit(solution)/shard_map/ppermute | solution.py:847
  226.3 8.4 %collective-permute-start.64 = (bf16[1024,128]{1,0:T(8,128)(2,1)S(1)}, bf16[1024,128]{1,0:T(8,128)(2,1)S(1)}, u32[]{:S(2)}, u32[]{:S(2)}) collective-permute-start(bf16[1024,128]{1,0:T(8,128)(2,1)S(1)} %get-tuple-element.995), channel_id=1, source_target_pairs={{0,1},{1,0},{2,3},{3,2},{4,5},{5,4},{6,7},{7,6},{8,9},{9,8},{10,11... | collective-permute-start | bytes 786440 | tf_op jit(solution)/shard_map/ppermute | solution.py:875
  228.1 7.8 %collective-permute-start.60 = (bf16[384,128]{1,0:T(8,128)(2,1)S(1)}, bf16[384,128]{1,0:T(8,128)(2,1)S(1)}, u32[]{:S(2)}, u32[]{:S(2)}) collective-permute-start(bf16[384,128]{1,0:T(8,128)(2,1)S(1)} %get-tuple-element.986), channel_id=1, source_target_pairs={{0,2},{1,3},{2,4},{3,5},{4,6},{5,7},{6,0},{7,1},{8,10},{9,11},{10,... | collective-permute-start | bytes 294920 | tf_op jit(solution)/shard_map/ppermute | solution.py:880
  228.5 12.0 %collective-permute-start.61 = (bf16[384,128]{1,0:T(8,128)(2,1)S(1)}, bf16[384,128]{1,0:T(8,128)(2,1)S(1)}, u32[]{:S(2)}, u32[]{:S(2)}) collective-permute-start(bf16[384,128]{1,0:T(8,128)(2,1)S(1)} %get-tuple-element.987), channel_id=1, source_target_pairs={{0,4},{1,5},{2,6},{3,7},{4,0},{5,1},{6,2},{7,3},{8,12},{9,13},{10,... | collective-permute-start | bytes 294920 | tf_op jit(solution)/shard_map/ppermute | solution.py:880
  230.7 9.8 %collective-permute-start.62 = (bf16[384,128]{1,0:T(8,128)(2,1)S(1)}, bf16[384,128]{1,0:T(8,128)(2,1)S(1)}, u32[]{:S(2)}, u32[]{:S(2)}) collective-permute-start(bf16[384,128]{1,0:T(8,128)(2,1)S(1)} %get-tuple-element.988), channel_id=1, source_target_pairs={{0,6},{1,7},{2,0},{3,1},{4,2},{5,3},{6,4},{7,5},{8,14},{9,15},{10,... | collective-permute-start | bytes 294920 | tf_op jit(solution)/shard_map/ppermute | solution.py:880
  242.7 9.9 %collective-permute-start.68 = (bf16[1600,128]{1,0:T(8,128)(2,1)}, bf16[1600,128]{1,0:T(8,128)(2,1)S(1)}, u32[]{:S(2)}, u32[]{:S(2)}) collective-permute-start(bf16[1600,128]{1,0:T(8,128)(2,1)} %get-tuple-element.1028), channel_id=1, source_target_pairs={{0,16},{8,24},{16,0},{24,8},{1,17},{9,25},{17,1},{25,9},{2,18},{10... | collective-permute-start | bytes 1228808 | tf_op jit(solution)/shard_map/ppermute | solution.py:847
  243.2 8.2 %collective-permute-start.65 = (bf16[256,128]{1,0:T(8,128)(2,1)}, bf16[256,128]{1,0:T(8,128)(2,1)S(1)}, u32[]{:S(2)}, u32[]{:S(2)}) collective-permute-start(bf16[256,128]{1,0:T(8,128)(2,1)} %get-tuple-element.1011), channel_id=1, source_target_pairs={{0,2},{1,3},{2,4},{3,5},{4,6},{5,7},{6,0},{7,1},{8,10},{9,11},{10,... | collective-permute-start | bytes 196616 | tf_op jit(solution)/shard_map/ppermute | solution.py:880
  245.8 6.3 %collective-permute-start.66 = (bf16[256,128]{1,0:T(8,128)(2,1)}, bf16[256,128]{1,0:T(8,128)(2,1)}, u32[]{:S(2)}, u32[]{:S(2)}) collective-permute-start(bf16[256,128]{1,0:T(8,128)(2,1)} %get-tuple-element.1012), channel_id=1, source_target_pairs={{0,4},{1,5},{2,6},{3,7},{4,0},{5,1},{6,2},{7,3},{8,12},{9,13},{10,... | collective-permute-start | bytes 196616 | tf_op jit(solution)/shard_map/ppermute | solution.py:880
  (104 other events, 797.5 us)
Sparse Core Ops, SparseCore 0:
  40.2 60.7 all-gather.2
  176.9 71.4 reduce-scatter.1
